TPU v7x, 32 devices: a whole 2x2x4 slice. The times are simulated.
32 devices in a mesh: member: 8 (over y, x, core), band: 4 (over z).
Axes of the slice: x: 2, y: 2, z: 4, core: 2. Of those that a mesh axis runs over, the one named last changes fastest.
Arguments:
- height_start: float32 [80, 256, 512], P(None, 'member', 'band'), may hold values from -6 to 6
- east_start: float32 [80, 256, 512], P(None, 'member', 'band'), may hold values from -6 to 6
- north_start: float32 [80, 256, 512], P(None, 'member', 'band'), may hold values from -6 to 6
- obs_value: float32 [256, 512], P('member', 'band'), may hold values from -8 to 8
- obs_mask: int32 [256, 512], P('member', 'band'), may hold values 0 or 1
- obs_precision: float32 [256, 512], P('member', 'band'), may hold values from 0.25 to 4
- step_sizes: int32 [2], replicated, may hold values from 4 to 12
Outputs:
- analysis_height: float32 [80, 256, 512], P(None, 'member', 'band')
- analysis_east: float32 [80, 256, 512], P(None, 'member', 'band')
- analysis_north: float32 [80, 256, 512], P(None, 'member', 'band')
All inputs are finite; a program needn't handle non-finite values. No bound on the sum of `obs_mask` on one device may be relied on, other than what follows from the above.
Results may differ from a plain program's by a relative error of at most 0.0001.
Values sent between devices are 32-bit elements; how exact they have to be, the bound alone decides.
No kernel may reach another device: no remote copies, remote signals or barrier semaphores. Data moves between devices by JAX's collectives and lax.ppermute only.
A program may use at most 128 MiB of HBM per device.

v0:
```python
import jax
import jax.numpy as jnp
from jax import lax
from jax.sharding import PartitionSpec as P

STEPS = 3
ITERS = 2
LWIDTH = 32
LSCALE = 12


highest = lax.Precision.HIGHEST


def extended(block, sides, width, periodic):
    for axis, dim in sides:
        count = lax.axis_size(axis)
        forward = [(i, i + 1) for i in range(count - 1)]
        if periodic:
            forward.append((count - 1, 0))
        backward = [(target, source) for source, target in forward]
        low = lax.ppermute(
            lax.slice_in_dim(block, block.shape[dim] - width, None, axis=dim), axis, forward
        )
        high = lax.ppermute(lax.slice_in_dim(block, 0, width, axis=dim), axis, backward)
        block = jnp.concatenate([low, block, high], axis=dim)
    return block


def taper_kernel(outputs, inputs, margin, spread):
    out_index = jnp.arange(outputs, dtype=jnp.int32)[:, None]
    in_index = jnp.arange(inputs, dtype=jnp.int32)[None, :]
    offset = (in_index - margin - out_index).astype(jnp.float32)
    scaled_off = offset / spread
    weight = jnp.exp(-0.5 * scaled_off * scaled_off)
    return jnp.where(jnp.abs(offset) <= margin, weight, jnp.zeros_like(weight))


def taper_rows(padded, row_count, margin, spread):
    kernel = taper_kernel(row_count, row_count + 2 * margin, margin, spread)
    return jnp.einsum("ab,mbc->mac", kernel, padded, precision=highest)


def taper_columns(padded, columns, margin, spread):
    block_size = 128
    windows = jnp.stack([padded], axis=2)
    kernel = taper_kernel(block_size, block_size + 2 * margin, margin, spread)
    result = jnp.einsum("mrjk,bk->mrjb", windows, kernel, precision=highest)
    return result.reshape(padded.shape[0], padded.shape[1], columns)


def wave_edges(stacked, margin):
    rows_done = extended(stacked, (("member", 2),), margin, False)
    return extended(rows_done, (("band", 3),), margin, True)


def advance_shallow(height, eastward, northward):
    padded = wave_edges(jnp.stack([eastward, northward]), 1)
    east_pad = padded[0]
    north_pad = padded[1]
    new_height = height - 0.2 * (
        east_pad[:, 1:-1, 2:]
        - east_pad[:, 1:-1, :-2]
        + (north_pad[:, 2:, 1:-1] - north_pad[:, :-2, 1:-1])
    )
    height_pad = wave_edges(new_height[None], 1)[0]
    new_east = (
        eastward + 0.1 * northward - 0.2 * (height_pad[:, 1:-1, 2:] - height_pad[:, 1:-1, :-2])
    )
    new_north = (
        northward - 0.1 * eastward - 0.2 * (height_pad[:, 2:, 1:-1] - height_pad[:, :-2, 1:-1])
    )
    return (new_height, new_east, new_north)


def descend(anomalies, member_means, observed, step_sizes, cell_total, gather_state, localize):
    weights = jnp.zeros_like(anomalies[0])
    for iteration in range(ITERS):
        if iteration == 0:
            analysis_state = member_means
        else:
            analysis_state = member_means + gather_state(jnp.sum(anomalies * weights[None], axis=1))
        residual = observed[1] * (
            observed[0]
            - analysis_state[0]
            - 0.15 * (analysis_state[1] * analysis_state[1] + analysis_state[2] * analysis_state[2])
        )
        contrib = (
            anomalies[0]
            + 0.3 * (analysis_state[1] * anomalies[1] + analysis_state[2] * anomalies[2])
        ) * residual
        gradient = weights - localize(contrib)
        square_total = lax.psum(jnp.sum(gradient * gradient), ("member", "band"))
        factor = (
            step_sizes[iteration].astype(jnp.float32)
            / 64.0
            / jnp.sqrt(square_total / cell_total + 1e-06)
        )
        weights = weights - factor * gradient
    return weights


def analyse_tiles(ensemble, observed, step_sizes, cell_total, root_scale, members):
    member_means = jnp.sum(ensemble, axis=1) / members
    anomalies = (ensemble - member_means[:, None]) / root_scale

    def local_state(partial_sum):
        return partial_sum

    def localize(contrib):
        padded = extended(contrib, (("member", 1),), LWIDTH, False)
        lat_done = taper_rows(padded, contrib.shape[1], LWIDTH, LSCALE)
        wrapped = extended(lat_done, (("band", 2),), LWIDTH, True)
        return taper_columns(wrapped, contrib.shape[2], LWIDTH, LSCALE)

    weights = descend(
        anomalies, member_means, observed, step_sizes, cell_total, local_state, localize
    )
    return jnp.sum(anomalies * weights[None], axis=1)


def per_device(
    height_start, east_start, north_start, obs_value, obs_mask, obs_precision, step_sizes
):
    members = height_start.shape[0]
    row_count = height_start.shape[1]
    col_count = height_start.shape[2]
    height, eastward, northward = (height_start, east_start, north_start)
    for section_number in range(STEPS):
        height, eastward, northward = advance_shallow(height, eastward, northward)
    ensemble = jnp.stack([height, eastward, northward])
    obs_weight = obs_mask.astype(jnp.float32) * obs_precision
    observed = jnp.stack([obs_value, obs_weight])
    cell_total = float(
        members * row_count * col_count * lax.axis_size("member") * lax.axis_size("band")
    )
    root_scale = jnp.sqrt(jnp.float32(members - 1))
    increment = analyse_tiles(ensemble, observed, step_sizes, cell_total, root_scale, members)
    analysis = ensemble + increment[:, None]
    return (analysis[0], analysis[1], analysis[2])


def solution(mesh):
    placed = (
        P(None, "member", "band"),
        P(None, "member", "band"),
        P(None, "member", "band"),
        P("member", "band"),
        P("member", "band"),
        P("member", "band"),
        P(),
    )
    return jax.shard_map(
        per_device,
        mesh=mesh,
        in_specs=placed,
        out_specs=(P(None, "member", "band"), P(None, "member", "band"), P(None, "member", "band")),
        check_vma=False,
    )
```

profile of v0, /device:TPU:0, one launch (start us, length us, event | category | flops | bytes accessed | tf_op | source)
XLA Modules:
  0.0 438.9 jit_solution(1061487402955503284)
XLA Ops:
  5.9 4.0 collective-permute-done.1
  10.4 3.7 fusion.115
  14.1 2.9 copy.10
  18.6 2.9 copy.11
  23.9 2.5 copy.12
  26.4 2.5 copy.13
  28.9 6.9 %pad_maximum_fusion = f32[2,80,34,130]{3,2,1,0:T(8,128)S(1)} fusion(f32[2,80,34,1]{3,2,1,0:T(8,128)} %copy.13, f32[2,80,1,128]{3,2,1,0:T(1,128)S(1)} %collective-permute-done.1, f32[1,80,32,128]{3,2,1,0:T(8,128)S(1)} %bitcast.128, f32[1,80,32,128]{3,2,1,0:T(8,128)S(1)} %bitcast.131, f32[2,80,1,128]{3,2,1,0:T(1,128)S(1)} %collective-permute-done, ...), kind=kLoop, calls=%fused_computation | loop fusion | flops 3536000 | bytes 5657600 | tf_op jit(solution)/shard_map/concatenate | solution.py:26
  38.4 4.5 %collective-permute-start.4 = (f32[1,80,1,128]{3,2,1,0:T(1,128)S(1)}, f32[1,80,1,128]{3,2,1,0:T(1,128)S(1)}, u32[]{:S(2)}, u32[]{:S(2)}) collective-permute-start(f32[1,80,1,128]{3,2,1,0:T(1,128)S(1)} %get-tuple-element.44), channel_id=1, source_target_pairs={{0,4},{4,8},{8,12},{12,16},{16,20},{20,24},{24,28},{1,5},{5,9},{9,... | collective-permute-start | bytes 122888 | tf_op jit(solution)/shard_map/ppermute | solution.py:22
  52.9 3.4 collective-permute-start.7
  59.8 3.8 maximum_bitcast_fusion
  64.9 4.3 collective-permute-start.8
  72.9 3.7 fusion.114
  76.7 2.9 copy.18
  79.7 2.9 copy.19
  82.7 3.8 collective-permute-start.11
  86.4 2.5 copy.20
  89.0 2.5 copy.21
  91.5 6.9 %pad_maximum_fusion.1 = f32[2,80,34,130]{3,2,1,0:T(8,128)S(1)} fusion(f32[2,80,34,1]{3,2,1,0:T(8,128)} %copy.21, f32[2,80,1,128]{3,2,1,0:T(1,128)S(1)} %collective-permute-done.9, f32[1,80,32,128]{3,2,1,0:T(8,128)S(1)} %bitcast.119, f32[1,80,32,128]{3,2,1,0:T(8,128)S(1)} %bitcast.116, f32[2,80,1,128]{3,2,1,0:T(1,128)S(1)} %collective-permute-done.8, ...), kind=kLoop, calls=%fused_computation.1 | loop fusion | flops 3536000 | bytes 5657600 | tf_op jit(solution)/shard_map/concatenate | solution.py:26
  100.9 5.2 %collective-permute-start.12 = (f32[1,80,1,128]{3,2,1,0:T(1,128)S(1)}, f32[1,80,1,128]{3,2,1,0:T(1,128)S(1)}, u32[]{:S(2)}, u32[]{:S(2)}) collective-permute-start(f32[1,80,1,128]{3,2,1,0:T(1,128)S(1)} %get-tuple-element.42), channel_id=1, source_target_pairs={{0,4},{4,8},{8,12},{12,16},{16,20},{20,24},{24,28},{1,5},{5,9},{9,... | collective-permute-start | bytes 122888 | tf_op jit(solution)/shard_map/ppermute | solution.py:22
  115.5 3.8 collective-permute-start.15
  122.8 3.8 maximum_bitcast_fusion.1
  127.9 5.3 %collective-permute-start.16 = (f32[2,80,1,128]{3,2,1,0:T(1,128)S(1)}, f32[2,80,1,128]{3,2,1,0:T(1,128)S(1)}, u32[]{:S(2)}, u32[]{:S(2)}) collective-permute-start(f32[2,80,1,128]{3,2,1,0:T(1,128)S(1)} %get-tuple-element.24), channel_id=1, source_target_pairs={{0,4},{4,8},{8,12},{12,16},{16,20},{20,24},{24,28},{1,5},{5,9},{9,... | collective-permute-start | bytes 245768 | tf_op jit(solution)/shard_map/ppermute | solution.py:22
  136.9 3.7 fusion.113
  140.6 2.9 copy.26
  143.6 2.9 copy.27
  146.5 4.0 collective-permute-start.19
  150.6 2.5 copy.28
  153.1 2.5 copy.29
  155.6 6.9 %pad_maximum_fusion.2 = f32[2,80,34,130]{3,2,1,0:T(8,128)S(1)} fusion(f32[2,80,34,1]{3,2,1,0:T(8,128)} %copy.29, f32[2,80,1,128]{3,2,1,0:T(1,128)S(1)} %collective-permute-done.17, f32[1,80,32,128]{3,2,1,0:T(8,128)S(1)} %bitcast.113, f32[1,80,32,128]{3,2,1,0:T(8,128)S(1)} %bitcast.110, f32[2,80,1,128]{3,2,1,0:T(1,128)S(1)} %collective-permute-done.16, ...), kind=kLoop, calls=%fused_computation.2 | loop fusion | flops 3536000 | bytes 5657600 | tf_op jit(solution)/shard_map/concatenate | solution.py:26
  165.1 5.0 %collective-permute-start.20 = (f32[1,80,1,128]{3,2,1,0:T(1,128)S(1)}, f32[1,80,1,128]{3,2,1,0:T(1,128)S(1)}, u32[]{:S(2)}, u32[]{:S(2)}) collective-permute-start(f32[1,80,1,128]{3,2,1,0:T(1,128)S(1)} %get-tuple-element.40), channel_id=1, source_target_pairs={{0,4},{4,8},{8,12},{12,16},{16,20},{20,24},{24,28},{1,5},{5,9},{9,... | collective-permute-start | bytes 122888 | tf_op jit(solution)/shard_map/ppermute | solution.py:22
  179.4 3.8 collective-permute-start.23
  186.8 3.8 maximum_bitcast_fusion.2
  195.2 5.6 %collective-permute-start.24 = (f32[80,32,128]{2,1,0:T(8,128)S(1)}, f32[80,32,128]{2,1,0:T(8,128)S(1)}, u32[]{:S(2)}, u32[]{:S(2)}) collective-permute-start(f32[80,32,128]{2,1,0:T(8,128)S(1)} %add_multiply_fusion.1), channel_id=1, source_target_pairs={{0,4},{4,8},{8,12},{12,16},{16,20},{20,24},{24,28},{1,5},{5,9},{9,... | collective-permute-start | bytes 3932168 | tf_op jit(solution)/shard_map/ppermute | solution.py:22
  212.1 2.8 copy.35
  214.9 3.8 collective-permute-start.27
  219.9 3.3 collective-permute-done.26
  223.3 3.0 copy.36
  228.8 3.0 copy.37
  231.8 6.5 %multiply_reduce_fusion.3 = (f32[]{:T(128)}, f32[80,32,128]{2,1,0:T(8,128)}) fusion(s32[192]{0:T(256)S(1)} %iota_add_fusion, f32[80,32,32]{2,1,0:T(8,128)} %copy.37, f32[80,32,128]{2,1,0:T(8,128)} %copy-done.17, f32[80,32,32]{2,1,0:T(8,128)} %copy.36), kind=kOutput, calls=%fused_computation.97 | convolution fusion | flops 757137408 | bytes 3277572 | tf_op jit(solution)/shard_map/mrjk,bk->mrjb/dot_general | solution.py:48
  238.3 74.2 %psum.14 = f32[]{:T(128)} all-reduce(f32[]{:T(128)} %get-tuple-element.52), channel_id=1, replica_groups=mesh['member'=8,'band'=4] {'member','band'}, use_global_device_ids=true, to_apply=%region_2.3 | all-reduce | flops 1 | bytes 8 | tf_op jit(solution)/shard_map/psum | solution.py:93
  321.4 4.8 %collective-permute-done.29 = f32[80,32,128]{2,1,0:T(8,128)S(1)} collective-permute-done((f32[80,32,128]{2,1,0:T(8,128)S(1)}, f32[80,32,128]{2,1,0:T(8,128)S(1)}, u32[]{:S(2)}, u32[]{:S(2)}) %collective-permute-start.29) | collective-permute-done | bytes 1310752 | tf_op jit(solution)/shard_map/ppermute | solution.py:25
  334.7 2.8 copy.39
  339.8 3.9 collective-permute-done.30
  343.7 3.0 copy.40
  346.8 2.5 collective-permute-done.31
  349.3 3.0 copy.41
  352.3 6.8 %multiply_reduce_fusion.2 = (f32[]{:T(128)}, f32[80,32,128]{2,1,0:T(8,128)}) fusion(s32[192]{0:T(256)S(1)} %iota_add_fusion, f32[80,32,32]{2,1,0:T(8,128)} %copy.41, f32[80,32,128]{2,1,0:T(8,128)} %copy-done.18, f32[80,32,32]{2,1,0:T(8,128)} %copy.40, f32[80,32,128]{2,1,0:T(8,128)} %get-tuple-element.53, f32[]{:T(128)S(6)} %div.55), kind=kOutput, calls=%fused_computation.94 | convolution fusion | flops 757792768 | bytes 4588296 | tf_op jit(solution)/shard_map/mrjk,bk->mrjb/dot_general | solution.py:48
  359.1 73.4 %psum.15 = f32[]{:T(128)} all-reduce(f32[]{:T(128)} %get-tuple-element.54), channel_id=1, replica_groups=mesh['member'=8,'band'=4] {'member','band'}, use_global_device_ids=true, to_apply=%region_5.6 | all-reduce | flops 1 | bytes 8 | tf_op jit(solution)/shard_map/psum | solution.py:93
  (164 shorter events, 108.9 us)
Async XLA Ops:
  0.6 9.3 %copy-start.19 = (f32[80,32,128]{2,1,0:T(8,128)S(1)}, f32[80,32,128]{2,1,0:T(8,128)}, u32[]{:S(2)}) copy-start(f32[80,32,128]{2,1,0:T(8,128)} %param.9) | copy-start | bytes 3932164
  0.6 9.2 %copy-start.21 = (f32[80,32,128]{2,1,0:T(8,128)S(1)}, f32[80,32,128]{2,1,0:T(8,128)}, u32[]{:S(2)}) copy-start(f32[80,32,128]{2,1,0:T(8,128)} %param.8) | copy-start | bytes 3932164
  2.2 3.7 collective-permute-start
  4.6 5.3 %collective-permute-start.1 = (f32[2,80,1,128]{3,2,1,0:T(1,128)S(1)}, f32[2,80,1,128]{3,2,1,0:T(1,128)S(1)}, u32[]{:S(2)}, u32[]{:S(2)}) collective-permute-start(f32[2,80,1,128]{3,2,1,0:T(1,128)S(1)} %get-tuple-element.29), channel_id=1, source_target_pairs={{4,0},{8,4},{12,8},{16,12},{20,16},{24,20},{28,24},{5,1},{9,5},{13... | collective-permute-start | bytes 245768 | tf_op jit(solution)/shard_map/ppermute | solution.py:25
  17.0 6.8 %collective-permute-start.2 = (f32[2,80,34,1]{1,0,3,2:T(2,128)S(1)}, f32[2,80,34,1]{1,0,3,2:T(2,128)S(1)}, u32[]{:S(2)}, u32[]{:S(2)}) collective-permute-start(f32[2,80,34,1]{1,0,3,2:T(2,128)S(1)} %copy.10), channel_id=1, source_target_pairs={{0,1},{1,2},{2,3},{3,0},{4,5},{5,6},{6,7},{7,4},{8,9},{9,10},{10,1... | collective-permute-start | bytes 65288 | tf_op jit(solution)/shard_map/ppermute | solution.py:22
  21.6 4.8 %collective-permute-start.3 = (f32[2,80,34,1]{1,0,3,2:T(2,128)S(1)}, f32[2,80,34,1]{1,0,3,2:T(2,128)S(1)}, u32[]{:S(2)}, u32[]{:S(2)}) collective-permute-start(f32[2,80,34,1]{1,0,3,2:T(2,128)S(1)} %copy.11), channel_id=1, source_target_pairs={{1,0},{2,1},{3,2},{0,3},{5,4},{6,5},{7,6},{4,7},{9,8},{10,9},{11,1... | collective-permute-start | bytes 65288 | tf_op jit(solution)/shard_map/ppermute | solution.py:25
  38.3 21.5 %copy-start.15 = (f32[80,32,128]{2,1,0:T(8,128)}, f32[80,32,128]{2,1,0:T(8,128)S(1)}, u32[]{:S(2)}) copy-start(f32[80,32,128]{2,1,0:T(8,128)S(1)} %fusion.59) | copy-start | bytes 3932164
  38.4 5.8 %collective-permute-start.4 = (f32[1,80,1,128]{3,2,1,0:T(1,128)S(1)}, f32[1,80,1,128]{3,2,1,0:T(1,128)S(1)}, u32[]{:S(2)}, u32[]{:S(2)}) collective-permute-start(f32[1,80,1,128]{3,2,1,0:T(1,128)S(1)} %get-tuple-element.44), channel_id=1, source_target_pairs={{0,4},{4,8},{8,12},{12,16},{16,20},{20,24},{24,28},{1,5},{5,9},{9,... | collective-permute-start | bytes 122888 | tf_op jit(solution)/shard_map/ppermute | solution.py:22
  42.9 3.1 collective-permute-start.5
  50.3 6.0 %collective-permute-start.6 = (f32[1,80,34,1]{1,3,2,0:T(1,128)S(1)}, f32[1,80,34,1]{1,3,2,0:T(1,128)S(1)}, u32[]{:S(2)}, u32[]{:S(2)}) collective-permute-start(f32[1,80,34,1]{1,3,2,0:T(1,128)S(1)} %copy.14), channel_id=1, source_target_pairs={{0,1},{1,2},{2,3},{3,0},{4,5},{5,6},{6,7},{7,4},{8,9},{9,10},{10,1... | collective-permute-start | bytes 32648 | tf_op jit(solution)/shard_map/ppermute | solution.py:22
  52.9 5.2 %collective-permute-start.7 = (f32[1,80,34,1]{1,3,2,0:T(1,128)S(1)}, f32[1,80,34,1]{1,3,2,0:T(1,128)S(1)}, u32[]{:S(2)}, u32[]{:S(2)}) collective-permute-start(f32[1,80,34,1]{1,3,2,0:T(1,128)S(1)} %copy.15), channel_id=1, source_target_pairs={{1,0},{2,1},{3,2},{0,3},{5,4},{6,5},{7,6},{4,7},{9,8},{10,9},{11,1... | collective-permute-start | bytes 32648 | tf_op jit(solution)/shard_map/ppermute | solution.py:25
  59.8 3.8 copy-start.20
  59.8 3.8 copy-start.22
  64.7 26.8 %copy-start.9 = (f32[80,32,128]{2,1,0:T(8,128)}, f32[80,32,128]{2,1,0:T(8,128)S(1)}, u32[]{:S(2)}) copy-start(f32[80,32,128]{2,1,0:T(8,128)S(1)} %get-tuple-element.13) | copy-start | bytes 3932164
  64.7 26.8 %copy-start.11 = (f32[80,32,128]{2,1,0:T(8,128)}, f32[80,32,128]{2,1,0:T(8,128)S(1)}, u32[]{:S(2)}) copy-start(f32[80,32,128]{2,1,0:T(8,128)S(1)} %get-tuple-element.14) | copy-start | bytes 3932164
  64.9 5.6 %collective-permute-start.8 = (f32[2,80,1,128]{3,2,1,0:T(1,128)S(1)}, f32[2,80,1,128]{3,2,1,0:T(1,128)S(1)}, u32[]{:S(2)}, u32[]{:S(2)}) collective-permute-start(f32[2,80,1,128]{3,2,1,0:T(1,128)S(1)} %get-tuple-element.26), channel_id=1, source_target_pairs={{0,4},{4,8},{8,12},{12,16},{16,20},{20,24},{24,28},{1,5},{5,9},{9,... | collective-permute-start | bytes 245768 | tf_op jit(solution)/shard_map/ppermute | solution.py:22
  69.2 3.2 collective-permute-start.9
  79.6 6.9 %collective-permute-start.10 = (f32[2,80,34,1]{1,0,3,2:T(2,128)S(1)}, f32[2,80,34,1]{1,0,3,2:T(2,128)S(1)}, u32[]{:S(2)}, u32[]{:S(2)}) collective-permute-start(f32[2,80,34,1]{1,0,3,2:T(2,128)S(1)} %copy.18), channel_id=1, source_target_pairs={{0,1},{1,2},{2,3},{3,0},{4,5},{5,6},{6,7},{7,4},{8,9},{9,10},{10,1... | collective-permute-start | bytes 65288 | tf_op jit(solution)/shard_map/ppermute | solution.py:22
  82.7 6.3 %collective-permute-start.11 = (f32[2,80,34,1]{1,0,3,2:T(2,128)S(1)}, f32[2,80,34,1]{1,0,3,2:T(2,128)S(1)}, u32[]{:S(2)}, u32[]{:S(2)}) collective-permute-start(f32[2,80,34,1]{1,0,3,2:T(2,128)S(1)} %copy.19), channel_id=1, source_target_pairs={{1,0},{2,1},{3,2},{0,3},{5,4},{6,5},{7,6},{4,7},{9,8},{10,9},{11,1... | collective-permute-start | bytes 65288 | tf_op jit(solution)/shard_map/ppermute | solution.py:25
  100.8 22.0 %copy-start.13 = (f32[80,32,128]{2,1,0:T(8,128)}, f32[80,32,128]{2,1,0:T(8,128)S(1)}, u32[]{:S(2)}) copy-start(f32[80,32,128]{2,1,0:T(8,128)S(1)} %fusion.52) | copy-start | bytes 3932164
  100.9 6.9 %collective-permute-start.12 = (f32[1,80,1,128]{3,2,1,0:T(1,128)S(1)}, f32[1,80,1,128]{3,2,1,0:T(1,128)S(1)}, u32[]{:S(2)}, u32[]{:S(2)}) collective-permute-start(f32[1,80,1,128]{3,2,1,0:T(1,128)S(1)} %get-tuple-element.42), channel_id=1, source_target_pairs={{0,4},{4,8},{8,12},{12,16},{16,20},{20,24},{24,28},{1,5},{5,9},{9,... | collective-permute-start | bytes 122888 | tf_op jit(solution)/shard_map/ppermute | solution.py:22
  106.1 3.1 collective-permute-start.13
  113.5 5.8 %collective-permute-start.14 = (f32[1,80,34,1]{1,3,2,0:T(1,128)S(1)}, f32[1,80,34,1]{1,3,2,0:T(1,128)S(1)}, u32[]{:S(2)}, u32[]{:S(2)}) collective-permute-start(f32[1,80,34,1]{1,3,2,0:T(1,128)S(1)} %copy.22), channel_id=1, source_target_pairs={{0,1},{1,2},{2,3},{3,0},{4,5},{5,6},{6,7},{7,4},{8,9},{9,10},{10,1... | collective-permute-start | bytes 32648 | tf_op jit(solution)/shard_map/ppermute | solution.py:22
  115.5 5.6 %collective-permute-start.15 = (f32[1,80,34,1]{1,3,2,0:T(1,128)S(1)}, f32[1,80,34,1]{1,3,2,0:T(1,128)S(1)}, u32[]{:S(2)}, u32[]{:S(2)}) collective-permute-start(f32[1,80,34,1]{1,3,2,0:T(1,128)S(1)} %copy.23), channel_id=1, source_target_pairs={{1,0},{2,1},{3,2},{0,3},{5,4},{6,5},{7,6},{4,7},{9,8},{10,9},{11,1... | collective-permute-start | bytes 32648 | tf_op jit(solution)/shard_map/ppermute | solution.py:25
  122.8 3.8 copy-start.10
  122.8 3.8 copy-start.12
  127.7 27.9 %copy-start.5 = (f32[80,32,128]{2,1,0:T(8,128)}, f32[80,32,128]{2,1,0:T(8,128)S(1)}, u32[]{:S(2)}) copy-start(f32[80,32,128]{2,1,0:T(8,128)S(1)} %get-tuple-element.11) | copy-start | bytes 3932164
  127.8 27.9 %copy-start.7 = (f32[80,32,128]{2,1,0:T(8,128)}, f32[80,32,128]{2,1,0:T(8,128)S(1)}, u32[]{:S(2)}) copy-start(f32[80,32,128]{2,1,0:T(8,128)S(1)} %get-tuple-element.12) | copy-start | bytes 3932164
  127.9 6.6 %collective-permute-start.16 = (f32[2,80,1,128]{3,2,1,0:T(1,128)S(1)}, f32[2,80,1,128]{3,2,1,0:T(1,128)S(1)}, u32[]{:S(2)}, u32[]{:S(2)}) collective-permute-start(f32[2,80,1,128]{3,2,1,0:T(1,128)S(1)} %get-tuple-element.24), channel_id=1, source_target_pairs={{0,4},{4,8},{8,12},{12,16},{16,20},{20,24},{24,28},{1,5},{5,9},{9,... | collective-permute-start | bytes 245768 | tf_op jit(solution)/shard_map/ppermute | solution.py:22
  133.2 3.2 collective-permute-start.17
  143.6 7.0 %collective-permute-start.18 = (f32[2,80,34,1]{1,0,3,2:T(2,128)S(1)}, f32[2,80,34,1]{1,0,3,2:T(2,128)S(1)}, u32[]{:S(2)}, u32[]{:S(2)}) collective-permute-start(f32[2,80,34,1]{1,0,3,2:T(2,128)S(1)} %copy.26), channel_id=1, source_target_pairs={{0,1},{1,2},{2,3},{3,0},{4,5},{5,6},{6,7},{7,4},{8,9},{9,10},{10,1... | collective-permute-start | bytes 65288 | tf_op jit(solution)/shard_map/ppermute | solution.py:22
  146.5 6.6 %collective-permute-start.19 = (f32[2,80,34,1]{1,0,3,2:T(2,128)S(1)}, f32[2,80,34,1]{1,0,3,2:T(2,128)S(1)}, u32[]{:S(2)}, u32[]{:S(2)}) collective-permute-start(f32[2,80,34,1]{1,0,3,2:T(2,128)S(1)} %copy.27), channel_id=1, source_target_pairs={{1,0},{2,1},{3,2},{0,3},{5,4},{6,5},{7,6},{4,7},{9,8},{10,9},{11,1... | collective-permute-start | bytes 65288 | tf_op jit(solution)/shard_map/ppermute | solution.py:25
  165.1 6.3 %collective-permute-start.20 = (f32[1,80,1,128]{3,2,1,0:T(1,128)S(1)}, f32[1,80,1,128]{3,2,1,0:T(1,128)S(1)}, u32[]{:S(2)}, u32[]{:S(2)}) collective-permute-start(f32[1,80,1,128]{3,2,1,0:T(1,128)S(1)} %get-tuple-element.40), channel_id=1, source_target_pairs={{0,4},{4,8},{8,12},{12,16},{16,20},{20,24},{24,28},{1,5},{5,9},{9,... | collective-permute-start | bytes 122888 | tf_op jit(solution)/shard_map/ppermute | solution.py:22
  170.1 3.1 collective-permute-start.21
  177.5 5.8 %collective-permute-start.22 = (f32[1,80,34,1]{1,3,2,0:T(1,128)S(1)}, f32[1,80,34,1]{1,3,2,0:T(1,128)S(1)}, u32[]{:S(2)}, u32[]{:S(2)}) collective-permute-start(f32[1,80,34,1]{1,3,2,0:T(1,128)S(1)} %copy.30), channel_id=1, source_target_pairs={{0,1},{1,2},{2,3},{3,0},{4,5},{5,6},{6,7},{7,4},{8,9},{9,10},{10,1... | collective-permute-start | bytes 32648 | tf_op jit(solution)/shard_map/ppermute | solution.py:22
  179.4 5.6 %collective-permute-start.23 = (f32[1,80,34,1]{1,3,2,0:T(1,128)S(1)}, f32[1,80,34,1]{1,3,2,0:T(1,128)S(1)}, u32[]{:S(2)}, u32[]{:S(2)}) collective-permute-start(f32[1,80,34,1]{1,3,2,0:T(1,128)S(1)} %copy.31), channel_id=1, source_target_pairs={{1,0},{2,1},{3,2},{0,3},{5,4},{6,5},{7,6},{4,7},{9,8},{10,9},{11,1... | collective-permute-start | bytes 32648 | tf_op jit(solution)/shard_map/ppermute | solution.py:25
  186.8 3.8 copy-start.6
  186.8 3.8 copy-start.8
  195.2 8.1 %collective-permute-start.24 = (f32[80,32,128]{2,1,0:T(8,128)S(1)}, f32[80,32,128]{2,1,0:T(8,128)S(1)}, u32[]{:S(2)}, u32[]{:S(2)}) collective-permute-start(f32[80,32,128]{2,1,0:T(8,128)S(1)} %add_multiply_fusion.1), channel_id=1, source_target_pairs={{0,4},{4,8},{8,12},{12,16},{16,20},{20,24},{24,28},{1,5},{5,9},{9,... | collective-permute-start | bytes 3932168 | tf_op jit(solution)/shard_map/ppermute | solution.py:22
  200.8 4.9 %collective-permute-start.25 = (f32[80,32,128]{2,1,0:T(8,128)S(1)}, f32[80,32,128]{2,1,0:T(8,128)S(1)}, u32[]{:S(2)}, u32[]{:S(2)}) collective-permute-start(f32[80,32,128]{2,1,0:T(8,128)S(1)} %add_multiply_fusion.1), channel_id=1, source_target_pairs={{4,0},{8,4},{12,8},{16,12},{20,16},{24,20},{28,24},{5,1},{9,5},{13... | collective-permute-start | bytes 3932168 | tf_op jit(solution)/shard_map/ppermute | solution.py:25
  212.0 6.7 %copy-start.27 = (s32[2]{0:T(128)S(1)}, s32[2]{0:T(128)}, u32[]{:S(2)}) copy-start(s32[2]{0:T(128)} %param.13) | copy-start | bytes 28
  212.0 11.3 %collective-permute-start.26 = (f32[80,32,32]{0,2,1:T(8,128)S(1)}, f32[80,32,32]{0,2,1:T(8,128)}, u32[]{:S(2)}, u32[]{:S(2)}) collective-permute-start(f32[80,32,32]{0,2,1:T(8,128)S(1)} %copy.34), channel_id=1, source_target_pairs={{0,1},{1,2},{2,3},{3,0},{4,5},{5,6},{6,7},{7,4},{8,9},{9,10},{10,1... | collective-permute-start | bytes 983048 | tf_op jit(solution)/shard_map/ppermute | solution.py:22
  214.9 13.9 %collective-permute-start.27 = (f32[80,32,32]{0,2,1:T(8,128)}, f32[80,32,32]{0,2,1:T(8,128)}, u32[]{:S(2)}, u32[]{:S(2)}) collective-permute-start(f32[80,32,32]{0,2,1:T(8,128)} %copy.35), channel_id=1, source_target_pairs={{1,0},{2,1},{3,2},{0,3},{5,4},{6,5},{7,6},{4,7},{9,8},{10,9},{11,1... | collective-permute-start | bytes 983048 | tf_op jit(solution)/shard_map/ppermute | solution.py:25
  317.5 3.9 collective-permute-start.28
  318.9 7.4 %collective-permute-start.29 = (f32[80,32,128]{2,1,0:T(8,128)S(1)}, f32[80,32,128]{2,1,0:T(8,128)S(1)}, u32[]{:S(2)}, u32[]{:S(2)}) collective-permute-start(f32[80,32,128]{2,1,0:T(8,128)S(1)} %add_multiply_fusion), channel_id=1, source_target_pairs={{4,0},{8,4},{12,8},{16,12},{20,16},{24,20},{28,24},{5,1},{9,5},{13... | collective-permute-start | bytes 3932168 | tf_op jit(solution)/shard_map/ppermute | solution.py:25
  332.5 11.2 %collective-permute-start.30 = (f32[80,32,32]{0,2,1:T(8,128)S(1)}, f32[80,32,32]{0,2,1:T(8,128)}, u32[]{:S(2)}, u32[]{:S(2)}) collective-permute-start(f32[80,32,32]{0,2,1:T(8,128)S(1)} %copy.38), channel_id=1, source_target_pairs={{0,1},{1,2},{2,3},{3,0},{4,5},{5,6},{6,7},{7,4},{8,9},{9,10},{10,1... | collective-permute-start | bytes 983048 | tf_op jit(solution)/shard_map/ppermute | solution.py:22
  337.5 11.7 %collective-permute-start.31 = (f32[80,32,32]{0,2,1:T(8,128)}, f32[80,32,32]{0,2,1:T(8,128)}, u32[]{:S(2)}, u32[]{:S(2)}) collective-permute-start(f32[80,32,32]{0,2,1:T(8,128)} %copy.39), channel_id=1, source_target_pairs={{1,0},{2,1},{3,2},{0,3},{5,4},{6,5},{7,6},{4,7},{9,8},{10,9},{11,1... | collective-permute-start | bytes 983048 | tf_op jit(solution)/shard_map/ppermute | solution.py:25
  433.2 2.1 copy-start.2
  (12 other events, 16.9 us)
where the time goes:
time: 448 us; the launch traced here: 439 us
  blocking collectives  148 us (33%)
  local copies, waits for them, and re-layouts  108 us (24%)
  starting transfers between devices  76.2 us (17%)
  other arithmetic  50.1 us (11%)
  waiting for transfers between devices  34.4 us (8%)
  matrix products  17.9 us (4%)
  between operations  4.52 us (1%)
    psum x2, blocking collectives, descend(): square_total = lax.psum(jnp.sum(gradient * gradient), ('member', 'band'))  148 us
    slice x19, local copies, waits for them, and re-layouts, extended(): lax.slice_in_dim(block, block.shape[dim] - width, None, axis=dim)  40.2 us
    ppermute x16, starting transfers between devices, extended(): lax.ppermute(lax.slice_in_dim(block, block.shape[dim] - width, None, axis...  38.5 us
    ppermute x16, starting transfers between devices, extended(): lax.ppermute(lax.slice_in_dim(block, 0, width, axis=dim), axis, backward)  37.7 us
    ppermute x16, waiting for transfers between devices, extended(): lax.ppermute(lax.slice_in_dim(block, 0, width, axis=dim), axis, backward)  24.9 us
    concatenate x9, other arithmetic, extended(): block = jnp.concatenate([low, block, high], axis=dim)  22.9 us
    slice x8, local copies, waits for them, and re-layouts, extended(): lax.slice_in_dim(block, 0, width, axis=dim)  19.9 us
    ppermute x8, local copies, waits for them, and re-layouts, extended(): lax.ppermute(lax.slice_in_dim(block, 0, width, axis=dim), axis, backward)  18.9 us
  transfers between devices with their start and end apart: 32, of which 14 were waited for; matrix products, arithmetic and copies ran while one was open for 9% of the time, Pallas kernels for 0%

commit v1 on v0

v1 whole, which is shorter than its diff:
```python
import functools

import jax
import jax.numpy as jnp
import numpy as np
from jax import lax
from jax.experimental import pallas as pl
from jax.experimental.pallas import tpu as pltpu
from jax.sharding import PartitionSpec as P

STEPS = 3
ITERS = 2
LWIDTH = 32
LSCALE = 12

LANES = 128
SUB = 8
SLOT = 16
EAST, SIDE = 2 * STEPS, 2 * STEPS - 1
PACK = LANES // SLOT
FOLD = LANES // LWIDTH

VMEM = pl.BlockSpec(memory_space=pltpu.VMEM)
SMEM = pl.BlockSpec(memory_space=pltpu.SMEM)


def f32(*shape):
    return jax.ShapeDtypeStruct(shape, jnp.float32)


def iota(shape, axis):
    return lax.broadcasted_iota(jnp.int32, shape, axis)


def spin(block, shift, axis):
    shift %= block.shape[axis]
    return block if shift == 0 else pltpu.roll(block, shift, axis)


def shifted(block, axis, step, periodic):
    count = lax.axis_size(axis)
    if periodic:
        pairs = [(i, (i + step) % count) for i in range(count)]
    else:
        pairs = [(i, i + step) for i in range(count) if 0 <= i + step < count]
    return lax.ppermute(block, axis, pairs)


def everywhere_sum(block):
    for axis in ("band", "member"):
        count = lax.axis_size(axis)
        if count & (count - 1):
            block = lax.psum(block, axis)
            continue
        reach = 1
        while reach < count:
            block = block + lax.ppermute(block, axis, [(i, i ^ reach) for i in range(count)])
            reach *= 2
    return block


def taper(offset):
    scaled = offset.astype(np.float32) / np.float32(LSCALE)
    weight = np.exp(np.float32(-0.5) * scaled * scaled)
    return np.where(np.abs(offset) <= LWIDTH, weight, np.float32(0)).astype(np.float32)


def two_terms(table):
    high = table.astype(jnp.bfloat16)
    low = (table - high.astype(np.float32)).astype(jnp.bfloat16)
    return high, low


def row_table(rows):
    out = np.arange(rows)[:, None]
    table = taper(np.arange(rows + 2 * LWIDTH)[None, :] - LWIDTH - out)
    high, low = two_terms(table)
    return np.block([[high, high], [low, np.zeros_like(low)]])


def column_table(cols):
    out = np.arange(cols)
    high, low = two_terms(taper(out[:, None] - out[None, :]))
    return np.block([[high, low], [high, np.zeros_like(low)]])


def strip_table(cols):
    near = np.arange(LWIDTH)
    left = taper((near - LWIDTH)[:, None] - near[None, :])
    right = taper((cols + near)[:, None] - (cols - LWIDTH + near)[None, :])
    table = np.zeros((2 * LANES, 2 * LANES), np.float32)
    for k in range(FOLD):
        src, dst = k * LWIDTH, 2 * k * LWIDTH
        table[src : src + LWIDTH, dst + LWIDTH : dst + 2 * LWIDTH] = left
        table[LANES + src : LANES + src + LWIDTH, dst : dst + LWIDTH] = right
    return two_terms(table)


def split(block):
    high = block.astype(jnp.bfloat16)
    low = (block - high.astype(jnp.float32)).astype(jnp.bfloat16)
    return high, low


def mm(a, b):
    return jnp.dot(a, b, preferred_element_type=jnp.float32)


def slot_pack(east, north, height, k, side):
    cols = east.shape[-1]
    lane = iota(east.shape, 1) - SLOT * k
    base = SLOT * k
    skip = (cols - EAST, cols - SIDE) if side else (0, 0)
    e = spin(east, base - skip[0], 1)
    n = spin(north, base + EAST - skip[1], 1)
    h = spin(height, base + EAST + SIDE - skip[1], 1)
    inner = jnp.where(lane < EAST, e, jnp.where(lane < EAST + SIDE, n, h))
    return jnp.where((lane >= 0) & (lane < SLOT), inner, 0.0)


def pack_kernel(h_ref, u_ref, v_ref, top_ref, bottom_ref, left_ref, right_ref):
    rows = h_ref.shape[1]
    sub = iota((SUB, LANES), 0)
    left = right = None
    for k in range(PACK):
        u, v, h = u_ref[k], v_ref[k], h_ref[k]
        uf, vf, hf = u[:SUB], v[:SUB], h[:SUB]
        top_ref[k, :SUB] = jnp.where(sub < 6, vf, spin(uf, 6, 0))
        top_ref[k, SUB:] = jnp.where(sub < 5, hf, spin(uf, 3, 0))
        ul, vl, hl = u[rows - SUB :], v[rows - SUB :], h[rows - SUB :]
        bottom_ref[k, :SUB] = jnp.where(sub < 2, spin(ul, 5, 0), vl)
        bottom_ref[k, SUB:] = jnp.where(sub < 3, spin(ul, 3, 0), hl)
        l, r = slot_pack(u, v, h, k, 0), slot_pack(u, v, h, k, 1)
        left, right = (l, r) if k == 0 else (left + l, right + r)
    left_ref[0] = left
    right_ref[0] = right


def pack_halos(height, eastward, northward):
    members, rows, cols = height.shape
    tile = pl.BlockSpec((PACK, rows, cols), lambda g: (g, 0, 0))
    edge = pl.BlockSpec((PACK, 2 * SUB, cols), lambda g: (g, 0, 0))
    strip = pl.BlockSpec((1, rows, LANES), lambda g: (g, 0, 0))
    groups = members // PACK
    return pl.pallas_call(
        pack_kernel,
        name="pack_halos",
        grid=(groups,),
        in_specs=[tile] * 3,
        out_specs=[edge, edge, strip, strip],
        out_shape=[f32(members, 2 * SUB, cols)] * 2 + [f32(groups, rows, LANES)] * 2,
    )(height, eastward, northward)


def forecast_kernel(
    h_ref, u_ref, v_ref, above_ref, below_ref, ownl_ref, ownr_ref, hall_ref, halr_ref,
    cornu_ref, cornd_ref, obs_ref, edge_ref,
    ho_ref, uo_ref, vo_ref, mean_ref, contrib_ref,
    ext_ref, wall_ref, sum_ref,
):
    members, rows, cols = h_ref.shape
    groups = members // PACK
    tall = rows + 2 * SUB
    lane = iota((tall, LANES), 1)
    slot = lane % SLOT
    row = iota((tall, LANES), 0)
    sub = iota((SUB, LANES), 0)
    outside = ((row < SUB) & (edge_ref[0] == 1)) | ((row >= rows + SUB) & (edge_ref[1] == 1))
    pull = jnp.where(outside, 0.0, 0.2)

    def dy(x):
        return spin(x, -1, 0) - spin(x, 1, 0)

    def march(h, u, v, dx):
        dh = dx(u)
        h = h - pull * (dh + dy(v))
        new_u = u + 0.1 * v - pull * dx(h)
        new_v = v - 0.1 * u - pull * dy(h)
        return h, new_u, new_v

    def flat(x):
        return spin(x, -1, 1) - spin(x, 1, 1)

    def group(g, _):
        packs = [[None, None], [None, None]]
        for k in range(PACK):
            m = g * PACK + k
            a0, a1 = above_ref[m, :SUB], above_ref[m, SUB:]
            b0, b1 = below_ref[m, :SUB], below_ref[m, SUB:]
            ua = jnp.where(sub < 5, spin(a0, 3, 0), spin(a1, 5, 0))
            ub = jnp.where(sub < 2, spin(b0, 2, 0), spin(b1, 5, 0))
            ext_ref[k, 0, :SUB] = ua
            ext_ref[k, 0, rows + SUB :] = ub
            for end, (u, v, h) in enumerate(((ua, a0, a1), (ub, b0, b1))):
                for side in (0, 1):
                    piece = slot_pack(u, v, h, k, side)
                    packs[side][end] = piece if k == 0 else packs[side][end] + piece
        own = [
            jnp.concatenate([packs[0][0], ownl_ref[g], packs[0][1]], axis=0),
            jnp.concatenate([packs[1][0], ownr_ref[g], packs[1][1]], axis=0),
        ]
        hal = [
            jnp.concatenate([cornu_ref[g], hall_ref[g], cornd_ref[g]], axis=0),
            jnp.concatenate([cornu_ref[groups + g], halr_ref[g], cornd_ref[groups + g]], axis=0),
        ]

        def fields(first, second, at, meet, length):
            out = []
            for start, size in ((0, EAST), (EAST, SIDE), (EAST + SIDE, SIDE)):
                head = spin(first, meet - size - start, 1)
                tail = spin(second, meet - start, 1)
                out.append(jnp.where(slot < meet, head, tail))
            return out

        lu, lv, lh = fields(hal[0], own[0], 2, SUB, EAST)
        ru, rv, rh = fields(own[1], hal[1], 0, EAST, EAST)
        for step in range(STEPS):
            wall_ref[2 * step] = jnp.where(slot == SUB - 1, lu, ru)
            lh, lu, lv = march(lh, lu, lv, flat)
            rh, ru, rv = march(rh, ru, rv, flat)
            wall_ref[2 * step + 1] = jnp.where(slot == SUB - 1, lh, rh)

        sums = [sum_ref[0], sum_ref[1], sum_ref[2]]
        for k in range(PACK):
            m = g * PACK + k
            u = jnp.concatenate([ext_ref[k, 0, :SUB], u_ref[m], ext_ref[k, 0, rows + SUB :]], 0)
            v = jnp.concatenate([above_ref[m, :SUB], v_ref[m], below_ref[m, :SUB]], 0)
            h = jnp.concatenate([above_ref[m, SUB:], h_ref[m], below_ref[m, SUB:]], 0)
            stage = [0]

            def dx(x):
                wall = spin(wall_ref[stage[0]], -(SLOT * k + SUB - 1), 1)
                stage[0] += 1
                ahead = jnp.where(lane == LANES - 1, wall, spin(x, -1, 1))
                behind = jnp.where(lane == 0, wall, spin(x, 1, 1))
                return ahead - behind

            for step in range(STEPS):
                h, u, v = march(h, u, v, dx)
            h, u, v = (x[SUB : rows + SUB] for x in (h, u, v))
            ho_ref[m], uo_ref[m], vo_ref[m] = h, u, v
            sums = [s + x for s, x in zip(sums, (h, u, v))]
        for i in range(3):
            sum_ref[i] = sums[i]
        return 0

    sum_ref[...] = jnp.zeros_like(sum_ref)
    lax.fori_loop(0, groups, group, 0)
    mh, mu, mv = (sum_ref[i] / members for i in range(3))
    mean_ref[0], mean_ref[1], mean_ref[2] = mh, mu, mv
    contributions(
        (ho_ref, uo_ref, vo_ref), (mh, mu, mv), (mh, mu, mv), obs_ref, contrib_ref
    )


def contributions(fields, means, states, obs_ref, contrib_ref):
    members = contrib_ref.shape[0]
    scale = 1.0 / float(np.sqrt(np.float32(members - 1)))
    mh, mu, mv = means
    sh, su, sv = states
    residual = obs_ref[1] * (obs_ref[0] - sh - 0.15 * (su * su + sv * sv))
    residual = residual * scale
    eu, ev = 0.3 * su, 0.3 * sv

    def member(m, _):
        h, u, v = (ref[m] for ref in fields)
        contrib_ref[m] = ((h - mh) + (eu * (u - mu) + ev * (v - mv))) * residual
        return 0

    lax.fori_loop(0, members, member, 0, unroll=4)


def forecast(h, u, v, above, below, ownl, ownr, hall, halr, cornu, cornd, obs, edge):
    members, rows, cols = h.shape
    tall = rows + 2 * SUB
    return pl.pallas_call(
        forecast_kernel,
        name="forecast",
        in_specs=[VMEM] * 12 + [SMEM],
        out_specs=[VMEM] * 5,
        out_shape=[f32(members, rows, cols)] * 3 + [f32(3, rows, cols), f32(members, rows, cols)],
        scratch_shapes=[
            pltpu.VMEM((PACK, 1, tall, LANES), jnp.float32),
            pltpu.VMEM((2 * STEPS, tall, LANES), jnp.float32),
            pltpu.VMEM((3, rows, cols), jnp.float32),
        ],
    )(h, u, v, above, below, ownl, ownr, hall, halr, cornu, cornd, obs, edge)


def rows_kernel(x_ref, above_ref, below_ref, table_ref, out_ref, left_ref, right_ref):
    members, rows, cols = x_ref.shape
    lane = iota((rows, LANES), 1)
    table = table_ref[...]

    def fold(g, _):
        left = right = None
        for pair in range(FOLD // 2):
            halves = []
            for k in (2 * pair, 2 * pair + 1):
                m = g * FOLD + k
                high, low = split(jnp.concatenate([above_ref[m], x_ref[m], below_ref[m]], axis=0))
                halves.append(jnp.concatenate([high, low], axis=0))
            both = mm(table, jnp.concatenate(halves, axis=1))
            both = both[:rows] + both[rows:]
            for k in (2 * pair, 2 * pair + 1):
                y = both[:, (k % 2) * cols : (k % 2 + 1) * cols]
                out_ref[g * FOLD + k] = y
                here = lane // LWIDTH == k
                l = jnp.where(here, spin(y, LWIDTH * k, 1), 0.0)
                r = jnp.where(here, spin(y, LWIDTH * k + LWIDTH - cols, 1), 0.0)
                left, right = (l, r) if k == 0 else (left + l, right + r)
        left_ref[g] = left
        right_ref[g] = right
        return 0

    lax.fori_loop(0, members // FOLD, fold, 0)


def taper_rows(x, above, below):
    members, rows, cols = x.shape
    folds = members // FOLD
    return pl.pallas_call(
        rows_kernel,
        name="taper_rows",
        in_specs=[VMEM] * 4,
        out_specs=[VMEM] * 3,
        out_shape=[f32(members, rows, cols)] + [f32(folds, rows, LANES)] * 2,
    )(x, above, below, row_table(rows))


def columns_kernel(
    first, x_ref, left_ref, right_ref, h_ref, u_ref, v_ref, mean_ref, *refs
):
    if first:
        table_ref, high_ref, low_ref, grad_ref, sums_ref, square_ref = refs
    else:
        prev_ref, factor_ref, table_ref, high_ref, low_ref, sums_ref, square_ref = refs
    members, rows, cols = x_ref.shape
    scale = 1.0 / float(np.sqrt(np.float32(members - 1)))
    lane = iota((rows, LANES), 1)
    rim = (lane < LWIDTH) | (lane >= cols - LWIDTH)
    table, high_table, low_table = table_ref[...], high_ref[...], low_ref[...]
    means = [mean_ref[i] for i in range(3)]
    fields = (h_ref, u_ref, v_ref)

    def fold(g, carry):
        sums, square = carry
        xh, xl = split(jnp.concatenate([left_ref[g], right_ref[g]], axis=1))
        strips = mm(xh, high_table) + (mm(xl, high_table) + mm(xh, low_table))
        block = jnp.concatenate([x_ref[g * FOLD + k] for k in range(FOLD)], axis=0)
        bh, bl = split(block)
        both = mm(jnp.concatenate([bh, bl], axis=1), table)
        both = both[:, :cols] + both[:, cols:]
        for k in range(FOLD):
            m = g * FOLD + k
            at = 2 * k * LWIDTH
            part = strips[:, at // LANES * LANES : at // LANES * LANES + LANES]
            part = spin(part, -(at % LANES + LWIDTH), 1)
            y = both[k * rows : (k + 1) * rows] + jnp.where(rim, part, 0.0)
            if first:
                grad_ref[m] = y
            else:
                y = factor_ref[0] * prev_ref[m] - y
            square = square + y * y
            sums = [s + (ref[m] - mean) * y for s, ref, mean in zip(sums, fields, means)]
        return sums, square

    zero = jnp.zeros((rows, cols), jnp.float32)
    sums, square = lax.fori_loop(0, members // FOLD, fold, ([zero] * 3, zero))
    for i in range(3):
        sums_ref[i] = sums[i] * scale
    total = square[:SUB]
    for start in range(SUB, rows, SUB):
        total = total + square[start : start + SUB]
    square_ref[...] = total


def taper_columns(x, left, right, fields, means, prev=None, factor=None):
    members, rows, cols = x.shape
    first = prev is None
    high, low = strip_table(cols)
    operands = [x, left, right, *fields, means]
    specs = [VMEM] * 7
    if not first:
        operands += [prev, factor]
        specs += [VMEM, SMEM]
    operands += [column_table(cols), high, low]
    specs += [VMEM] * 3
    outs = [f32(3, rows, cols), f32(SUB, LANES)]
    if first:
        outs = [f32(members, rows, cols)] + outs
    return pl.pallas_call(
        functools.partial(columns_kernel, first),
        name="taper_columns",
        in_specs=specs,
        out_specs=[VMEM] * len(outs),
        out_shape=outs,
    )(*operands)


def contrib_kernel(h_ref, u_ref, v_ref, mean_ref, sums_ref, obs_ref, factor_ref, contrib_ref):
    means = [mean_ref[i] for i in range(3)]
    states = [mean_ref[i] + factor_ref[0] * sums_ref[i] for i in range(3)]
    contributions((h_ref, u_ref, v_ref), means, states, obs_ref, contrib_ref)


def second_contributions(fields, means, sums, obs, factor):
    return pl.pallas_call(
        contrib_kernel,
        name="second_contributions",
        in_specs=[VMEM] * 6 + [SMEM],
        out_specs=VMEM,
        out_shape=f32(*fields[0].shape),
    )(*fields, means, sums, obs, factor)


def per_device(
    height_start, east_start, north_start, obs_value, obs_mask, obs_precision, step_sizes
):
    members, rows, cols = height_start.shape
    top, bottom, ownl, ownr = pack_halos(height_start, east_start, north_start)
    hall = shifted(ownr, "band", 1, True)
    halr = shifted(ownl, "band", -1, True)
    above = shifted(bottom, "member", 1, False)
    below = shifted(top, "member", -1, False)
    ends = jnp.concatenate([hall, halr], axis=0)
    cornu = shifted(ends[:, rows - SUB :], "member", 1, False)
    cornd = shifted(ends[:, :SUB], "member", -1, False)

    obs = jnp.stack([obs_value, obs_mask.astype(jnp.float32) * obs_precision])
    here = lax.axis_index("member")
    edge = jnp.stack([here == 0, here == lax.axis_size("member") - 1]).astype(jnp.int32)
    h, u, v, means, contrib = forecast(
        height_start, east_start, north_start, above, below, ownl, ownr, hall, halr,
        cornu, cornd, obs, edge,
    )
    fields = (h, u, v)
    cells = float(members * rows * cols * lax.axis_size("member") * lax.axis_size("band"))

    def localized(contrib, *more):
        above = shifted(contrib, "member", 1, False)
        below = shifted(contrib, "member", -1, False)
        x, first, last = taper_rows(contrib, above, below)
        left = shifted(last, "band", 1, True)
        right = shifted(first, "band", -1, True)
        return taper_columns(x, left, right, fields, means, *more)

    def factor_of(square, k):
        total = jnp.sum(everywhere_sum(square))
        return step_sizes[k].astype(jnp.float32) / 64.0 / jnp.sqrt(total / cells + 1e-06)

    smooth, sums0, square = localized(contrib)
    f0 = factor_of(square, 0)
    contrib = second_contributions(fields, means, sums0, obs, f0[None])
    sums1, square = localized(contrib, smooth, f0[None])
    f1 = factor_of(square, 1)
    increment = f0 * sums0 - f1 * sums1
    return tuple(field + increment[i] for i, field in enumerate(fields))


def solution(mesh):
    tile, flat = P(None, "member", "band"), P("member", "band")
    return jax.shard_map(
        per_device,
        mesh=mesh,
        in_specs=(tile, tile, tile, flat, flat, flat, P()),
        out_specs=(tile, tile, tile),
        check_vma=False,
    )
```

time: 448 us -> 259 us (0.58); the launches traced: 439 us -> 259 us
  blocking collectives: 148 us -> 0 us
  local copies, waits for them, and re-layouts: 108 us -> 6.98 us
  Pallas kernels: 0 us -> 86.4 us
  other arithmetic: 50.1 us -> 7.65 us
  starting transfers between devices: 76.2 us -> 106 us
  matrix products: 17.9 us -> 0 us
  waiting for transfers between devices: 34.4 us -> 48.1 us
    psum x2 -> x0, blocking collectives: 148 us -> none  [descend(): square_total = lax.psum(jnp.sum(gradient * gradient), ('member', 'band'))]
    pallas_call x0 -> x7, Pallas kernels: none -> 86.4 us  [the longest x1 38.2 us: forecast(): pl.pallas_call(forecast_kernel, name='forecast', in_specs=[VMEM] * 12 + [...]
    slice x28 -> x2, local copies, waits for them, and re-layouts: 60.7 us -> 0.59 us  [the longest x1 0.58 us: factor_of(): step_sizes[k].astype(jnp.float32) / 64.0 / jnp.sqrt(total / cells + 1e-06)]
    ppermute x16 -> x0, local copies, waits for them, and re-layouts: 37.8 us -> none  [the longest x8 18.9 us: extended(): lax.ppermute(lax.slice_in_dim(block, 0, width, axis=dim), axis, backward)]
    ppermute x32 -> x24, starting transfers between devices: 76.2 us -> 106 us  [the longest x10 69.8 us: everywhere_sum(): lax.ppermute(block, axis, [(i, i ^ reach) for i in range(count)])]
    concatenate x9 -> x0, other arithmetic: 22.9 us -> none  [extended(): block = jnp.concatenate([low, block, high], axis=dim)]
    dot_general x4 -> x0, matrix products: 17.9 us -> none  [the longest x2 13.3 us: taper_columns(): result = jnp.einsum('mrjk,bk->mrjb', windows, kernel, precision=highest)]
    ppermute x32 -> x24, waiting for transfers between devices: 34.4 us -> 48.1 us  [the longest x14 26.2 us: shifted(): return lax.ppermute(block, axis, pairs)]
  transfers between devices with their start and end apart: 32 -> 24, of which waited for: 14 -> 20; matrix products, arithmetic and copies ran while one was open for 9% -> 1% of each run, Pallas kernels for 0% -> 0%
where the time goes in v1:
time: 259 us
  starting transfers between devices  106 us (41%)
  Pallas kernels  86.4 us (33%)
  waiting for transfers between devices  48.1 us (19%)
  other arithmetic  7.65 us (3%)
  local copies, waits for them, and re-layouts  6.98 us (3%)
  between operations  3.43 us (1%)
    ppermute x10, starting transfers between devices, everywhere_sum(): lax.ppermute(block, axis, [(i, i ^ reach) for i in range(count)])  69.8 us
    pallas_call x1, Pallas kernels, forecast(): pl.pallas_call(forecast_kernel, name='forecast', in_specs=[VMEM] * 12 + [...  38.2 us
    ppermute x14, starting transfers between devices, shifted(): return lax.ppermute(block, axis, pairs)  36.4 us
    ppermute x14, waiting for transfers between devices, shifted(): return lax.ppermute(block, axis, pairs)  26.2 us
    ppermute x10, waiting for transfers between devices, everywhere_sum(): lax.ppermute(block, axis, [(i, i ^ reach) for i in range(count)])  22 us
    pallas_call x2, Pallas kernels, taper_columns(): pl.pallas_call(functools.partial(columns_kernel, first), name='taper_colu...  19.9 us
    pallas_call x2, Pallas kernels, taper_rows(): pl.pallas_call(rows_kernel, name='taper_rows', in_specs=[VMEM] * 4, out_s...  16.8 us
    pallas_call x1, Pallas kernels, pack_halos(): pl.pallas_call(pack_kernel, name='pack_halos', grid=(groups,), in_specs=[...  7.8 us
  transfers between devices with their start and end apart: 24, of which 20 were waited for; matrix products, arithmetic and copies ran while one was open for 1% of the time, Pallas kernels for 0%

profile of v1, /device:TPU:0, one launch (start us, length us, event | category | flops | bytes accessed | tf_op | source)
XLA Modules:
  0.0 258.8 jit_solution(11571074605201239594)
XLA Ops:
  0.7 7.8 %pack_halos.1 = (f32[80,16,128]{2,1,0:T(8,128)}, f32[80,16,128]{2,1,0:T(8,128)}, f32[10,32,128]{2,1,0:T(8,128)}, f32[10,32,128]{2,1,0:T(8,128)}) custom-call(f32[80,32,128]{2,1,0:T(8,128)} %h_ref.3, f32[80,32,128]{2,1,0:T(8,128)} %u_ref.3, f32[80,32,128]{2,1,0:T(8,128)} %v_ref.3), custom_call_target="tpu_custom_call" | custom-call | tf_op jit(solution)/shard_map/pack_halos/pallas_call | solution.py:145
  8.5 5.1 %collective-permute-start.3 = (f32[10,32,128]{2,1,0:T(8,128)}, f32[10,32,128]{2,1,0:T(8,128)S(1)}, u32[]{:S(2)}, u32[]{:S(2)}) collective-permute-start(f32[10,32,128]{2,1,0:T(8,128)} %get-tuple-element.25.ownl_ref), channel_id=1, source_target_pairs={{0,3},{1,0},{2,1},{3,2},{4,7},{5,4},{6,5},{7,6},{8,11},{9,8},{10,9... | collective-permute-start | bytes 491528 | tf_op jit(solution)/shard_map/ppermute | solution.py:46
  13.6 1.5 collective-permute-start
  15.1 1.3 collective-permute-start.1
  17.0 4.6 %collective-permute-done.2.hall_ref = f32[10,32,128]{2,1,0:T(8,128)S(1)} collective-permute-done((f32[10,32,128]{2,1,0:T(8,128)}, f32[10,32,128]{2,1,0:T(8,128)S(1)}, u32[]{:S(2)}, u32[]{:S(2)}) %collective-permute-start.2) | collective-permute-done | bytes 163872 | tf_op jit(solution)/shard_map/ppermute | solution.py:46
  21.7 1.3 collective-permute-start.5
  23.0 3.0 %collective-permute-start.4 = (f32[20,8,128]{2,1,0:T(8,128)S(1)}, f32[20,8,128]{2,1,0:T(8,128)S(1)}, u32[]{:S(2)}, u32[]{:S(2)}) collective-permute-start(f32[20,8,128]{2,1,0:T(8,128)S(1)} %get-tuple-element.44), channel_id=1, source_target_pairs={{0,4},{4,8},{8,12},{12,16},{16,20},{20,24},{24,28},{1,5},{5,9},{9,... | collective-permute-start | bytes 245768 | tf_op jit(solution)/shard_map/ppermute | solution.py:46
  27.8 0.8 copy-done.10
  28.7 38.2 %forecast.1 = (f32[80,32,128]{2,1,0:T(8,128)}, f32[80,32,128]{2,1,0:T(8,128)}, f32[80,32,128]{2,1,0:T(8,128)}, f32[3,32,128]{2,1,0:T(8,128)}, f32[80,32,128]{2,1,0:T(8,128)}) custom-call(f32[80,32,128]{2,1,0:T(8,128)} %h_ref.3, f32[80,32,128]{2,1,0:T(8,128)} %u_ref.3, f32[80,32,128]{2,1,0:T(8,128)} %v_ref.3, f32[80,16,128]{2,1,0:T(8,128)} %copy-done.9, ...), custom_call_target="tpu_custom_call" | custom-call | tf_op jit(solution)/shard_map/forecast/pallas_call | solution.py:276
  66.9 1.3 collective-permute-start.7
  68.2 10.9 %collective-permute-start.6 = (f32[80,32,128]{2,1,0:T(8,128)}, f32[80,32,128]{2,1,0:T(8,128)S(1)}, u32[]{:S(2)}, u32[]{:S(2)}) collective-permute-start(f32[80,32,128]{2,1,0:T(8,128)} %get-tuple-element.28.x_ref), channel_id=1, source_target_pairs={{0,4},{4,8},{8,12},{12,16},{16,20},{20,24},{24,28},{1,5},{5,9},{9,... | collective-permute-start | bytes 3932168 | tf_op jit(solution)/shard_map/ppermute | solution.py:46
  79.8 2.0 collective-permute-done.6.above_ref
  81.9 1.1 copy-done.6
  82.9 8.4 %taper_rows.2 = (f32[80,32,128]{2,1,0:T(8,128)}, f32[20,32,128]{2,1,0:T(8,128)}, f32[20,32,128]{2,1,0:T(8,128)}) custom-call(f32[80,32,128]{2,1,0:T(8,128)} %get-tuple-element.28.x_ref, f32[80,32,128]{2,1,0:T(8,128)} %copy-done.6, f32[80,32,128]{2,1,0:T(8,128)} %copy-done.4, bf16[64,192]{1,0:T(8,128)(2,1)} %constant.32.clone.table_ref), custom_call_target="tpu_custom_call" | custom-call | tf_op jit(solution)/shard_map/taper_rows/pallas_call | solution.py:322
  91.4 3.8 %collective-permute-start.9 = (f32[20,32,128]{2,1,0:T(8,128)}, f32[20,32,128]{2,1,0:T(8,128)S(1)}, u32[]{:S(2)}, u32[]{:S(2)}) collective-permute-start(f32[20,32,128]{2,1,0:T(8,128)} %get-tuple-element.31), channel_id=1, source_target_pairs={{0,3},{1,0},{2,1},{3,2},{4,7},{5,4},{6,5},{7,6},{8,11},{9,8},{10,9... | collective-permute-start | bytes 983048 | tf_op jit(solution)/shard_map/ppermute | solution.py:46
  95.2 5.4 %collective-permute-done.8.left_ref = f32[20,32,128]{2,1,0:T(8,128)S(1)} collective-permute-done((f32[20,32,128]{2,1,0:T(8,128)}, f32[20,32,128]{2,1,0:T(8,128)S(1)}, u32[]{:S(2)}, u32[]{:S(2)}) %collective-permute-start.8) | collective-permute-done | bytes 327712 | tf_op jit(solution)/shard_map/ppermute | solution.py:46
  100.5 1.6 collective-permute-done.9.right_ref
  102.9 9.9 %taper_columns.2 = (f32[80,32,128]{2,1,0:T(8,128)}, f32[3,32,128]{2,1,0:T(8,128)}, f32[8,128]{1,0:T(8,128)}) custom-call(f32[80,32,128]{2,1,0:T(8,128)} %get-tuple-element.29.x_ref, f32[20,32,128]{2,1,0:T(8,128)} %copy-done.13, f32[20,32,128]{2,1,0:T(8,128)} %copy-done.14, f32[80,32,128]{2,1,0:T(8,128)} %get-tuple-element.27.h_ref, ...), custom_call_target="tpu_custom_call" | custom-call | tf_op jit(solution)/shard_map/taper_columns/pallas_call | solution.py:392
  112.8 2.4 collective-permute-start.10
  115.2 1.8 collective-permute-done.10
  117.6 2.1 collective-permute-start.11
  119.8 4.1 %collective-permute-done.11 = f32[8,128]{1,0:T(8,128)S(1)} collective-permute-done((f32[8,128]{1,0:T(8,128)S(1)}, f32[8,128]{1,0:T(8,128)S(1)}, u32[]{:S(2)}, u32[]{:S(2)}) %collective-permute-start.11) | collective-permute-done | bytes 4128 | tf_op jit(solution)/shard_map/ppermute | solution.py:57
  123.8 19.4 %collective-permute-start.12 = (f32[8,128]{1,0:T(8,128)S(1)}, f32[8,128]{1,0:T(8,128)S(1)}, u32[]{:S(2)}, u32[]{:S(2)}) collective-permute-start(f32[8,128]{1,0:T(8,128)S(1)} %add.67), channel_id=1, source_target_pairs={{0,4},{4,0},{8,12},{12,8},{16,20},{20,16},{24,28},{28,24},{1,5},{5... | collective-permute-start | bytes 12296 | tf_op jit(solution)/shard_map/ppermute | solution.py:57
  143.2 0.8 collective-permute-done.12
  144.0 8.8 %collective-permute-start.13 = (f32[8,128]{1,0:T(8,128)S(1)}, f32[8,128]{1,0:T(8,128)S(1)}, u32[]{:S(2)}, u32[]{:S(2)}) collective-permute-start(f32[8,128]{1,0:T(8,128)S(1)} %add.68), channel_id=1, source_target_pairs={{0,8},{4,12},{8,0},{12,4},{16,24},{20,28},{24,16},{28,20},{1,9},{5... | collective-permute-start | bytes 12296 | tf_op jit(solution)/shard_map/ppermute | solution.py:57
  152.9 1.6 collective-permute-done.13
  154.5 4.1 %collective-permute-start.14 = (f32[8,128]{1,0:T(8,128)S(1)}, f32[8,128]{1,0:T(8,128)S(1)}, u32[]{:S(2)}, u32[]{:S(2)}) collective-permute-start(f32[8,128]{1,0:T(8,128)S(1)} %add.69), channel_id=1, source_target_pairs={{0,16},{4,20},{8,24},{12,28},{16,0},{20,4},{24,8},{28,12},{1,17},{... | collective-permute-start | bytes 12296 | tf_op jit(solution)/shard_map/ppermute | solution.py:57
  161.4 3.7 %second_contributions.1.x_ref = f32[80,32,128]{2,1,0:T(8,128)} custom-call(f32[80,32,128]{2,1,0:T(8,128)} %get-tuple-element.27.h_ref, f32[80,32,128]{2,1,0:T(8,128)} %get-tuple-element.32.u_ref, f32[80,32,128]{2,1,0:T(8,128)} %get-tuple-element.33.v_ref, f32[3,32,128]{2,1,0:T(8,128)} %get-tuple-element.34.mean_ref, ...), custom_call_target="tpu_custom_call" | custom-call | tf_op jit(solution)/shard_map/second_contributions/pallas_call | solution.py:408
  165.1 1.3 collective-permute-start.16
  166.4 3.1 %collective-permute-start.15 = (f32[80,32,128]{2,1,0:T(8,128)}, f32[80,32,128]{2,1,0:T(8,128)S(1)}, u32[]{:S(2)}, u32[]{:S(2)}) collective-permute-start(f32[80,32,128]{2,1,0:T(8,128)} %second_contributions.1.x_ref), channel_id=1, source_target_pairs={{0,4},{4,8},{8,12},{12,16},{16,20},{20,24},{24,28},{1,5},{5,9},{9,... | collective-permute-start | bytes 3932168 | tf_op jit(solution)/shard_map/ppermute | solution.py:46
  170.2 2.0 collective-permute-done.15.above_ref
  172.3 1.1 copy-done.5
  173.4 8.4 %taper_rows.3 = (f32[80,32,128]{2,1,0:T(8,128)}, f32[20,32,128]{2,1,0:T(8,128)}, f32[20,32,128]{2,1,0:T(8,128)}) custom-call(f32[80,32,128]{2,1,0:T(8,128)} %second_contributions.1.x_ref, f32[80,32,128]{2,1,0:T(8,128)} %copy-done.5, f32[80,32,128]{2,1,0:T(8,128)} %copy-done.3, bf16[64,192]{1,0:T(8,128)(2,1)} %constant.32.clone.table_ref), custom_call_target="tpu_custom_call" | custom-call | tf_op jit(solution)/shard_map/taper_rows/pallas_call | solution.py:322
  181.8 2.0 collective-permute-start.17
  183.8 1.8 collective-permute-start.18
  185.6 5.4 %collective-permute-done.17.left_ref = f32[20,32,128]{2,1,0:T(8,128)S(1)} collective-permute-done((f32[20,32,128]{2,1,0:T(8,128)}, f32[20,32,128]{2,1,0:T(8,128)S(1)}, u32[]{:S(2)}, u32[]{:S(2)}) %collective-permute-start.17) | collective-permute-done | bytes 327712 | tf_op jit(solution)/shard_map/ppermute | solution.py:46
  190.9 3.4 %collective-permute-done.18.right_ref = f32[20,32,128]{2,1,0:T(8,128)S(1)} collective-permute-done((f32[20,32,128]{2,1,0:T(8,128)}, f32[20,32,128]{2,1,0:T(8,128)S(1)}, u32[]{:S(2)}, u32[]{:S(2)}) %collective-permute-start.18) | collective-permute-done | bytes 327712 | tf_op jit(solution)/shard_map/ppermute | solution.py:46
  195.1 10.0 %taper_columns.3 = (f32[3,32,128]{2,1,0:T(8,128)}, f32[8,128]{1,0:T(8,128)}) custom-call(f32[80,32,128]{2,1,0:T(8,128)} %get-tuple-element.37.x_ref, f32[20,32,128]{2,1,0:T(8,128)} %copy-done.11, f32[20,32,128]{2,1,0:T(8,128)} %copy-done.12, f32[80,32,128]{2,1,0:T(8,128)} %get-tuple-element.27.h_ref, f32[80,32,128]{2,1,0:T(8,128)} %get-tuple-element.32.u_ref, ...), custom_call_target="tpu_custom_call" | custom-call | tf_op jit(solution)/shard_map/taper_columns/pallas_call | solution.py:392
  205.6 5.5 %collective-permute-done.19 = f32[8,128]{1,0:T(8,128)S(1)} collective-permute-done((f32[8,128]{1,0:T(8,128)}, f32[8,128]{1,0:T(8,128)S(1)}, u32[]{:S(2)}, u32[]{:S(2)}) %collective-permute-start.19) | collective-permute-done | bytes 4128 | tf_op jit(solution)/shard_map/ppermute | solution.py:57
  211.8 4.5 %collective-permute-done.20 = f32[8,128]{1,0:T(8,128)S(1)} collective-permute-done((f32[8,128]{1,0:T(8,128)S(1)}, f32[8,128]{1,0:T(8,128)S(1)}, u32[]{:S(2)}, u32[]{:S(2)}) %collective-permute-start.20) | collective-permute-done | bytes 4128 | tf_op jit(solution)/shard_map/ppermute | solution.py:57
  216.3 15.4 %collective-permute-start.21 = (f32[8,128]{1,0:T(8,128)S(1)}, f32[8,128]{1,0:T(8,128)S(1)}, u32[]{:S(2)}, u32[]{:S(2)}) collective-permute-start(f32[8,128]{1,0:T(8,128)S(1)} %add.73), channel_id=1, source_target_pairs={{0,4},{4,0},{8,12},{12,8},{16,20},{20,16},{24,28},{28,24},{1,5},{5... | collective-permute-start | bytes 12296 | tf_op jit(solution)/shard_map/ppermute | solution.py:57
  231.6 0.8 collective-permute-done.21
  232.5 8.2 %collective-permute-start.22 = (f32[8,128]{1,0:T(8,128)S(1)}, f32[8,128]{1,0:T(8,128)S(1)}, u32[]{:S(2)}, u32[]{:S(2)}) collective-permute-start(f32[8,128]{1,0:T(8,128)S(1)} %add.74), channel_id=1, source_target_pairs={{0,8},{4,12},{8,0},{12,4},{16,24},{20,28},{24,16},{28,20},{1,9},{5... | collective-permute-start | bytes 12296 | tf_op jit(solution)/shard_map/ppermute | solution.py:57
  240.7 1.6 collective-permute-done.22
  242.3 8.9 %collective-permute-start.23 = (f32[8,128]{1,0:T(8,128)S(1)}, f32[8,128]{1,0:T(8,128)S(1)}, u32[]{:S(2)}, u32[]{:S(2)}) collective-permute-start(f32[8,128]{1,0:T(8,128)S(1)} %add.75), channel_id=1, source_target_pairs={{0,16},{4,20},{8,24},{12,28},{16,0},{20,4},{24,8},{28,12},{1,17},{... | collective-permute-start | bytes 12296 | tf_op jit(solution)/shard_map/ppermute | solution.py:57
  251.8 1.0 collective-permute-done.23
  254.8 1.2 broadcast_add_fusion.2
  257.0 1.8 broadcast_add_fusion
  (72 shorter events, 11.2 us)
Async XLA Ops:
  0.6 15.7 %copy-start.18 = (f32[32,128]{1,0:T(8,128)S(1)}, f32[32,128]{1,0:T(8,128)}, u32[]{:S(2)}) copy-start(f32[32,128]{1,0:T(8,128)} %param.20) | copy-start | bytes 49156
  0.6 15.7 %copy-start.19 = (s32[32,128]{1,0:T(8,128)S(1)}, s32[32,128]{1,0:T(8,128)}, u32[]{:S(2)}) copy-start(s32[32,128]{1,0:T(8,128)} %param.19) | copy-start | bytes 49156
  0.7 15.7 %copy-start.20 = (f32[32,128]{1,0:T(8,128)S(1)}, f32[32,128]{1,0:T(8,128)}, u32[]{:S(2)}) copy-start(f32[32,128]{1,0:T(8,128)} %param.18) | copy-start | bytes 49156
  8.5 13.2 %collective-permute-start.3 = (f32[10,32,128]{2,1,0:T(8,128)}, f32[10,32,128]{2,1,0:T(8,128)S(1)}, u32[]{:S(2)}, u32[]{:S(2)}) collective-permute-start(f32[10,32,128]{2,1,0:T(8,128)} %get-tuple-element.25.ownl_ref), channel_id=1, source_target_pairs={{0,3},{1,0},{2,1},{3,2},{4,7},{5,4},{6,5},{7,6},{8,11},{9,8},{10,9... | collective-permute-start | bytes 491528 | tf_op jit(solution)/shard_map/ppermute | solution.py:46
  13.6 8.1 %collective-permute-start.2 = (f32[10,32,128]{2,1,0:T(8,128)}, f32[10,32,128]{2,1,0:T(8,128)S(1)}, u32[]{:S(2)}, u32[]{:S(2)}) collective-permute-start(f32[10,32,128]{2,1,0:T(8,128)} %get-tuple-element.26.ownr_ref), channel_id=1, source_target_pairs={{0,1},{1,2},{2,3},{3,0},{4,5},{5,6},{6,7},{7,4},{8,9},{9,10},{10,1... | collective-permute-start | bytes 491528 | tf_op jit(solution)/shard_map/ppermute | solution.py:46
  13.6 13.4 %collective-permute-start = (f32[80,16,128]{2,1,0:T(8,128)}, f32[80,16,128]{2,1,0:T(8,128)S(1)}, u32[]{:S(2)}, u32[]{:S(2)}) collective-permute-start(f32[80,16,128]{2,1,0:T(8,128)} %get-tuple-element.23), channel_id=1, source_target_pairs={{0,4},{4,8},{8,12},{12,16},{16,20},{20,24},{24,28},{1,5},{5,9},{9,... | collective-permute-start | bytes 1966088 | tf_op jit(solution)/shard_map/ppermute | solution.py:46
  15.1 11.9 %collective-permute-start.1 = (f32[80,16,128]{2,1,0:T(8,128)}, f32[80,16,128]{2,1,0:T(8,128)S(1)}, u32[]{:S(2)}, u32[]{:S(2)}) collective-permute-start(f32[80,16,128]{2,1,0:T(8,128)} %get-tuple-element.24), channel_id=1, source_target_pairs={{4,0},{8,4},{12,8},{16,12},{20,16},{24,20},{28,24},{5,1},{9,5},{13... | collective-permute-start | bytes 1966088 | tf_op jit(solution)/shard_map/ppermute | solution.py:46
  21.6 5.3 %copy-start.8 = (f32[10,32,128]{2,1,0:T(8,128)}, f32[10,32,128]{2,1,0:T(8,128)S(1)}, u32[]{:S(2)}) copy-start(f32[10,32,128]{2,1,0:T(8,128)S(1)} %collective-permute-done.2.hall_ref) | copy-start | bytes 491524
  21.7 5.3 %copy-start.7 = (f32[10,32,128]{2,1,0:T(8,128)}, f32[10,32,128]{2,1,0:T(8,128)S(1)}, u32[]{:S(2)}) copy-start(f32[10,32,128]{2,1,0:T(8,128)S(1)} %collective-permute-done.3.halr_ref) | copy-start | bytes 491524
  21.7 5.0 %collective-permute-start.5 = (f32[20,8,128]{2,1,0:T(8,128)S(1)}, f32[20,8,128]{2,1,0:T(8,128)S(1)}, u32[]{:S(2)}, u32[]{:S(2)}) collective-permute-start(f32[20,8,128]{2,1,0:T(8,128)S(1)} %get-tuple-element.43), channel_id=1, source_target_pairs={{4,0},{8,4},{12,8},{16,12},{20,16},{24,20},{28,24},{5,1},{9,5},{13... | collective-permute-start | bytes 245768 | tf_op jit(solution)/shard_map/ppermute | solution.py:46
  23.0 3.9 %collective-permute-start.4 = (f32[20,8,128]{2,1,0:T(8,128)S(1)}, f32[20,8,128]{2,1,0:T(8,128)S(1)}, u32[]{:S(2)}, u32[]{:S(2)}) collective-permute-start(f32[20,8,128]{2,1,0:T(8,128)S(1)} %get-tuple-element.44), channel_id=1, source_target_pairs={{0,4},{4,8},{8,12},{12,16},{16,20},{20,24},{24,28},{1,5},{5,9},{9,... | collective-permute-start | bytes 245768 | tf_op jit(solution)/shard_map/ppermute | solution.py:46
  26.7 0.6 copy-start.16
  27.0 0.6 copy-start.17
  27.0 0.9 copy-start.9
  27.8 0.8 copy-start.10
  66.9 12.9 %collective-permute-start.7 = (f32[80,32,128]{2,1,0:T(8,128)}, f32[80,32,128]{2,1,0:T(8,128)S(1)}, u32[]{:S(2)}, u32[]{:S(2)}) collective-permute-start(f32[80,32,128]{2,1,0:T(8,128)} %get-tuple-element.28.x_ref), channel_id=1, source_target_pairs={{4,0},{8,4},{12,8},{16,12},{20,16},{24,20},{28,24},{5,1},{9,5},{13... | collective-permute-start | bytes 3932168 | tf_op jit(solution)/shard_map/ppermute | solution.py:46
  68.2 13.7 %collective-permute-start.6 = (f32[80,32,128]{2,1,0:T(8,128)}, f32[80,32,128]{2,1,0:T(8,128)S(1)}, u32[]{:S(2)}, u32[]{:S(2)}) collective-permute-start(f32[80,32,128]{2,1,0:T(8,128)} %get-tuple-element.28.x_ref), channel_id=1, source_target_pairs={{0,4},{4,8},{8,12},{12,16},{16,20},{20,24},{24,28},{1,5},{5,9},{9,... | collective-permute-start | bytes 3932168 | tf_op jit(solution)/shard_map/ppermute | solution.py:46
  79.8 2.1 copy-start.4
  81.9 1.1 copy-start.6
  91.4 9.2 %collective-permute-start.8 = (f32[20,32,128]{2,1,0:T(8,128)}, f32[20,32,128]{2,1,0:T(8,128)S(1)}, u32[]{:S(2)}, u32[]{:S(2)}) collective-permute-start(f32[20,32,128]{2,1,0:T(8,128)} %get-tuple-element.30), channel_id=1, source_target_pairs={{0,1},{1,2},{2,3},{3,0},{4,5},{5,6},{6,7},{7,4},{8,9},{9,10},{10,1... | collective-permute-start | bytes 983048 | tf_op jit(solution)/shard_map/ppermute | solution.py:46
  91.4 10.8 %collective-permute-start.9 = (f32[20,32,128]{2,1,0:T(8,128)}, f32[20,32,128]{2,1,0:T(8,128)S(1)}, u32[]{:S(2)}, u32[]{:S(2)}) collective-permute-start(f32[20,32,128]{2,1,0:T(8,128)} %get-tuple-element.31), channel_id=1, source_target_pairs={{0,3},{1,0},{2,1},{3,2},{4,7},{5,4},{6,5},{7,6},{8,11},{9,8},{10,9... | collective-permute-start | bytes 983048 | tf_op jit(solution)/shard_map/ppermute | solution.py:46
  100.5 1.6 copy-start.13
  102.2 0.7 copy-start.14
  102.9 55.6 %copy-start.21 = (s32[2]{0:T(128)S(1)}, s32[2]{0:T(128)}, u32[]{:S(2)}) copy-start(s32[2]{0:T(128)} %param.21) | copy-start | bytes 28
  112.8 4.2 %collective-permute-start.10 = (f32[8,128]{1,0:T(8,128)}, f32[8,128]{1,0:T(8,128)S(1)}, u32[]{:S(2)}, u32[]{:S(2)}) collective-permute-start(f32[8,128]{1,0:T(8,128)} %get-tuple-element.35), channel_id=1, source_target_pairs={{0,1},{1,0},{2,3},{3,2},{4,5},{5,4},{6,7},{7,6},{8,9},{9,8},{10,11... | collective-permute-start | bytes 12296 | tf_op jit(solution)/shard_map/ppermute | solution.py:57
  117.6 6.2 %collective-permute-start.11 = (f32[8,128]{1,0:T(8,128)S(1)}, f32[8,128]{1,0:T(8,128)S(1)}, u32[]{:S(2)}, u32[]{:S(2)}) collective-permute-start(f32[8,128]{1,0:T(8,128)S(1)} %add.66), channel_id=1, source_target_pairs={{0,2},{1,3},{2,0},{3,1},{4,6},{5,7},{6,4},{7,5},{8,10},{9,11},{10,... | collective-permute-start | bytes 12296 | tf_op jit(solution)/shard_map/ppermute | solution.py:57
  123.8 20.2 %collective-permute-start.12 = (f32[8,128]{1,0:T(8,128)S(1)}, f32[8,128]{1,0:T(8,128)S(1)}, u32[]{:S(2)}, u32[]{:S(2)}) collective-permute-start(f32[8,128]{1,0:T(8,128)S(1)} %add.67), channel_id=1, source_target_pairs={{0,4},{4,0},{8,12},{12,8},{16,20},{20,16},{24,28},{28,24},{1,5},{5... | collective-permute-start | bytes 12296 | tf_op jit(solution)/shard_map/ppermute | solution.py:57
  144.0 10.4 %collective-permute-start.13 = (f32[8,128]{1,0:T(8,128)S(1)}, f32[8,128]{1,0:T(8,128)S(1)}, u32[]{:S(2)}, u32[]{:S(2)}) collective-permute-start(f32[8,128]{1,0:T(8,128)S(1)} %add.68), channel_id=1, source_target_pairs={{0,8},{4,12},{8,0},{12,4},{16,24},{20,28},{24,16},{28,20},{1,9},{5... | collective-permute-start | bytes 12296 | tf_op jit(solution)/shard_map/ppermute | solution.py:57
  154.5 5.6 %collective-permute-start.14 = (f32[8,128]{1,0:T(8,128)S(1)}, f32[8,128]{1,0:T(8,128)S(1)}, u32[]{:S(2)}, u32[]{:S(2)}) collective-permute-start(f32[8,128]{1,0:T(8,128)S(1)} %add.69), channel_id=1, source_target_pairs={{0,16},{4,20},{8,24},{12,28},{16,0},{20,4},{24,8},{28,12},{1,17},{... | collective-permute-start | bytes 12296 | tf_op jit(solution)/shard_map/ppermute | solution.py:57
  165.1 5.1 %collective-permute-start.16 = (f32[80,32,128]{2,1,0:T(8,128)}, f32[80,32,128]{2,1,0:T(8,128)S(1)}, u32[]{:S(2)}, u32[]{:S(2)}) collective-permute-start(f32[80,32,128]{2,1,0:T(8,128)} %second_contributions.1.x_ref), channel_id=1, source_target_pairs={{4,0},{8,4},{12,8},{16,12},{20,16},{24,20},{28,24},{5,1},{9,5},{13... | collective-permute-start | bytes 3932168 | tf_op jit(solution)/shard_map/ppermute | solution.py:46
  166.4 5.9 %collective-permute-start.15 = (f32[80,32,128]{2,1,0:T(8,128)}, f32[80,32,128]{2,1,0:T(8,128)S(1)}, u32[]{:S(2)}, u32[]{:S(2)}) collective-permute-start(f32[80,32,128]{2,1,0:T(8,128)} %second_contributions.1.x_ref), channel_id=1, source_target_pairs={{0,4},{4,8},{8,12},{12,16},{16,20},{20,24},{24,28},{1,5},{5,9},{9,... | collective-permute-start | bytes 3932168 | tf_op jit(solution)/shard_map/ppermute | solution.py:46
  170.2 2.1 copy-start.3
  172.3 1.1 copy-start.5
  181.8 9.2 %collective-permute-start.17 = (f32[20,32,128]{2,1,0:T(8,128)}, f32[20,32,128]{2,1,0:T(8,128)S(1)}, u32[]{:S(2)}, u32[]{:S(2)}) collective-permute-start(f32[20,32,128]{2,1,0:T(8,128)} %get-tuple-element.38), channel_id=1, source_target_pairs={{0,1},{1,2},{2,3},{3,0},{4,5},{5,6},{6,7},{7,4},{8,9},{9,10},{10,1... | collective-permute-start | bytes 983048 | tf_op jit(solution)/shard_map/ppermute | solution.py:46
  183.8 10.6 %collective-permute-start.18 = (f32[20,32,128]{2,1,0:T(8,128)}, f32[20,32,128]{2,1,0:T(8,128)S(1)}, u32[]{:S(2)}, u32[]{:S(2)}) collective-permute-start(f32[20,32,128]{2,1,0:T(8,128)} %get-tuple-element.39), channel_id=1, source_target_pairs={{0,3},{1,0},{2,1},{3,2},{4,7},{5,4},{6,5},{7,6},{8,11},{9,8},{10,9... | collective-permute-start | bytes 983048 | tf_op jit(solution)/shard_map/ppermute | solution.py:46
  190.9 3.4 %copy-start.11 = (f32[20,32,128]{2,1,0:T(8,128)}, f32[20,32,128]{2,1,0:T(8,128)S(1)}, u32[]{:S(2)}) copy-start(f32[20,32,128]{2,1,0:T(8,128)S(1)} %collective-permute-done.17.left_ref) | copy-start | bytes 983044
  194.4 0.7 copy-start.12
  195.1 58.9 %copy-start.15 = (f32[3,32,128]{2,1,0:T(8,128)S(1)}, f32[3,32,128]{2,1,0:T(8,128)}, u32[]{:S(2)}) copy-start(f32[3,32,128]{2,1,0:T(8,128)} %get-tuple-element.36.sums_ref) | copy-start | bytes 147460
  195.1 59.7 %copy-start.2 = (f32[80,32,128]{2,1,0:T(8,128)S(1)}, f32[80,32,128]{2,1,0:T(8,128)}, u32[]{:S(2)}) copy-start(f32[80,32,128]{2,1,0:T(8,128)} %get-tuple-element.27.h_ref) | copy-start | bytes 3932164
  205.1 6.0 %collective-permute-start.19 = (f32[8,128]{1,0:T(8,128)}, f32[8,128]{1,0:T(8,128)S(1)}, u32[]{:S(2)}, u32[]{:S(2)}) collective-permute-start(f32[8,128]{1,0:T(8,128)} %get-tuple-element.41), channel_id=1, source_target_pairs={{0,1},{1,0},{2,3},{3,2},{4,5},{5,4},{6,7},{7,6},{8,9},{9,8},{10,11... | collective-permute-start | bytes 12296 | tf_op jit(solution)/shard_map/ppermute | solution.py:57
  211.8 4.5 %collective-permute-start.20 = (f32[8,128]{1,0:T(8,128)S(1)}, f32[8,128]{1,0:T(8,128)S(1)}, u32[]{:S(2)}, u32[]{:S(2)}) collective-permute-start(f32[8,128]{1,0:T(8,128)S(1)} %add.72), channel_id=1, source_target_pairs={{0,2},{1,3},{2,0},{3,1},{4,6},{5,7},{6,4},{7,5},{8,10},{9,11},{10,... | collective-permute-start | bytes 12296 | tf_op jit(solution)/shard_map/ppermute | solution.py:57
  216.3 16.2 %collective-permute-start.21 = (f32[8,128]{1,0:T(8,128)S(1)}, f32[8,128]{1,0:T(8,128)S(1)}, u32[]{:S(2)}, u32[]{:S(2)}) collective-permute-start(f32[8,128]{1,0:T(8,128)S(1)} %add.73), channel_id=1, source_target_pairs={{0,4},{4,0},{8,12},{12,8},{16,20},{20,16},{24,28},{28,24},{1,5},{5... | collective-permute-start | bytes 12296 | tf_op jit(solution)/shard_map/ppermute | solution.py:57
  232.5 9.8 %collective-permute-start.22 = (f32[8,128]{1,0:T(8,128)S(1)}, f32[8,128]{1,0:T(8,128)S(1)}, u32[]{:S(2)}, u32[]{:S(2)}) collective-permute-start(f32[8,128]{1,0:T(8,128)S(1)} %add.74), channel_id=1, source_target_pairs={{0,8},{4,12},{8,0},{12,4},{16,24},{20,28},{24,16},{28,20},{1,9},{5... | collective-permute-start | bytes 12296 | tf_op jit(solution)/shard_map/ppermute | solution.py:57
  242.3 10.5 %collective-permute-start.23 = (f32[8,128]{1,0:T(8,128)S(1)}, f32[8,128]{1,0:T(8,128)S(1)}, u32[]{:S(2)}, u32[]{:S(2)}) collective-permute-start(f32[8,128]{1,0:T(8,128)S(1)} %add.75), channel_id=1, source_target_pairs={{0,16},{4,20},{8,24},{12,28},{16,0},{20,4},{24,8},{28,12},{1,17},{... | collective-permute-start | bytes 12296 | tf_op jit(solution)/shard_map/ppermute | solution.py:57
  254.8 1.8 copy-start
  254.8 2.2 copy-start.1

commit v2 on v1

v2 whole, which is shorter than its diff:
```python
import functools

import jax
import jax.numpy as jnp
import numpy as np
from jax import lax
from jax.experimental import pallas as pl
from jax.experimental.pallas import tpu as pltpu
from jax.sharding import PartitionSpec as P

STEPS = 3
ITERS = 2
LWIDTH = 32
LSCALE = 12

LANES = 128
SUB = 8
SLOT = 16
EAST, SIDE = 2 * STEPS, 2 * STEPS - 1
PACK = LANES // SLOT
FOLD = LANES // LWIDTH
SHARES = (0.6, 0.4)

VMEM = pl.BlockSpec(memory_space=pltpu.VMEM)
SMEM = pl.BlockSpec(memory_space=pltpu.SMEM)
GRANT = pltpu.CompilerParams(vmem_limit_bytes=16 << 20)


def f32(*shape):
    return jax.ShapeDtypeStruct(shape, jnp.float32)


def iota(shape, axis):
    return lax.broadcasted_iota(jnp.int32, shape, axis)


def spin(block, shift, axis):
    shift %= block.shape[axis]
    return block if shift == 0 else pltpu.roll(block, shift, axis)


def shifted(block, axis, step, periodic):
    count = lax.axis_size(axis)
    if periodic:
        pairs = [(i, (i + step) % count) for i in range(count)]
    else:
        pairs = [(i, i + step) for i in range(count) if 0 <= i + step < count]
    return lax.ppermute(block, axis, pairs)


def everywhere_sum(block):
    half = jnp.zeros_like(block)
    for axis in ("band", "member"):
        count = lax.axis_size(axis)
        if count & (count - 1):
            block, half = lax.psum(block + half, axis), jnp.zeros_like(block)
            continue
        reach = 1
        while reach < count:
            block = block + half
            half = lax.ppermute(block, axis, [(i, i ^ reach) for i in range(count)])
            reach *= 2
    return jnp.stack([block, half])


def taper(offset):
    scaled = offset.astype(np.float32) / np.float32(LSCALE)
    weight = np.exp(np.float32(-0.5) * scaled * scaled)
    return np.where(np.abs(offset) <= LWIDTH, weight, np.float32(0)).astype(np.float32)


def two_terms(table):
    high = table.astype(jnp.bfloat16)
    low = (table - high.astype(np.float32)).astype(jnp.bfloat16)
    return high, low


def row_table(rows):
    out = np.arange(rows)[:, None]
    table = taper(np.arange(rows + 2 * LWIDTH)[None, :] - LWIDTH - out)
    high, low = two_terms(table)
    return np.block([[high, high], [low, np.zeros_like(low)]])


def column_table(cols):
    out = np.arange(cols)
    high, low = two_terms(taper(out[:, None] - out[None, :]))
    return np.block([[high, low], [high, np.zeros_like(low)]])


def strip_table(cols):
    near = np.arange(LWIDTH)
    left = taper((near - LWIDTH)[:, None] - near[None, :])
    right = taper((cols + near)[:, None] - (cols - LWIDTH + near)[None, :])
    table = np.zeros((2 * LANES, 2 * LANES), np.float32)
    for k in range(FOLD):
        src, dst = k * LWIDTH, 2 * k * LWIDTH
        table[src : src + LWIDTH, dst + LWIDTH : dst + 2 * LWIDTH] = left
        table[LANES + src : LANES + src + LWIDTH, dst : dst + LWIDTH] = right
    return two_terms(table)


def split(block):
    high = block.astype(jnp.bfloat16)
    low = (block - high.astype(jnp.float32)).astype(jnp.bfloat16)
    return high, low


def mm(a, b):
    return jnp.dot(a, b, preferred_element_type=jnp.float32)


SEAM = SLOT // 2


def slot_pack(block, k):
    lane = iota(block.shape, 1) // SLOT
    return jnp.where(lane == k, spin(block, SLOT * k + SEAM, 1), 0.0)


def row_pack_kernel(u_ref, v_ref, h_ref, top_ref, bottom_ref):
    members, rows, _ = u_ref.shape
    sub = iota((SUB, LANES), 0)
    last = slice(rows - SUB, rows)

    def member(k, _):
        u = u_ref[k, :SUB]
        top_ref[k, :SUB] = jnp.where(sub < 6, v_ref[k, :SUB], spin(u, 6, 0))
        top_ref[k, SUB:] = jnp.where(sub < 5, h_ref[k, :SUB], spin(u, 3, 0))
        u = u_ref[k, last]
        bottom_ref[k, :SUB] = jnp.where(sub < 2, spin(u, 5, 0), v_ref[k, last])
        bottom_ref[k, SUB:] = jnp.where(sub < 3, spin(u, 3, 0), h_ref[k, last])
        return 0

    lax.fori_loop(0, members, member, 0, unroll=8)


def pack_rows(height, eastward, northward):
    members, rows, cols = height.shape
    return pl.pallas_call(
        row_pack_kernel,
        name="pack_rows",
        compiler_params=GRANT,
        in_specs=[VMEM] * 3,
        out_specs=[VMEM] * 2,
        out_shape=[f32(members, 2 * SUB, cols)] * 2,
    )(eastward, northward, height)


def column_pack_kernel(u_ref, v_ref, h_ref, left_ref, right_ref, *own_refs):
    members, rows, _ = u_ref.shape
    slot = iota((rows, LANES), 1) % SLOT

    def group(g, _):
        packs = []
        for ref, own in zip((u_ref, v_ref, h_ref), own_refs):
            pack = slot_pack(ref[g * PACK], 0)
            for k in range(1, PACK):
                pack = pack + slot_pack(ref[g * PACK + k], k)
            own[g] = pack
            packs.append(pack)

        def sent(starts):
            u, v, h = (spin(p, at - start, 1) for p, start, at in zip(packs, starts, PLACES))
            return jnp.where(slot < PLACES[1], u, jnp.where(slot < PLACES[2], v, h))

        left_ref[g] = sent((SEAM, SEAM, SEAM))
        right_ref[g] = sent((SEAM - EAST, SEAM - SIDE, SEAM - SIDE))
        return 0

    lax.fori_loop(0, members // PACK, group, 0)


PLACES = (0, EAST, EAST + SIDE)


def pack_columns(height, eastward, northward):
    members, rows, cols = height.shape
    groups = members // PACK
    return pl.pallas_call(
        column_pack_kernel,
        name="pack_columns",
        compiler_params=GRANT,
        in_specs=[VMEM] * 3,
        out_specs=[VMEM] * 5,
        out_shape=[f32(groups, rows, LANES)] * 5,
    )(eastward, northward, height)


def difference_table(cols):
    lane = np.arange(cols)
    inner = (lane[:, None] == lane[None, :] + 1).astype(np.float32)
    inner -= lane[:, None] == lane[None, :] - 1
    wall = np.zeros((LANES, cols), np.float32)
    wall[SEAM - 1 :: SLOT, 0] = -1
    wall[SEAM::SLOT, cols - 1] = 1
    return np.concatenate([inner, inner, wall, wall]).astype(jnp.bfloat16)


def slot_masks(tall):
    lane = np.arange(LANES) // SLOT
    masks = lane[None, None, :] == np.arange(PACK)[:, None, None]
    return np.broadcast_to(masks, (PACK, tall, LANES)).astype(jnp.bfloat16)


def forecast_kernel(
    h_ref, u_ref, v_ref, above_ref, below_ref, ownu_ref, ownv_ref, ownh_ref, hall_ref, halr_ref,
    cornu_ref, cornd_ref, table_ref, mask_ref, edge_ref,
    ho_ref, uo_ref, vo_ref, mean_ref,
    us_ref, vs_ref, hs_ref, lhs_ref, sum_ref,
):
    members, rows, cols = h_ref.shape
    groups = members // PACK
    tall = rows + 2 * SUB
    batch = PACK + 2
    half = batch // 2
    slot = iota((tall, LANES), 1) % SLOT
    row = iota((tall, LANES), 0)
    sub = iota((SUB, LANES), 0)
    outside = ((row < SUB) & (edge_ref[0] == 1)) | ((row >= rows + SUB) & (edge_ref[1] == 1))
    pull = jnp.where(outside, 0.0, 0.2)
    mid, low, high = slice(SUB, SUB + tall), slice(SUB - 1, SUB + tall - 1), slice(SUB + 1, SUB + tall + 1)
    core = slice(2 * SUB, 2 * SUB + rows)

    def differences(ref):
        wall = jnp.where(slot == SEAM - 1, ref[PACK, mid], ref[PACK + 1, mid])
        walls = split(wall)
        for j in range(batch):
            for i, part in enumerate(split(ref[j, mid])):
                lhs_ref[j, :, i * LANES : (i + 1) * LANES] = part
            if j < PACK:
                for i, part in enumerate(walls):
                    lhs_ref[j, :, (i + 2) * LANES : (i + 3) * LANES] = part * mask_ref[j]
        out = []
        for start in (0, half):
            stack = lhs_ref[start : start + half].reshape(half * tall, 4 * LANES)
            d = mm(stack, table_ref[...])
            out += [d[j * tall : (j + 1) * tall] for j in range(half)]
        return out

    def group(g, _):
        packs = [[None] * 2 for _ in range(3)]
        for k in range(PACK):
            m = g * PACK + k
            a0, a1 = above_ref[m, :SUB], above_ref[m, SUB:]
            b0, b1 = below_ref[m, :SUB], below_ref[m, SUB:]
            ua = jnp.where(sub < 5, spin(a0, 3, 0), spin(a1, 5, 0))
            ub = jnp.where(sub < 2, spin(b0, 2, 0), spin(b1, 5, 0))
            ends = ((us_ref, ua, ub, u_ref), (vs_ref, a0, b0, v_ref), (hs_ref, a1, b1, h_ref))
            for i, (state, a, b, ref) in enumerate(ends):
                state[k, SUB : 2 * SUB] = a
                state[k, core] = ref[m]
                state[k, 2 * SUB + rows : 3 * SUB + rows] = b
                for end, edge in enumerate((a, b)):
                    piece = slot_pack(edge, k)
                    packs[i][end] = piece if k == 0 else packs[i][end] + piece
        left = jnp.concatenate([cornu_ref[g], hall_ref[g], cornd_ref[g]], axis=0)
        right = jnp.concatenate([cornu_ref[groups + g], halr_ref[g], cornd_ref[groups + g]], axis=0)
        owns = ((us_ref, ownu_ref, EAST), (vs_ref, ownv_ref, SIDE), (hs_ref, ownh_ref, SIDE))
        for i, (state, own_ref, size) in enumerate(owns):
            own = jnp.concatenate([packs[i][0], own_ref[g], packs[i][1]], axis=0)
            state[PACK, mid] = jnp.where(slot < SEAM, spin(left, SEAM - size - PLACES[i], 1), own)
            state[PACK + 1, mid] = jnp.where(slot < SEAM, own, spin(right, SEAM - PLACES[i], 1))

        for step in range(STEPS):
            last = step == STEPS - 1
            for j, d in enumerate(differences(us_ref)):
                hs_ref[j, mid] = hs_ref[j, mid] - pull * (d + (vs_ref[j, high] - vs_ref[j, low]))
            for j, d in enumerate(differences(hs_ref)):
                if last and j >= PACK:
                    continue
                u, v = us_ref[j, mid], vs_ref[j, mid]
                us_ref[j, mid] = u + 0.1 * v - pull * d
                vs_ref[j, mid] = v - 0.1 * u - pull * (hs_ref[j, high] - hs_ref[j, low])

        for i, (state, out) in enumerate(((hs_ref, ho_ref), (us_ref, uo_ref), (vs_ref, vo_ref))):
            total = sum_ref[i]
            for k in range(PACK):
                x = state[k, core]
                out[g * PACK + k] = x
                total = total + x
            sum_ref[i] = total
        return 0

    sum_ref[...] = jnp.zeros_like(sum_ref)
    lhs_ref[...] = jnp.zeros_like(lhs_ref)
    for state in (us_ref, vs_ref, hs_ref):
        for j in range(batch):
            state[j, :SUB] = jnp.zeros((SUB, LANES), jnp.float32)
            state[j, SUB + tall :] = jnp.zeros((SUB, LANES), jnp.float32)
    lax.fori_loop(0, groups, group, 0)
    for i in range(3):
        mean_ref[i] = sum_ref[i] / members


def forecast(h, u, v, *rest):
    members, rows, cols = h.shape
    tall = rows + 2 * SUB
    state = pltpu.VMEM((PACK + 2, tall + 2 * SUB, LANES), jnp.float32)
    *halos, edge = rest
    return pl.pallas_call(
        forecast_kernel,
        name="forecast",
        compiler_params=GRANT,
        in_specs=[VMEM] * (len(halos) + 5) + [SMEM],
        out_specs=[VMEM] * 4,
        out_shape=[f32(members, rows, cols)] * 3 + [f32(3, rows, cols)],
        scratch_shapes=[
            state,
            state,
            state,
            pltpu.VMEM((PACK + 2, tall, 4 * LANES), jnp.bfloat16),
            pltpu.VMEM((3, rows, cols), jnp.float32),
        ],
    )(h, u, v, *halos, difference_table(cols), slot_masks(tall), edge)


def factor(square_ref, step_ref, cells):
    total = jnp.sum(square_ref[0] + square_ref[1], keepdims=True)
    return step_ref[0] / jnp.sqrt(total / cells + 1e-06)


def contrib_kernel(begin, cells, h_ref, u_ref, v_ref, mean_ref, obs_ref, *refs):
    if len(refs) == 1:
        (contrib_ref,) = refs
        states = means = [mean_ref[i] for i in range(3)]
    else:
        sums_ref, square_ref, step_ref, contrib_ref = refs
        means = [mean_ref[i] for i in range(3)]
        f = factor(square_ref, step_ref, cells)
        states = [means[i] + f * sums_ref[i] for i in range(3)]
    members = h_ref.shape[0]
    scale = 1.0 / float(np.sqrt(np.float32(members - 1)))
    sh, su, sv = states
    residual = obs_ref[1] * (obs_ref[0] - sh - 0.15 * (su * su + sv * sv))
    residual = residual * scale
    eu, ev = 0.3 * su, 0.3 * sv
    mh, mu, mv = means

    def member(m, _):
        h, u, v = (ref[begin + m] for ref in (h_ref, u_ref, v_ref))
        contrib_ref[m] = ((h - mh) + (eu * (u - mu) + ev * (v - mv))) * residual
        return 0

    lax.fori_loop(0, contrib_ref.shape[0], member, 0, unroll=4)


def contributions(part, cells, fields, means, obs, *more):
    begin, count = part
    return pl.pallas_call(
        functools.partial(contrib_kernel, begin, cells),
        name="contributions",
        compiler_params=GRANT,
        in_specs=[VMEM] * 5 + ([VMEM, VMEM, SMEM] if more else []),
        out_specs=VMEM,
        out_shape=f32(count, *fields[0].shape[1:]),
    )(*fields, means, obs, *more)


def rows_kernel(x_ref, above_ref, below_ref, table_ref, out_ref, left_ref, right_ref):
    members, rows, cols = x_ref.shape
    lane = iota((rows, LANES), 1)
    table = table_ref[...]

    def fold(g, _):
        left = right = None
        for pair in range(FOLD // 2):
            halves = []
            for k in (2 * pair, 2 * pair + 1):
                m = g * FOLD + k
                high, low = split(jnp.concatenate([above_ref[m], x_ref[m], below_ref[m]], axis=0))
                halves.append(jnp.concatenate([high, low], axis=0))
            both = mm(table, jnp.concatenate(halves, axis=1))
            both = both[:rows] + both[rows:]
            for k in (2 * pair, 2 * pair + 1):
                y = both[:, (k % 2) * cols : (k % 2 + 1) * cols]
                out_ref[g * FOLD + k] = y
                here = lane // LWIDTH == k
                l = jnp.where(here, spin(y, LWIDTH * k, 1), 0.0)
                r = jnp.where(here, spin(y, LWIDTH * k + LWIDTH - cols, 1), 0.0)
                left, right = (l, r) if k == 0 else (left + l, right + r)
        left_ref[g] = left
        right_ref[g] = right
        return 0

    lax.fori_loop(0, members // FOLD, fold, 0, unroll=2)


def taper_rows(x, above, below):
    members, rows, cols = x.shape
    folds = members // FOLD
    return pl.pallas_call(
        rows_kernel,
        name="taper_rows",
        compiler_params=GRANT,
        in_specs=[VMEM] * 4,
        out_specs=[VMEM] * 3,
        out_shape=[f32(members, rows, cols)] + [f32(folds, rows, LANES)] * 2,
    )(x, above, below, row_table(rows))


def columns_kernel(begin, cells, kinds, *refs):
    names = dict(zip(kinds, refs))
    x_ref, left_ref, right_ref = (names[n] for n in ("x", "left", "right"))
    mean_ref, sums_ref, square_ref = (names[n] for n in ("means", "sums", "square"))
    grad_ref = names["grad"]
    fields = [names[n] for n in "huv"]
    count, rows, cols = x_ref.shape
    scale = 1.0 / float(np.sqrt(np.float32(fields[0].shape[0] - 1)))
    lane = iota((rows, LANES), 1)
    rim = (lane < LWIDTH) | (lane >= cols - LWIDTH)

    def fold(g, _):
        xh, xl = split(jnp.concatenate([left_ref[g], right_ref[g]], axis=1))
        high_table = names["high"][...]
        strips = mm(xh, high_table) + (mm(xl, high_table) + mm(xh, names["low"][...]))
        block = jnp.concatenate([x_ref[g * FOLD + k] for k in range(FOLD)], axis=0)
        bh, bl = split(block)
        both = mm(jnp.concatenate([bh, bl], axis=1), names["table"][...])
        both = both[:, :cols] + both[:, cols:]
        for k in range(FOLD):
            at = 2 * k * LWIDTH
            part = strips[:, at // LANES * LANES : at // LANES * LANES + LANES]
            part = spin(part, -(at % LANES + LWIDTH), 1)
            y = both[k * rows : (k + 1) * rows] + jnp.where(rim, part, 0.0)
            grad_ref[g * FOLD + k] = y
        return 0

    lax.fori_loop(0, count // FOLD, fold, 0, unroll=2)
    zero = jnp.zeros((SUB, cols), jnp.float32)
    square = names["square0"][...] if "square0" in names else zero
    if "prev" in names:
        f = factor(names["squares"], names["step"], cells)
    for start in range(0, rows, SUB):
        part = slice(start, start + SUB)
        means = [mean_ref[i, part] for i in range(3)]

        def member(m, carry):
            square, *sums = carry
            y = grad_ref[m, part]
            if "prev" in names:
                y = f * names["prev"][m, part] - y
            square = square + y * y
            terms = ((ref[begin + m, part] - mean) * y for ref, mean in zip(fields, means))
            return (square, *(s + t for s, t in zip(sums, terms)))

        square, *sums = lax.fori_loop(0, count, member, (square, zero, zero, zero), unroll=4)
        for i in range(3):
            total = sums[i] * scale
            if "sums0" in names:
                total = total + names["sums0"][i, part]
            sums_ref[i, part] = total
    square_ref[...] = square


def taper_columns(part, cells, x, left, right, fields, means, carried, before):
    count, rows, cols = x.shape
    high, low = strip_table(cols)
    ins = dict(x=x, left=left, right=right, means=means, table=column_table(cols), high=high, low=low)
    ins.update(zip("huv", fields))
    if carried:
        ins.update(sums0=carried[0], square0=carried[1])
    if before:
        ins.update(prev=before[0], squares=before[1], step=before[2])
    grad = f32(count, rows, cols)
    outs = dict(sums=f32(3, rows, cols), square=f32(SUB, LANES))
    if not before:
        outs["grad"] = grad
    kinds = (*ins, *outs, *(() if "grad" in outs else ("grad",)))
    result = pl.pallas_call(
        functools.partial(columns_kernel, part[0], cells, kinds),
        name="taper_columns",
        compiler_params=GRANT,
        in_specs=[SMEM if n == "step" else VMEM for n in ins],
        out_specs=[VMEM] * len(outs),
        out_shape=list(outs.values()),
        scratch_shapes=[] if "grad" in outs else [pltpu.VMEM(grad.shape, jnp.float32)],
    )(*ins.values())
    return result[:2], result[2:]


def analysis_kernel(cells, h_ref, u_ref, v_ref, *refs):
    s0_ref, s1_ref, q0_ref, q1_ref, step0_ref, step1_ref, *outs, increment_ref = refs

    @pl.when(pl.program_id(0) == 0)
    def _():
        f0, f1 = factor(q0_ref, step0_ref, cells), factor(q1_ref, step1_ref, cells)
        increment_ref[...] = f0 * s0_ref[...] - f1 * s1_ref[...]

    begin = pl.program_id(0) * outs[0].shape[0]
    for i, (ref, out) in enumerate(zip((h_ref, u_ref, v_ref), outs)):
        for k in range(outs[0].shape[0]):
            out[k] = ref[begin + k] + increment_ref[i]


def analysis(cells, fields, *rest):
    members, rows, cols = fields[0].shape
    block = pl.BlockSpec((2 * PACK, rows, cols), lambda g: (g, 0, 0))
    return pl.pallas_call(
        functools.partial(analysis_kernel, cells),
        name="analysis",
        compiler_params=GRANT,
        grid=(members // (2 * PACK),),
        in_specs=[VMEM] * 7 + [SMEM] * 2,
        out_specs=[block] * 3,
        out_shape=[f32(members, rows, cols)] * 3,
        scratch_shapes=[pltpu.VMEM((3, rows, cols), jnp.float32)],
    )(*fields, *rest)


def parts_of(members):
    sizes, left = [], members // FOLD
    for share in SHARES[:-1]:
        sizes.append(int(round(share * members / FOLD)))
        left -= sizes[-1]
    sizes.append(left)
    begins = np.cumsum([0] + sizes[:-1])
    return [(int(b) * FOLD, n * FOLD) for b, n in zip(begins, sizes) if n]


def per_device(
    height_start, east_start, north_start, obs_value, obs_mask, obs_precision, step_sizes
):
    members, rows, cols = height_start.shape
    starts = (height_start, east_start, north_start)
    top, bottom = pack_rows(*starts)
    above = shifted(bottom, "member", 1, False)
    below = shifted(top, "member", -1, False)
    starts, bottom = lax.optimization_barrier((starts, bottom))
    first, last, *own = pack_columns(*starts)
    hall = shifted(last, "band", 1, True)
    halr = shifted(first, "band", -1, True)
    ends = jnp.concatenate([hall, halr], axis=0)
    cornu = shifted(ends[:, rows - SUB :], "member", 1, False)
    cornd = shifted(ends[:, :SUB], "member", -1, False)

    obs = jnp.stack([obs_value, obs_mask.astype(jnp.float32) * obs_precision])
    here = lax.axis_index("member")
    edge = jnp.stack([here == 0, here == lax.axis_size("member") - 1]).astype(jnp.int32)
    *fields, means = forecast(*starts, above, below, *own, hall, halr, cornu, cornd, edge)
    cells = float(members * rows * cols * lax.axis_size("member") * lax.axis_size("band"))
    parts = parts_of(members)
    steps = [(step_sizes[k : k + 1].astype(jnp.float32) / 64.0) for k in range(ITERS)]

    def localized(contribs, before):
        sent = [
            (shifted(c, "member", 1, False), shifted(c, "member", -1, False)) for c in contribs
        ]
        tapered = []
        for c, (above, below) in zip(contribs, sent):
            x, first, last = taper_rows(c, above, below)
            tapered.append((x, shifted(last, "band", 1, True), shifted(first, "band", -1, True)))
        carried, grads = (), []
        for i, (part, arrays) in enumerate(zip(parts, tapered)):
            more = (before[0][i], *before[1:]) if before else ()
            carried, grad = taper_columns(part, cells, *arrays, fields, means, carried, more)
            grads += grad
        return carried[0], everywhere_sum(carried[1]), grads

    first = [contributions(part, cells, fields, means, obs) for part in parts]
    sums0, squares0, grads = localized(first, ())
    second = [
        contributions(part, cells, fields, means, obs, sums0, squares0, steps[0]) for part in parts
    ]
    sums1, squares1, _ = localized(second, (grads, squares0, steps[0]))
    return tuple(analysis(cells, fields, sums0, sums1, squares0, squares1, *steps))


def solution(mesh):
    tile, flat = P(None, "member", "band"), P("member", "band")
    return jax.shard_map(
        per_device,
        mesh=mesh,
        in_specs=(tile, tile, tile, flat, flat, flat, P()),
        out_specs=(tile, tile, tile),
        check_vma=False,
    )
```

time: 259 us -> 184 us (0.71)
  Pallas kernels: 86.4 us -> 44.6 us
  waiting for transfers between devices: 48.1 us -> 32.6 us
  starting transfers between devices: 106 us -> 95.6 us
  other arithmetic: 7.65 us -> 0.12 us
    pallas_call x7 -> x16, Pallas kernels: 86.4 us -> 44.6 us  [the longest x1 20.3 us: forecast(): pl.pallas_call(forecast_kernel, name='forecast', compiler_params=GRANT, i...]
    ppermute x10, starting transfers between devices: 69.8 us -> 48.2 us  [everywhere_sum(): half = lax.ppermute(block, axis, [(i, i ^ reach) for i in range(count)])]
    ppermute x14 -> x22, waiting for transfers between devices: 26.2 us -> 9.61 us  [shifted(): return lax.ppermute(block, axis, pairs)]
    ppermute x14 -> x22, starting transfers between devices: 36.4 us -> 47.5 us  [shifted(): return lax.ppermute(block, axis, pairs)]
    add x10 -> x8, other arithmetic: 4.34 us -> 0.03 us  [everywhere_sum(): block = block + half]
    unnamed x45 -> x33, local copies, waits for them, and re-layouts: 6.37 us -> 7.11 us
  transfers between devices with their start and end apart: 24 -> 32, of which waited for: 20 -> 13; matrix products, arithmetic and copies ran while one was open for 1% -> 0% of each run, Pallas kernels for 0% -> 8%
where the time goes in v2:
time: 184 us; the launch traced here: 183 us
  starting transfers between devices  95.6 us (52%)
  Pallas kernels  44.6 us (24%)
  waiting for transfers between devices  32.6 us (18%)
  local copies, waits for them, and re-layouts  7.72 us (4%)
  between operations  2.39 us (1%)
    ppermute x10, starting transfers between devices, everywhere_sum(): half = lax.ppermute(block, axis, [(i, i ^ reach) for i in range(count)])  48.2 us
    ppermute x22, starting transfers between devices, shifted(): return lax.ppermute(block, axis, pairs)  47.5 us
    ppermute x10, waiting for transfers between devices, everywhere_sum(): half = lax.ppermute(block, axis, [(i, i ^ reach) for i in range(count)])  23 us
    pallas_call x1, Pallas kernels, forecast(): pl.pallas_call(forecast_kernel, name='forecast', compiler_params=GRANT, i...  20.3 us
    pallas_call x4, Pallas kernels, taper_columns(): pl.pallas_call(functools.partial(columns_kernel, part[0], cells, kinds),...  9.96 us
    ppermute x22, waiting for transfers between devices, shifted(): return lax.ppermute(block, axis, pairs)  9.61 us
    unnamed x33, local copies, waits for them, and re-layouts  7.11 us
    pallas_call x4, Pallas kernels, taper_rows(): pl.pallas_call(rows_kernel, name='taper_rows', compiler_params=GRANT, in_...  5.73 us
  transfers between devices with their start and end apart: 32, of which 13 were waited for; matrix products, arithmetic and copies ran while one was open for 0% of the time, Pallas kernels for 8%

profile of v2, /device:TPU:0, one launch (start us, length us, event | category | flops | bytes accessed | tf_op | source)
XLA Modules:
  0.0 183.1 jit_solution(7722216296186522744)
XLA Ops:
  0.6 1.3 copy-done
  2.0 1.3 copy-done.2
  3.3 1.3 copy-done.4
  5.8 3.4 %collective-permute-start = (f32[80,16,128]{2,1,0:T(8,128)}, f32[80,16,128]{2,1,0:T(8,128)}, u32[]{:S(2)}, u32[]{:S(2)}) collective-permute-start(f32[80,16,128]{2,1,0:T(8,128)} %get-tuple-element.39), channel_id=1, source_target_pairs={{0,4},{4,8},{8,12},{12,16},{16,20},{20,24},{24,28},{1,5},{5,9},{9,... | collective-permute-start | bytes 1966088 | tf_op jit(solution)/shard_map/ppermute | solution.py:48
  9.2 3.3 %pack_columns.1 = (f32[10,32,128]{2,1,0:T(8,128)}, f32[10,32,128]{2,1,0:T(8,128)}, f32[10,32,128]{2,1,0:T(8,128)S(1)}, f32[10,32,128]{2,1,0:T(8,128)S(1)}, f32[10,32,128]{2,1,0:T(8,128)S(1)}) custom-call(f32[80,32,128]{2,1,0:T(8,128)S(1)} %copy-done.2, f32[80,32,128]{2,1,0:T(8,128)S(1)} %copy-done.4, f32[80,32,128]{2,1,0:T(8,128)S(1)} %copy-done), custom_call_target="tpu_custom_call" | custom-call | tf_op jit(solution)/shard_map/pack_columns/pallas_call | solution.py:180
  12.4 2.4 %collective-permute-start.2 = (f32[10,32,128]{2,1,0:T(8,128)}, f32[10,32,128]{2,1,0:T(8,128)S(1)}, u32[]{:S(2)}, u32[]{:S(2)}) collective-permute-start(f32[10,32,128]{2,1,0:T(8,128)} %get-tuple-element.47), channel_id=1, source_target_pairs={{0,1},{1,2},{2,3},{3,0},{4,5},{5,6},{6,7},{7,4},{8,9},{9,10},{10,1... | collective-permute-start | bytes 491528 | tf_op jit(solution)/shard_map/ppermute | solution.py:48
  14.8 2.0 %collective-permute-start.3 = (f32[10,32,128]{2,1,0:T(8,128)}, f32[10,32,128]{2,1,0:T(8,128)S(1)}, u32[]{:S(2)}, u32[]{:S(2)}) collective-permute-start(f32[10,32,128]{2,1,0:T(8,128)} %get-tuple-element.48), channel_id=1, source_target_pairs={{0,3},{1,0},{2,1},{3,2},{4,7},{5,4},{6,5},{7,6},{8,11},{9,8},{10,9... | collective-permute-start | bytes 491528 | tf_op jit(solution)/shard_map/ppermute | solution.py:48
  16.9 1.3 collective-permute-start.1
  18.2 3.7 %collective-permute-done.2.hall_ref = f32[10,32,128]{2,1,0:T(8,128)S(1)} collective-permute-done((f32[10,32,128]{2,1,0:T(8,128)}, f32[10,32,128]{2,1,0:T(8,128)S(1)}, u32[]{:S(2)}, u32[]{:S(2)}) %collective-permute-start.2) | collective-permute-done | bytes 163872 | tf_op jit(solution)/shard_map/ppermute | solution.py:48
  22.0 3.3 %collective-permute-done.3.halr_ref = f32[10,32,128]{2,1,0:T(8,128)S(1)} collective-permute-done((f32[10,32,128]{2,1,0:T(8,128)}, f32[10,32,128]{2,1,0:T(8,128)S(1)}, u32[]{:S(2)}, u32[]{:S(2)}) %collective-permute-start.3) | collective-permute-done | bytes 163872 | tf_op jit(solution)/shard_map/ppermute | solution.py:48
  25.4 1.7 collective-permute-start.4
  27.1 1.3 collective-permute-start.5
  28.5 2.4 %collective-permute-done.5.cornd_ref = f32[20,8,128]{2,1,0:T(8,128)S(1)} collective-permute-done((f32[20,8,128]{2,1,0:T(8,128)S(1)}, f32[20,8,128]{2,1,0:T(8,128)S(1)}, u32[]{:S(2)}, u32[]{:S(2)}) %collective-permute-start.5) | collective-permute-done | bytes 81952 | tf_op jit(solution)/shard_map/ppermute | solution.py:48
  30.9 1.3 copy-done.5
  34.0 20.3 %forecast.1 = (f32[80,32,128]{2,1,0:T(8,128)S(1)}, f32[80,32,128]{2,1,0:T(8,128)S(1)}, f32[80,32,128]{2,1,0:T(8,128)S(1)}, f32[3,32,128]{2,1,0:T(8,128)S(1)}) custom-call(f32[80,32,128]{2,1,0:T(8,128)S(1)} %copy-done.1, f32[80,32,128]{2,1,0:T(8,128)S(1)} %copy-done.3, f32[80,32,128]{2,1,0:T(8,128)S(1)} %copy-done.5, ...), custom_call_target="tpu_custom_call" | custom-call | tf_op jit(solution)/shard_map/forecast/pallas_call | solution.py:301
  54.7 5.0 %collective-permute-start.10 = (f32[48,32,128]{2,1,0:T(8,128)S(1)}, f32[48,32,128]{2,1,0:T(8,128)S(1)}, u32[]{:S(2)}, u32[]{:S(2)}) collective-permute-start(f32[48,32,128]{2,1,0:T(8,128)S(1)} %contributions.5.x_ref), channel_id=1, source_target_pairs={{0,4},{4,8},{8,12},{12,16},{16,20},{20,24},{24,28},{1,5},{5,9},{9,... | collective-permute-start | bytes 2359304 | tf_op jit(solution)/shard_map/ppermute | solution.py:48
  59.7 1.3 collective-permute-start.11
  61.2 3.1 %collective-permute-start.6 = (f32[32,32,128]{2,1,0:T(8,128)S(1)}, f32[32,32,128]{2,1,0:T(8,128)S(1)}, u32[]{:S(2)}, u32[]{:S(2)}) collective-permute-start(f32[32,32,128]{2,1,0:T(8,128)S(1)} %contributions.4.x_ref), channel_id=1, source_target_pairs={{0,4},{4,8},{8,12},{12,16},{16,20},{20,24},{24,28},{1,5},{5,9},{9,... | collective-permute-start | bytes 1572872 | tf_op jit(solution)/shard_map/ppermute | solution.py:48
  64.3 1.3 collective-permute-start.7
  65.6 1.7 taper_rows.5
  68.5 2.8 %collective-permute-start.13 = (f32[12,32,128]{2,1,0:T(8,128)S(1)}, f32[12,32,128]{2,1,0:T(8,128)S(1)}, u32[]{:S(2)}, u32[]{:S(2)}) collective-permute-start(f32[12,32,128]{2,1,0:T(8,128)S(1)} %get-tuple-element.58), channel_id=1, source_target_pairs={{0,3},{1,0},{2,1},{3,2},{4,7},{5,4},{6,5},{7,6},{8,11},{9,8},{10,9... | collective-permute-start | bytes 589832 | tf_op jit(solution)/shard_map/ppermute | solution.py:48
  72.5 3.8 %collective-permute-start.9 = (f32[8,32,128]{2,1,0:T(8,128)S(1)}, f32[8,32,128]{2,1,0:T(8,128)S(1)}, u32[]{:S(2)}, u32[]{:S(2)}) collective-permute-start(f32[8,32,128]{2,1,0:T(8,128)S(1)} %get-tuple-element.55), channel_id=1, source_target_pairs={{0,3},{1,0},{2,1},{3,2},{4,7},{5,4},{6,5},{7,6},{8,11},{9,8},{10,9... | collective-permute-start | bytes 393224 | tf_op jit(solution)/shard_map/ppermute | solution.py:48
  76.3 2.9 %taper_columns.4 = (f32[3,32,128]{2,1,0:T(8,128)S(1)}, f32[8,128]{1,0:T(8,128)S(1)}, f32[48,32,128]{2,1,0:T(8,128)S(1)}) custom-call(f32[48,32,128]{2,1,0:T(8,128)S(1)} %get-tuple-element.56.refs_0_, f32[12,32,128]{2,1,0:T(8,128)S(1)} %collective-permute-done.12.refs_1_, f32[12,32,128]{2,1,0:T(8,128)S(1)} %collective-permute-done.13.refs_2_, ...), custom_call_target="tpu_custom_call" | custom-call | tf_op jit(solution)/shard_map/taper_columns/pallas_call | solution.py:470
  79.2 1.9 %taper_columns.5 = (f32[3,32,128]{2,1,0:T(8,128)S(1)}, f32[8,128]{1,0:T(8,128)S(1)}, f32[32,32,128]{2,1,0:T(8,128)S(1)}) custom-call(f32[32,32,128]{2,1,0:T(8,128)S(1)} %get-tuple-element.53.refs_0_, f32[8,32,128]{2,1,0:T(8,128)S(1)} %collective-permute-done.8.refs_1_, f32[8,32,128]{2,1,0:T(8,128)S(1)} %collective-permute-done.9.refs_2_, ...), custom_call_target="tpu_custom_call" | custom-call | tf_op jit(solution)/shard_map/taper_columns/pallas_call | solution.py:470
  81.2 3.6 %collective-permute-done.14 = f32[8,128]{1,0:T(8,128)S(1)} collective-permute-done((f32[8,128]{1,0:T(8,128)S(1)}, f32[8,128]{1,0:T(8,128)S(1)}, u32[]{:S(2)}, u32[]{:S(2)}) %collective-permute-start.14) | collective-permute-done | bytes 4128 | tf_op jit(solution)/shard_map/ppermute | solution.py:61
  84.8 2.4 %collective-permute-start.15 = (f32[8,128]{1,0:T(8,128)S(1)}, f32[8,128]{1,0:T(8,128)S(1)}, u32[]{:S(2)}, u32[]{:S(2)}) collective-permute-start(f32[8,128]{1,0:T(8,128)S(1)} %add.24), channel_id=1, source_target_pairs={{0,2},{1,3},{2,0},{3,1},{4,6},{5,7},{6,4},{7,5},{8,10},{9,11},{10,... | collective-permute-start | bytes 12296 | tf_op jit(solution)/shard_map/ppermute | solution.py:61
  87.2 3.5 %collective-permute-done.15 = f32[8,128]{1,0:T(8,128)S(1)} collective-permute-done((f32[8,128]{1,0:T(8,128)S(1)}, f32[8,128]{1,0:T(8,128)S(1)}, u32[]{:S(2)}, u32[]{:S(2)}) %collective-permute-start.15) | collective-permute-done | bytes 4128 | tf_op jit(solution)/shard_map/ppermute | solution.py:61
  90.7 15.3 %collective-permute-start.16 = (f32[8,128]{1,0:T(8,128)S(1)}, f32[8,128]{1,0:T(8,128)S(1)}, u32[]{:S(2)}, u32[]{:S(2)}) collective-permute-start(f32[8,128]{1,0:T(8,128)S(1)} %add.25), channel_id=1, source_target_pairs={{0,4},{4,0},{8,12},{12,8},{16,20},{20,16},{24,28},{28,24},{1,5},{5... | collective-permute-start | bytes 12296 | tf_op jit(solution)/shard_map/ppermute | solution.py:61
  106.9 6.4 %collective-permute-start.17 = (f32[8,128]{1,0:T(8,128)S(1)}, f32[8,128]{1,0:T(8,128)S(1)}, u32[]{:S(2)}, u32[]{:S(2)}) collective-permute-start(f32[8,128]{1,0:T(8,128)S(1)} %add.26), channel_id=1, source_target_pairs={{0,8},{4,12},{8,0},{12,4},{16,24},{20,28},{24,16},{28,20},{1,9},{5... | collective-permute-start | bytes 12296 | tf_op jit(solution)/shard_map/ppermute | solution.py:61
  113.3 1.6 collective-permute-done.17
  116.1 2.4 %collective-permute-done.18 = f32[8,128]{1,0:T(8,128)S(1)} collective-permute-done((f32[8,128]{1,0:T(8,128)S(1)}, f32[8,128]{1,0:T(8,128)S(1)}, u32[]{:S(2)}, u32[]{:S(2)}) %collective-permute-start.18) | collective-permute-done | bytes 4128 | tf_op jit(solution)/shard_map/ppermute | solution.py:61
  118.9 1.3 collective-permute-start.23
  120.2 1.3 collective-permute-start.24
  121.9 5.3 %collective-permute-start.19 = (f32[32,32,128]{2,1,0:T(8,128)S(1)}, f32[32,32,128]{2,1,0:T(8,128)S(1)}, u32[]{:S(2)}, u32[]{:S(2)}) collective-permute-start(f32[32,32,128]{2,1,0:T(8,128)S(1)} %contributions.6.x_ref), channel_id=1, source_target_pairs={{0,4},{4,8},{8,12},{12,16},{16,20},{20,24},{24,28},{1,5},{5,9},{9,... | collective-permute-start | bytes 1572872 | tf_op jit(solution)/shard_map/ppermute | solution.py:48
  127.1 1.3 collective-permute-start.20
  128.5 1.7 taper_rows.7
  130.3 3.8 %collective-permute-start.26 = (f32[12,32,128]{2,1,0:T(8,128)S(1)}, f32[12,32,128]{2,1,0:T(8,128)S(1)}, u32[]{:S(2)}, u32[]{:S(2)}) collective-permute-start(f32[12,32,128]{2,1,0:T(8,128)S(1)} %get-tuple-element.68), channel_id=1, source_target_pairs={{0,3},{1,0},{2,1},{3,2},{4,7},{5,4},{6,5},{7,6},{8,11},{9,8},{10,9... | collective-permute-start | bytes 589832 | tf_op jit(solution)/shard_map/ppermute | solution.py:48
  135.3 3.8 %collective-permute-start.22 = (f32[8,32,128]{2,1,0:T(8,128)S(1)}, f32[8,32,128]{2,1,0:T(8,128)S(1)}, u32[]{:S(2)}, u32[]{:S(2)}) collective-permute-start(f32[8,32,128]{2,1,0:T(8,128)S(1)} %get-tuple-element.65), channel_id=1, source_target_pairs={{0,3},{1,0},{2,1},{3,2},{4,7},{5,4},{6,5},{7,6},{8,11},{9,8},{10,9... | collective-permute-start | bytes 393224 | tf_op jit(solution)/shard_map/ppermute | solution.py:48
  139.1 3.1 %taper_columns.6 = (f32[3,32,128]{2,1,0:T(8,128)S(1)}, f32[8,128]{1,0:T(8,128)S(1)}) custom-call(f32[48,32,128]{2,1,0:T(8,128)S(1)} %get-tuple-element.66.refs_0_, f32[12,32,128]{2,1,0:T(8,128)S(1)} %collective-permute-done.25.refs_1_, f32[12,32,128]{2,1,0:T(8,128)S(1)} %collective-permute-done.26.refs_2_, ...), custom_call_target="tpu_custom_call" | custom-call | tf_op jit(solution)/shard_map/taper_columns/pallas_call | solution.py:470
  142.2 2.1 %taper_columns.7 = (f32[3,32,128]{2,1,0:T(8,128)S(1)}, f32[8,128]{1,0:T(8,128)S(1)}) custom-call(f32[32,32,128]{2,1,0:T(8,128)S(1)} %get-tuple-element.63.refs_0_, f32[8,32,128]{2,1,0:T(8,128)S(1)} %collective-permute-done.21.refs_1_, f32[8,32,128]{2,1,0:T(8,128)S(1)} %collective-permute-done.22.refs_2_, ...), custom_call_target="tpu_custom_call" | custom-call | tf_op jit(solution)/shard_map/taper_columns/pallas_call | solution.py:470
  145.2 2.8 %collective-permute-done.27 = f32[8,128]{1,0:T(8,128)S(1)} collective-permute-done((f32[8,128]{1,0:T(8,128)S(1)}, f32[8,128]{1,0:T(8,128)S(1)}, u32[]{:S(2)}, u32[]{:S(2)}) %collective-permute-start.27) | collective-permute-done | bytes 4128 | tf_op jit(solution)/shard_map/ppermute | solution.py:61
  148.0 2.2 %collective-permute-start.28 = (f32[8,128]{1,0:T(8,128)S(1)}, f32[8,128]{1,0:T(8,128)S(1)}, u32[]{:S(2)}, u32[]{:S(2)}) collective-permute-start(f32[8,128]{1,0:T(8,128)S(1)} %add.28), channel_id=1, source_target_pairs={{0,2},{1,3},{2,0},{3,1},{4,6},{5,7},{6,4},{7,5},{8,10},{9,11},{10,... | collective-permute-start | bytes 12296 | tf_op jit(solution)/shard_map/ppermute | solution.py:61
  150.2 2.9 %collective-permute-done.28 = f32[8,128]{1,0:T(8,128)S(1)} collective-permute-done((f32[8,128]{1,0:T(8,128)S(1)}, f32[8,128]{1,0:T(8,128)S(1)}, u32[]{:S(2)}, u32[]{:S(2)}) %collective-permute-start.28) | collective-permute-done | bytes 4128 | tf_op jit(solution)/shard_map/ppermute | solution.py:61
  153.1 13.6 %collective-permute-start.29 = (f32[8,128]{1,0:T(8,128)S(1)}, f32[8,128]{1,0:T(8,128)S(1)}, u32[]{:S(2)}, u32[]{:S(2)}) collective-permute-start(f32[8,128]{1,0:T(8,128)S(1)} %add.29), channel_id=1, source_target_pairs={{0,4},{4,0},{8,12},{12,8},{16,20},{20,16},{24,28},{28,24},{1,5},{5... | collective-permute-start | bytes 12296 | tf_op jit(solution)/shard_map/ppermute | solution.py:61
  167.6 7.4 %collective-permute-start.30 = (f32[8,128]{1,0:T(8,128)S(1)}, f32[8,128]{1,0:T(8,128)S(1)}, u32[]{:S(2)}, u32[]{:S(2)}) collective-permute-start(f32[8,128]{1,0:T(8,128)S(1)} %add.30), channel_id=1, source_target_pairs={{0,8},{4,12},{8,0},{12,4},{16,24},{20,28},{24,16},{28,20},{1,9},{5... | collective-permute-start | bytes 12296 | tf_op jit(solution)/shard_map/ppermute | solution.py:61
  175.0 1.6 collective-permute-done.30
  177.2 2.9 %collective-permute-done.31 = f32[8,128]{1,0:T(8,128)S(1)} collective-permute-done((f32[8,128]{1,0:T(8,128)S(1)}, f32[8,128]{1,0:T(8,128)S(1)}, u32[]{:S(2)}, u32[]{:S(2)}) %collective-permute-start.31) | collective-permute-done | bytes 4128 | tf_op jit(solution)/shard_map/ppermute | solution.py:61
  180.2 2.9 %analysis.1 = (f32[80,32,128]{2,1,0:T(8,128)}, f32[80,32,128]{2,1,0:T(8,128)}, f32[80,32,128]{2,1,0:T(8,128)}) custom-call(f32[80,32,128]{2,1,0:T(8,128)S(1)} %get-tuple-element.49.h_ref.refs_7_, f32[80,32,128]{2,1,0:T(8,128)S(1)} %get-tuple-element.50.u_ref.refs_8_, f32[80,32,128]{2,1,0:T(8,128)S(1)} %get-tuple-element.51.v_ref.refs_9_, ...), custom_call_target="tpu_custom_call" | custom-call | tf_op jit(solution)/shard_map/analysis/pallas_call | solution.py:499
  (81 shorter events, 11.3 us)
Async XLA Ops:
  0.6 1.3 copy-start
  1.9 1.3 copy-start.2
  3.3 1.3 copy-start.4
  5.8 12.4 %copy-start.12 = (f32[32,128]{1,0:T(8,128)S(1)}, f32[32,128]{1,0:T(8,128)}, u32[]{:S(2)}) copy-start(f32[32,128]{1,0:T(8,128)} %param.30) | copy-start | bytes 49156
  5.8 12.4 %copy-start.13 = (s32[32,128]{1,0:T(8,128)S(1)}, s32[32,128]{1,0:T(8,128)}, u32[]{:S(2)}) copy-start(s32[32,128]{1,0:T(8,128)} %param.29) | copy-start | bytes 49156
  5.8 12.4 %copy-start.14 = (f32[32,128]{1,0:T(8,128)S(1)}, f32[32,128]{1,0:T(8,128)}, u32[]{:S(2)}) copy-start(f32[32,128]{1,0:T(8,128)} %param.28) | copy-start | bytes 49156
  5.8 25.1 %collective-permute-start = (f32[80,16,128]{2,1,0:T(8,128)}, f32[80,16,128]{2,1,0:T(8,128)}, u32[]{:S(2)}, u32[]{:S(2)}) collective-permute-start(f32[80,16,128]{2,1,0:T(8,128)} %get-tuple-element.39), channel_id=1, source_target_pairs={{0,4},{4,8},{8,12},{12,16},{16,20},{20,24},{24,28},{1,5},{5,9},{9,... | collective-permute-start | bytes 1966088 | tf_op jit(solution)/shard_map/ppermute | solution.py:48
  9.2 21.7 %copy-start.1 = (f32[80,32,128]{2,1,0:T(8,128)S(1)}, f32[80,32,128]{2,1,0:T(8,128)}, u32[]{:S(2)}) copy-start(f32[80,32,128]{2,1,0:T(8,128)} %h_ref.3) | copy-start | bytes 3932164
  9.2 21.7 %copy-start.3 = (f32[80,32,128]{2,1,0:T(8,128)S(1)}, f32[80,32,128]{2,1,0:T(8,128)}, u32[]{:S(2)}) copy-start(f32[80,32,128]{2,1,0:T(8,128)} %u_ref.3) | copy-start | bytes 3932164
  12.4 9.5 %collective-permute-start.2 = (f32[10,32,128]{2,1,0:T(8,128)}, f32[10,32,128]{2,1,0:T(8,128)S(1)}, u32[]{:S(2)}, u32[]{:S(2)}) collective-permute-start(f32[10,32,128]{2,1,0:T(8,128)} %get-tuple-element.47), channel_id=1, source_target_pairs={{0,1},{1,2},{2,3},{3,0},{4,5},{5,6},{6,7},{7,4},{8,9},{9,10},{10,1... | collective-permute-start | bytes 491528 | tf_op jit(solution)/shard_map/ppermute | solution.py:48
  14.8 10.5 %collective-permute-start.3 = (f32[10,32,128]{2,1,0:T(8,128)}, f32[10,32,128]{2,1,0:T(8,128)S(1)}, u32[]{:S(2)}, u32[]{:S(2)}) collective-permute-start(f32[10,32,128]{2,1,0:T(8,128)} %get-tuple-element.48), channel_id=1, source_target_pairs={{0,3},{1,0},{2,1},{3,2},{4,7},{5,4},{6,5},{7,6},{8,11},{9,8},{10,9... | collective-permute-start | bytes 491528 | tf_op jit(solution)/shard_map/ppermute | solution.py:48
  16.9 14.0 %collective-permute-start.1 = (f32[80,16,128]{2,1,0:T(8,128)}, f32[80,16,128]{2,1,0:T(8,128)}, u32[]{:S(2)}, u32[]{:S(2)}) collective-permute-start(f32[80,16,128]{2,1,0:T(8,128)} %get-tuple-element.43), channel_id=1, source_target_pairs={{4,0},{8,4},{12,8},{16,12},{20,16},{24,20},{28,24},{5,1},{9,5},{13... | collective-permute-start | bytes 1966088 | tf_op jit(solution)/shard_map/ppermute | solution.py:48
  25.4 3.1 %collective-permute-start.4 = (f32[20,8,128]{2,1,0:T(8,128)S(1)}, f32[20,8,128]{2,1,0:T(8,128)S(1)}, u32[]{:S(2)}, u32[]{:S(2)}) collective-permute-start(f32[20,8,128]{2,1,0:T(8,128)S(1)} %get-tuple-element.76), channel_id=1, source_target_pairs={{0,4},{4,8},{8,12},{12,16},{16,20},{20,24},{24,28},{1,5},{5,9},{9,... | collective-permute-start | bytes 245768 | tf_op jit(solution)/shard_map/ppermute | solution.py:48
  27.1 3.8 %collective-permute-start.5 = (f32[20,8,128]{2,1,0:T(8,128)S(1)}, f32[20,8,128]{2,1,0:T(8,128)S(1)}, u32[]{:S(2)}, u32[]{:S(2)}) collective-permute-start(f32[20,8,128]{2,1,0:T(8,128)S(1)} %get-tuple-element.75), channel_id=1, source_target_pairs={{4,0},{8,4},{12,8},{16,12},{20,16},{24,20},{28,24},{5,1},{9,5},{13... | collective-permute-start | bytes 245768 | tf_op jit(solution)/shard_map/ppermute | solution.py:48
  30.9 1.3 copy-start.5
  32.2 0.9 copy-start.10
  33.1 0.9 copy-start.11
  54.7 11.0 %copy-start.9 = (bf16[64,192]{1,0:T(8,128)(2,1)S(1)}, bf16[64,192]{1,0:T(8,128)(2,1)}, u32[]{:S(2)}) copy-start(bf16[64,192]{1,0:T(8,128)(2,1)} %constant.28.clone.table_ref) | copy-start | bytes 73732
  54.7 10.9 %collective-permute-start.10 = (f32[48,32,128]{2,1,0:T(8,128)S(1)}, f32[48,32,128]{2,1,0:T(8,128)S(1)}, u32[]{:S(2)}, u32[]{:S(2)}) collective-permute-start(f32[48,32,128]{2,1,0:T(8,128)S(1)} %contributions.5.x_ref), channel_id=1, source_target_pairs={{0,4},{4,8},{8,12},{12,16},{16,20},{20,24},{24,28},{1,5},{5,9},{9,... | collective-permute-start | bytes 2359304 | tf_op jit(solution)/shard_map/ppermute | solution.py:48
  59.7 5.9 %collective-permute-start.11 = (f32[48,32,128]{2,1,0:T(8,128)S(1)}, f32[48,32,128]{2,1,0:T(8,128)S(1)}, u32[]{:S(2)}, u32[]{:S(2)}) collective-permute-start(f32[48,32,128]{2,1,0:T(8,128)S(1)} %contributions.5.x_ref), channel_id=1, source_target_pairs={{4,0},{8,4},{12,8},{16,12},{20,16},{24,20},{28,24},{5,1},{9,5},{13... | collective-permute-start | bytes 2359304 | tf_op jit(solution)/shard_map/ppermute | solution.py:48
  61.2 10.0 %collective-permute-start.6 = (f32[32,32,128]{2,1,0:T(8,128)S(1)}, f32[32,32,128]{2,1,0:T(8,128)S(1)}, u32[]{:S(2)}, u32[]{:S(2)}) collective-permute-start(f32[32,32,128]{2,1,0:T(8,128)S(1)} %contributions.4.x_ref), channel_id=1, source_target_pairs={{0,4},{4,8},{8,12},{12,16},{16,20},{20,24},{24,28},{1,5},{5,9},{9,... | collective-permute-start | bytes 1572872 | tf_op jit(solution)/shard_map/ppermute | solution.py:48
  64.3 7.0 %collective-permute-start.7 = (f32[32,32,128]{2,1,0:T(8,128)S(1)}, f32[32,32,128]{2,1,0:T(8,128)S(1)}, u32[]{:S(2)}, u32[]{:S(2)}) collective-permute-start(f32[32,32,128]{2,1,0:T(8,128)S(1)} %contributions.4.x_ref), channel_id=1, source_target_pairs={{4,0},{8,4},{12,8},{16,12},{20,16},{24,20},{28,24},{5,1},{9,5},{13... | collective-permute-start | bytes 1572872 | tf_op jit(solution)/shard_map/ppermute | solution.py:48
  67.4 9.0 %copy-start.6 = (bf16[256,256]{1,0:T(8,128)(2,1)S(1)}, bf16[256,256]{1,0:T(8,128)(2,1)}, u32[]{:S(2)}) copy-start(bf16[256,256]{1,0:T(8,128)(2,1)} %constant.29.clone.refs_4_) | copy-start | bytes 393220
  67.4 8.9 %copy-start.7 = (bf16[256,256]{1,0:T(8,128)(2,1)S(1)}, bf16[256,256]{1,0:T(8,128)(2,1)}, u32[]{:S(2)}) copy-start(bf16[256,256]{1,0:T(8,128)(2,1)} %constant.30.clone.refs_5_) | copy-start | bytes 393220
  67.4 8.9 %copy-start.8 = (bf16[256,256]{1,0:T(8,128)(2,1)S(1)}, bf16[256,256]{1,0:T(8,128)(2,1)}, u32[]{:S(2)}) copy-start(bf16[256,256]{1,0:T(8,128)(2,1)} %constant.31.clone.refs_6_) | copy-start | bytes 393220
  67.4 8.9 %collective-permute-start.12 = (f32[12,32,128]{2,1,0:T(8,128)S(1)}, f32[12,32,128]{2,1,0:T(8,128)S(1)}, u32[]{:S(2)}, u32[]{:S(2)}) collective-permute-start(f32[12,32,128]{2,1,0:T(8,128)S(1)} %get-tuple-element.57), channel_id=1, source_target_pairs={{0,1},{1,2},{2,3},{3,0},{4,5},{5,6},{6,7},{7,4},{8,9},{9,10},{10,1... | collective-permute-start | bytes 589832 | tf_op jit(solution)/shard_map/ppermute | solution.py:48
  68.5 7.8 %collective-permute-start.13 = (f32[12,32,128]{2,1,0:T(8,128)S(1)}, f32[12,32,128]{2,1,0:T(8,128)S(1)}, u32[]{:S(2)}, u32[]{:S(2)}) collective-permute-start(f32[12,32,128]{2,1,0:T(8,128)S(1)} %get-tuple-element.58), channel_id=1, source_target_pairs={{0,3},{1,0},{2,1},{3,2},{4,7},{5,4},{6,5},{7,6},{8,11},{9,8},{10,9... | collective-permute-start | bytes 589832 | tf_op jit(solution)/shard_map/ppermute | solution.py:48
  72.4 6.8 %collective-permute-start.8 = (f32[8,32,128]{2,1,0:T(8,128)S(1)}, f32[8,32,128]{2,1,0:T(8,128)S(1)}, u32[]{:S(2)}, u32[]{:S(2)}) collective-permute-start(f32[8,32,128]{2,1,0:T(8,128)S(1)} %get-tuple-element.54), channel_id=1, source_target_pairs={{0,1},{1,2},{2,3},{3,0},{4,5},{5,6},{6,7},{7,4},{8,9},{9,10},{10,1... | collective-permute-start | bytes 393224 | tf_op jit(solution)/shard_map/ppermute | solution.py:48
  72.5 6.8 %collective-permute-start.9 = (f32[8,32,128]{2,1,0:T(8,128)S(1)}, f32[8,32,128]{2,1,0:T(8,128)S(1)}, u32[]{:S(2)}, u32[]{:S(2)}) collective-permute-start(f32[8,32,128]{2,1,0:T(8,128)S(1)} %get-tuple-element.55), channel_id=1, source_target_pairs={{0,3},{1,0},{2,1},{3,2},{4,7},{5,4},{6,5},{7,6},{8,11},{9,8},{10,9... | collective-permute-start | bytes 393224 | tf_op jit(solution)/shard_map/ppermute | solution.py:48
  79.2 35.6 %copy-start.15 = (s32[2]{0:T(128)S(1)}, s32[2]{0:T(128)}, u32[]{:S(2)}) copy-start(s32[2]{0:T(128)} %param.31) | copy-start | bytes 28
  81.2 3.7 %collective-permute-start.14 = (f32[8,128]{1,0:T(8,128)S(1)}, f32[8,128]{1,0:T(8,128)S(1)}, u32[]{:S(2)}, u32[]{:S(2)}) collective-permute-start(f32[8,128]{1,0:T(8,128)S(1)} %get-tuple-element.62), channel_id=1, source_target_pairs={{0,1},{1,0},{2,3},{3,2},{4,5},{5,4},{6,7},{7,6},{8,9},{9,8},{10,11... | collective-permute-start | bytes 12296 | tf_op jit(solution)/shard_map/ppermute | solution.py:61
  84.8 5.9 %collective-permute-start.15 = (f32[8,128]{1,0:T(8,128)S(1)}, f32[8,128]{1,0:T(8,128)S(1)}, u32[]{:S(2)}, u32[]{:S(2)}) collective-permute-start(f32[8,128]{1,0:T(8,128)S(1)} %add.24), channel_id=1, source_target_pairs={{0,2},{1,3},{2,0},{3,1},{4,6},{5,7},{6,4},{7,5},{8,10},{9,11},{10,... | collective-permute-start | bytes 12296 | tf_op jit(solution)/shard_map/ppermute | solution.py:61
  90.7 16.1 %collective-permute-start.16 = (f32[8,128]{1,0:T(8,128)S(1)}, f32[8,128]{1,0:T(8,128)S(1)}, u32[]{:S(2)}, u32[]{:S(2)}) collective-permute-start(f32[8,128]{1,0:T(8,128)S(1)} %add.25), channel_id=1, source_target_pairs={{0,4},{4,0},{8,12},{12,8},{16,20},{20,16},{24,28},{28,24},{1,5},{5... | collective-permute-start | bytes 12296 | tf_op jit(solution)/shard_map/ppermute | solution.py:61
  106.9 8.0 %collective-permute-start.17 = (f32[8,128]{1,0:T(8,128)S(1)}, f32[8,128]{1,0:T(8,128)S(1)}, u32[]{:S(2)}, u32[]{:S(2)}) collective-permute-start(f32[8,128]{1,0:T(8,128)S(1)} %add.26), channel_id=1, source_target_pairs={{0,8},{4,12},{8,0},{12,4},{16,24},{20,28},{24,16},{28,20},{1,9},{5... | collective-permute-start | bytes 12296 | tf_op jit(solution)/shard_map/ppermute | solution.py:61
  114.8 3.6 %collective-permute-start.18 = (f32[8,128]{1,0:T(8,128)S(1)}, f32[8,128]{1,0:T(8,128)S(1)}, u32[]{:S(2)}, u32[]{:S(2)}) collective-permute-start(f32[8,128]{1,0:T(8,128)S(1)} %add.27), channel_id=1, source_target_pairs={{0,16},{4,20},{8,24},{12,28},{16,0},{20,4},{24,8},{28,12},{1,17},{... | collective-permute-start | bytes 12296 | tf_op jit(solution)/shard_map/ppermute | solution.py:61
  118.9 9.6 %collective-permute-start.23 = (f32[48,32,128]{2,1,0:T(8,128)S(1)}, f32[48,32,128]{2,1,0:T(8,128)S(1)}, u32[]{:S(2)}, u32[]{:S(2)}) collective-permute-start(f32[48,32,128]{2,1,0:T(8,128)S(1)} %contributions.7.x_ref), channel_id=1, source_target_pairs={{0,4},{4,8},{8,12},{12,16},{16,20},{20,24},{24,28},{1,5},{5,9},{9,... | collective-permute-start | bytes 2359304 | tf_op jit(solution)/shard_map/ppermute | solution.py:48
  120.2 8.2 %collective-permute-start.24 = (f32[48,32,128]{2,1,0:T(8,128)S(1)}, f32[48,32,128]{2,1,0:T(8,128)S(1)}, u32[]{:S(2)}, u32[]{:S(2)}) collective-permute-start(f32[48,32,128]{2,1,0:T(8,128)S(1)} %contributions.7.x_ref), channel_id=1, source_target_pairs={{4,0},{8,4},{12,8},{16,12},{20,16},{24,20},{28,24},{5,1},{9,5},{13... | collective-permute-start | bytes 2359304 | tf_op jit(solution)/shard_map/ppermute | solution.py:48
  121.9 12.2 %collective-permute-start.19 = (f32[32,32,128]{2,1,0:T(8,128)S(1)}, f32[32,32,128]{2,1,0:T(8,128)S(1)}, u32[]{:S(2)}, u32[]{:S(2)}) collective-permute-start(f32[32,32,128]{2,1,0:T(8,128)S(1)} %contributions.6.x_ref), channel_id=1, source_target_pairs={{0,4},{4,8},{8,12},{12,16},{16,20},{20,24},{24,28},{1,5},{5,9},{9,... | collective-permute-start | bytes 1572872 | tf_op jit(solution)/shard_map/ppermute | solution.py:48
  127.1 6.9 %collective-permute-start.20 = (f32[32,32,128]{2,1,0:T(8,128)S(1)}, f32[32,32,128]{2,1,0:T(8,128)S(1)}, u32[]{:S(2)}, u32[]{:S(2)}) collective-permute-start(f32[32,32,128]{2,1,0:T(8,128)S(1)} %contributions.6.x_ref), channel_id=1, source_target_pairs={{4,0},{8,4},{12,8},{16,12},{20,16},{24,20},{28,24},{5,1},{9,5},{13... | collective-permute-start | bytes 1572872 | tf_op jit(solution)/shard_map/ppermute | solution.py:48
  130.2 8.9 %collective-permute-start.25 = (f32[12,32,128]{2,1,0:T(8,128)S(1)}, f32[12,32,128]{2,1,0:T(8,128)S(1)}, u32[]{:S(2)}, u32[]{:S(2)}) collective-permute-start(f32[12,32,128]{2,1,0:T(8,128)S(1)} %get-tuple-element.67), channel_id=1, source_target_pairs={{0,1},{1,2},{2,3},{3,0},{4,5},{5,6},{6,7},{7,4},{8,9},{9,10},{10,1... | collective-permute-start | bytes 589832 | tf_op jit(solution)/shard_map/ppermute | solution.py:48
  130.3 8.8 %collective-permute-start.26 = (f32[12,32,128]{2,1,0:T(8,128)S(1)}, f32[12,32,128]{2,1,0:T(8,128)S(1)}, u32[]{:S(2)}, u32[]{:S(2)}) collective-permute-start(f32[12,32,128]{2,1,0:T(8,128)S(1)} %get-tuple-element.68), channel_id=1, source_target_pairs={{0,3},{1,0},{2,1},{3,2},{4,7},{5,4},{6,5},{7,6},{8,11},{9,8},{10,9... | collective-permute-start | bytes 589832 | tf_op jit(solution)/shard_map/ppermute | solution.py:48
  135.2 7.0 %collective-permute-start.21 = (f32[8,32,128]{2,1,0:T(8,128)S(1)}, f32[8,32,128]{2,1,0:T(8,128)S(1)}, u32[]{:S(2)}, u32[]{:S(2)}) collective-permute-start(f32[8,32,128]{2,1,0:T(8,128)S(1)} %get-tuple-element.64), channel_id=1, source_target_pairs={{0,1},{1,2},{2,3},{3,0},{4,5},{5,6},{6,7},{7,4},{8,9},{9,10},{10,1... | collective-permute-start | bytes 393224 | tf_op jit(solution)/shard_map/ppermute | solution.py:48
  135.3 6.9 %collective-permute-start.22 = (f32[8,32,128]{2,1,0:T(8,128)S(1)}, f32[8,32,128]{2,1,0:T(8,128)S(1)}, u32[]{:S(2)}, u32[]{:S(2)}) collective-permute-start(f32[8,32,128]{2,1,0:T(8,128)S(1)} %get-tuple-element.65), channel_id=1, source_target_pairs={{0,3},{1,0},{2,1},{3,2},{4,7},{5,4},{6,5},{7,6},{8,11},{9,8},{10,9... | collective-permute-start | bytes 393224 | tf_op jit(solution)/shard_map/ppermute | solution.py:48
  144.4 3.7 %collective-permute-start.27 = (f32[8,128]{1,0:T(8,128)S(1)}, f32[8,128]{1,0:T(8,128)S(1)}, u32[]{:S(2)}, u32[]{:S(2)}) collective-permute-start(f32[8,128]{1,0:T(8,128)S(1)} %get-tuple-element.74), channel_id=1, source_target_pairs={{0,1},{1,0},{2,3},{3,2},{4,5},{5,4},{6,7},{7,6},{8,9},{9,8},{10,11... | collective-permute-start | bytes 12296 | tf_op jit(solution)/shard_map/ppermute | solution.py:61
  148.0 5.1 %collective-permute-start.28 = (f32[8,128]{1,0:T(8,128)S(1)}, f32[8,128]{1,0:T(8,128)S(1)}, u32[]{:S(2)}, u32[]{:S(2)}) collective-permute-start(f32[8,128]{1,0:T(8,128)S(1)} %add.28), channel_id=1, source_target_pairs={{0,2},{1,3},{2,0},{3,1},{4,6},{5,7},{6,4},{7,5},{8,10},{9,11},{10,... | collective-permute-start | bytes 12296 | tf_op jit(solution)/shard_map/ppermute | solution.py:61
  153.1 14.4 %collective-permute-start.29 = (f32[8,128]{1,0:T(8,128)S(1)}, f32[8,128]{1,0:T(8,128)S(1)}, u32[]{:S(2)}, u32[]{:S(2)}) collective-permute-start(f32[8,128]{1,0:T(8,128)S(1)} %add.29), channel_id=1, source_target_pairs={{0,4},{4,0},{8,12},{12,8},{16,20},{20,16},{24,28},{28,24},{1,5},{5... | collective-permute-start | bytes 12296 | tf_op jit(solution)/shard_map/ppermute | solution.py:61
  167.6 9.0 %collective-permute-start.30 = (f32[8,128]{1,0:T(8,128)S(1)}, f32[8,128]{1,0:T(8,128)S(1)}, u32[]{:S(2)}, u32[]{:S(2)}) collective-permute-start(f32[8,128]{1,0:T(8,128)S(1)} %add.30), channel_id=1, source_target_pairs={{0,8},{4,12},{8,0},{12,4},{16,24},{20,28},{24,16},{28,20},{1,9},{5... | collective-permute-start | bytes 12296 | tf_op jit(solution)/shard_map/ppermute | solution.py:61
  176.6 3.6 %collective-permute-start.31 = (f32[8,128]{1,0:T(8,128)S(1)}, f32[8,128]{1,0:T(8,128)S(1)}, u32[]{:S(2)}, u32[]{:S(2)}) collective-permute-start(f32[8,128]{1,0:T(8,128)S(1)} %add.31), channel_id=1, source_target_pairs={{0,16},{4,20},{8,24},{12,28},{16,0},{20,4},{24,8},{28,12},{1,17},{... | collective-permute-start | bytes 12296 | tf_op jit(solution)/shard_map/ppermute | solution.py:61

commit v3 on v2

--- a/solution.py
+++ b/solution.py
@@ -8,8 +8,8 @@
 from jax.experimental.pallas import tpu as pltpu
 from jax.sharding import PartitionSpec as P
 
+
 STEPS = 3
-ITERS = 2
 LWIDTH = 32
 LSCALE = 12
 
@@ -60,7 +60,7 @@
             block = block + half
             half = lax.ppermute(block, axis, [(i, i ^ reach) for i in range(count)])
             reach *= 2
-    return jnp.stack([block, half])
+    return block, half
 
 
 def taper(offset):
@@ -118,45 +118,52 @@
     return jnp.where(lane == k, spin(block, SLOT * k + SEAM, 1), 0.0)
 
 
-def row_pack_kernel(u_ref, v_ref, h_ref, top_ref, bottom_ref):
-    members, rows, _ = u_ref.shape
+def row_pack_kernel(uf_ref, vf_ref, hf_ref, ul_ref, vl_ref, hl_ref, top_ref, bottom_ref):
     sub = iota((SUB, LANES), 0)
-    last = slice(rows - SUB, rows)
 
     def member(k, _):
-        u = u_ref[k, :SUB]
-        top_ref[k, :SUB] = jnp.where(sub < 6, v_ref[k, :SUB], spin(u, 6, 0))
-        top_ref[k, SUB:] = jnp.where(sub < 5, h_ref[k, :SUB], spin(u, 3, 0))
-        u = u_ref[k, last]
-        bottom_ref[k, :SUB] = jnp.where(sub < 2, spin(u, 5, 0), v_ref[k, last])
-        bottom_ref[k, SUB:] = jnp.where(sub < 3, spin(u, 3, 0), h_ref[k, last])
+        u = uf_ref[k]
+        top_ref[k, :SUB] = jnp.where(sub < 6, vf_ref[k], spin(u, 6, 0))
+        top_ref[k, SUB:] = jnp.where(sub < 5, hf_ref[k], spin(u, 3, 0))
+        u = ul_ref[k]
+        bottom_ref[k, :SUB] = jnp.where(sub < 2, spin(u, 5, 0), vl_ref[k])
+        bottom_ref[k, SUB:] = jnp.where(sub < 3, spin(u, 3, 0), hl_ref[k])
         return 0
 
-    lax.fori_loop(0, members, member, 0, unroll=8)
+    lax.fori_loop(0, uf_ref.shape[0], member, 0, unroll=4)
 
 
 def pack_rows(height, eastward, northward):
     members, rows, cols = height.shape
+    count = members // 2
+    first = pl.BlockSpec((count, SUB, cols), lambda g: (g, 0, 0))
+    last = pl.BlockSpec((count, SUB, cols), lambda g: (g, rows // SUB - 1, 0))
+    edge = pl.BlockSpec((count, 2 * SUB, cols), lambda g: (g, 0, 0))
+    fields = (eastward, northward, height)
     return pl.pallas_call(
         row_pack_kernel,
         name="pack_rows",
-        compiler_params=GRANT,
-        in_specs=[VMEM] * 3,
-        out_specs=[VMEM] * 2,
+        grid=(members // count,),
+        in_specs=[first] * 3 + [last] * 3,
+        out_specs=[edge] * 2,
         out_shape=[f32(members, 2 * SUB, cols)] * 2,
-    )(eastward, northward, height)
-
-
-def column_pack_kernel(u_ref, v_ref, h_ref, left_ref, right_ref, *own_refs):
+    )(*fields, *fields)
+
+
+def column_pack_kernel(u_ref, v_ref, h_ref, left_ref, right_ref, *refs):
+    own_refs, kept_refs = refs[:3], refs[3:]
     members, rows, _ = u_ref.shape
     slot = iota((rows, LANES), 1) % SLOT
 
     def group(g, _):
         packs = []
-        for ref, own in zip((u_ref, v_ref, h_ref), own_refs):
-            pack = slot_pack(ref[g * PACK], 0)
-            for k in range(1, PACK):
-                pack = pack + slot_pack(ref[g * PACK + k], k)
+        for ref, own, kept in zip((u_ref, v_ref, h_ref), own_refs, kept_refs):
+            pack = None
+            for k in range(PACK):
+                x = ref[g * PACK + k]
+                kept[g * PACK + k] = x
+                piece = slot_pack(x, k)
+                pack = piece if k == 0 else pack + piece
             own[g] = pack
             packs.append(pack)
 
@@ -182,66 +189,61 @@
         name="pack_columns",
         compiler_params=GRANT,
         in_specs=[VMEM] * 3,
-        out_specs=[VMEM] * 5,
-        out_shape=[f32(groups, rows, LANES)] * 5,
+        out_specs=[VMEM] * 8,
+        out_shape=[f32(groups, rows, LANES)] * 5 + [f32(members, rows, cols)] * 3,
     )(eastward, northward, height)
 
 
 def difference_table(cols):
     lane = np.arange(cols)
-    inner = (lane[:, None] == lane[None, :] + 1).astype(np.float32)
-    inner -= lane[:, None] == lane[None, :] - 1
-    wall = np.zeros((LANES, cols), np.float32)
-    wall[SEAM - 1 :: SLOT, 0] = -1
-    wall[SEAM::SLOT, cols - 1] = 1
-    return np.concatenate([inner, inner, wall, wall]).astype(jnp.bfloat16)
-
-
-def slot_masks(tall):
-    lane = np.arange(LANES) // SLOT
-    masks = lane[None, None, :] == np.arange(PACK)[:, None, None]
-    return np.broadcast_to(masks, (PACK, tall, LANES)).astype(jnp.bfloat16)
+    table = (lane[:, None] == lane[None, :] + 1).astype(np.float32)
+    table -= lane[:, None] == lane[None, :] - 1
+    return np.concatenate([table, table]).astype(jnp.bfloat16)
 
 
 def forecast_kernel(
     h_ref, u_ref, v_ref, above_ref, below_ref, ownu_ref, ownv_ref, ownh_ref, hall_ref, halr_ref,
-    cornu_ref, cornd_ref, table_ref, mask_ref, edge_ref,
+    cornu_ref, cornd_ref, table_ref,
     ho_ref, uo_ref, vo_ref, mean_ref,
     us_ref, vs_ref, hs_ref, lhs_ref, sum_ref,
 ):
-    members, rows, cols = h_ref.shape
-    groups = members // PACK
+    _, rows, _ = h_ref.shape
+    groups = pl.num_programs(0)
+    members = groups * PACK
     tall = rows + 2 * SUB
     batch = PACK + 2
     half = batch // 2
     slot = iota((tall, LANES), 1) % SLOT
     row = iota((tall, LANES), 0)
     sub = iota((SUB, LANES), 0)
-    outside = ((row < SUB) & (edge_ref[0] == 1)) | ((row >= rows + SUB) & (edge_ref[1] == 1))
+    here, tiles = lax.axis_index("member"), lax.axis_size("member")
+    outside = ((row < SUB) & (here == 0)) | ((row >= rows + SUB) & (here == tiles - 1))
     pull = jnp.where(outside, 0.0, 0.2)
     mid, low, high = slice(SUB, SUB + tall), slice(SUB - 1, SUB + tall - 1), slice(SUB + 1, SUB + tall + 1)
     core = slice(2 * SUB, 2 * SUB + rows)
 
+    ends = (iota((tall, LANES), 1) == 0) | (iota((tall, LANES), 1) == LANES - 1)
+    order = (PACK, PACK + 1, *range(PACK))
+
     def differences(ref):
-        wall = jnp.where(slot == SEAM - 1, ref[PACK, mid], ref[PACK + 1, mid])
-        walls = split(wall)
-        for j in range(batch):
-            for i, part in enumerate(split(ref[j, mid])):
-                lhs_ref[j, :, i * LANES : (i + 1) * LANES] = part
-            if j < PACK:
-                for i, part in enumerate(walls):
-                    lhs_ref[j, :, (i + 2) * LANES : (i + 3) * LANES] = part * mask_ref[j]
-        out = []
+        right = spin(ref[PACK + 1, mid], -2, 1)
+        wall = jnp.where(slot == SEAM - 1, -ref[PACK, mid], right)
         for start in (0, half):
-            stack = lhs_ref[start : start + half].reshape(half * tall, 4 * LANES)
+            for at, j in enumerate(order[start : start + half], start):
+                for i, part in enumerate(split(ref[j, mid])):
+                    lhs_ref[at, :, i * LANES : (i + 1) * LANES] = part
+            stack = lhs_ref[start : start + half].reshape(half * tall, 2 * LANES)
             d = mm(stack, table_ref[...])
-            out += [d[j * tall : (j + 1) * tall] for j in range(half)]
-        return out
-
-    def group(g, _):
+            for at, j in enumerate(order[start : start + half]):
+                piece = d[at * tall : (at + 1) * tall]
+                if j < PACK:
+                    piece += jnp.where(ends, spin(wall, -(SLOT * j + SEAM - 1), 1), 0.0)
+                yield j, piece
+
+    def group():
         packs = [[None] * 2 for _ in range(3)]
         for k in range(PACK):
-            m = g * PACK + k
+            m = k
             a0, a1 = above_ref[m, :SUB], above_ref[m, SUB:]
             b0, b1 = below_ref[m, :SUB], below_ref[m, SUB:]
             ua = jnp.where(sub < 5, spin(a0, 3, 0), spin(a1, 5, 0))
@@ -254,19 +256,19 @@
                 for end, edge in enumerate((a, b)):
                     piece = slot_pack(edge, k)
                     packs[i][end] = piece if k == 0 else packs[i][end] + piece
-        left = jnp.concatenate([cornu_ref[g], hall_ref[g], cornd_ref[g]], axis=0)
-        right = jnp.concatenate([cornu_ref[groups + g], halr_ref[g], cornd_ref[groups + g]], axis=0)
+        left = jnp.concatenate([cornu_ref[0, 0], hall_ref[0], cornd_ref[0, 0]], axis=0)
+        right = jnp.concatenate([cornu_ref[1, 0], halr_ref[0], cornd_ref[1, 0]], axis=0)
         owns = ((us_ref, ownu_ref, EAST), (vs_ref, ownv_ref, SIDE), (hs_ref, ownh_ref, SIDE))
         for i, (state, own_ref, size) in enumerate(owns):
-            own = jnp.concatenate([packs[i][0], own_ref[g], packs[i][1]], axis=0)
+            own = jnp.concatenate([packs[i][0], own_ref[0], packs[i][1]], axis=0)
             state[PACK, mid] = jnp.where(slot < SEAM, spin(left, SEAM - size - PLACES[i], 1), own)
             state[PACK + 1, mid] = jnp.where(slot < SEAM, own, spin(right, SEAM - PLACES[i], 1))
 
         for step in range(STEPS):
             last = step == STEPS - 1
-            for j, d in enumerate(differences(us_ref)):
+            for j, d in differences(us_ref):
                 hs_ref[j, mid] = hs_ref[j, mid] - pull * (d + (vs_ref[j, high] - vs_ref[j, low]))
-            for j, d in enumerate(differences(hs_ref)):
+            for j, d in differences(hs_ref):
                 if last and j >= PACK:
                     continue
                 u, v = us_ref[j, mid], vs_ref[j, mid]
@@ -277,90 +279,125 @@
             total = sum_ref[i]
             for k in range(PACK):
                 x = state[k, core]
-                out[g * PACK + k] = x
+                out[k] = x
                 total = total + x
             sum_ref[i] = total
-        return 0
-
-    sum_ref[...] = jnp.zeros_like(sum_ref)
-    lhs_ref[...] = jnp.zeros_like(lhs_ref)
-    for state in (us_ref, vs_ref, hs_ref):
-        for j in range(batch):
-            state[j, :SUB] = jnp.zeros((SUB, LANES), jnp.float32)
-            state[j, SUB + tall :] = jnp.zeros((SUB, LANES), jnp.float32)
-    lax.fori_loop(0, groups, group, 0)
-    for i in range(3):
-        mean_ref[i] = sum_ref[i] / members
-
-
-def forecast(h, u, v, *rest):
+
+    @pl.when(pl.program_id(0) == 0)
+    def _():
+        sum_ref[...] = jnp.zeros_like(sum_ref)
+        for state in (us_ref, vs_ref, hs_ref):
+            for j in range(batch):
+                state[j, :SUB] = jnp.zeros((SUB, LANES), jnp.float32)
+                state[j, SUB + tall :] = jnp.zeros((SUB, LANES), jnp.float32)
+
+    group()
+
+    @pl.when(pl.program_id(0) == groups - 1)
+    def _():
+        for i in range(3):
+            mean_ref[i] = sum_ref[i] * (1.0 / members)
+
+
+def forecast(h, u, v, above, below, *rest):
     members, rows, cols = h.shape
+    groups = members // PACK
     tall = rows + 2 * SUB
     state = pltpu.VMEM((PACK + 2, tall + 2 * SUB, LANES), jnp.float32)
-    *halos, edge = rest
+    *strips, cornu, cornd = rest
+    cornu, cornd = (x.reshape(2, groups, SUB, LANES) for x in (cornu, cornd))
+    tile = pl.BlockSpec((PACK, rows, cols), lambda g: (g, 0, 0))
+    side = pl.BlockSpec((PACK, 2 * SUB, cols), lambda g: (g, 0, 0))
+    strip = pl.BlockSpec((1, rows, LANES), lambda g: (g, 0, 0))
+    corner = pl.BlockSpec((2, 1, SUB, LANES), lambda g: (0, g, 0, 0))
+    mean = pl.BlockSpec((3, rows, cols), lambda g: (0, 0, 0))
     return pl.pallas_call(
         forecast_kernel,
         name="forecast",
         compiler_params=GRANT,
-        in_specs=[VMEM] * (len(halos) + 5) + [SMEM],
-        out_specs=[VMEM] * 4,
+        grid=(groups,),
+        in_specs=[tile] * 3 + [side] * 2 + [strip] * 5 + [corner] * 2 + [VMEM],
+        out_specs=[tile] * 3 + [mean],
         out_shape=[f32(members, rows, cols)] * 3 + [f32(3, rows, cols)],
         scratch_shapes=[
             state,
             state,
             state,
-            pltpu.VMEM((PACK + 2, tall, 4 * LANES), jnp.bfloat16),
+            pltpu.VMEM((PACK + 2, tall, 2 * LANES), jnp.bfloat16),
             pltpu.VMEM((3, rows, cols), jnp.float32),
         ],
-    )(h, u, v, *halos, difference_table(cols), slot_masks(tall), edge)
-
-
-def factor(square_ref, step_ref, cells):
-    total = jnp.sum(square_ref[0] + square_ref[1], keepdims=True)
-    return step_ref[0] / jnp.sqrt(total / cells + 1e-06)
-
-
-def contrib_kernel(begin, cells, h_ref, u_ref, v_ref, mean_ref, obs_ref, *refs):
-    if len(refs) == 1:
-        (contrib_ref,) = refs
-        states = means = [mean_ref[i] for i in range(3)]
+    )(h, u, v, above, below, *strips, cornu, cornd, difference_table(cols))
+
+
+def factor(k, square_ref, half_ref, step_ref, cells):
+    total = jnp.sum(square_ref[...] + half_ref[...], keepdims=True)
+    return step_ref[k].astype(jnp.float32) / 64.0 / jnp.sqrt(total / cells + 1e-06)
+
+
+def slope_kernel(begin, h_ref, u_ref, v_ref, mean_ref, value_ref, seen_ref, precise_ref, *refs):
+    *sums, out_ref = refs
+    members = h_ref.shape[0]
+    extra = 2 if sums else 1
+    count = out_ref.shape[0] - (0 if begin else extra)
+    scale = 1.0 / float(np.sqrt(np.float32(members - 1)))
+    mh, mu, mv = (mean_ref[i] for i in range(3))
+    value, weight = value_ref[...], seen_ref[...].astype(jnp.float32) * precise_ref[...]
+    if sums:
+        dh, du, dv = (sums[0][i] for i in range(3))
+        eu, ev = (0.3 * scale) * du, (0.3 * scale) * dv
+        rests = (
+            -weight * (dh + 0.3 * (mu * du + mv * dv)),
+            (-0.15 * weight) * (du * du + dv * dv),
+        )
     else:
-        sums_ref, square_ref, step_ref, contrib_ref = refs
-        means = [mean_ref[i] for i in range(3)]
-        f = factor(square_ref, step_ref, cells)
-        states = [means[i] + f * sums_ref[i] for i in range(3)]
-    members = h_ref.shape[0]
-    scale = 1.0 / float(np.sqrt(np.float32(members - 1)))
-    sh, su, sv = states
-    residual = obs_ref[1] * (obs_ref[0] - sh - 0.15 * (su * su + sv * sv))
-    residual = residual * scale
-    eu, ev = 0.3 * su, 0.3 * sv
-    mh, mu, mv = means
+        eu, ev = (0.3 * scale) * mu, (0.3 * scale) * mv
+        rests = (weight * (value - mh - 0.15 * (mu * mu + mv * mv)),)
+    if not begin:
+        for i, rest in enumerate(rests):
+            out_ref[count + i] = rest
 
     def member(m, _):
-        h, u, v = (ref[begin + m] for ref in (h_ref, u_ref, v_ref))
-        contrib_ref[m] = ((h - mh) + (eu * (u - mu) + ev * (v - mv))) * residual
+        slope = eu * (u_ref[begin + m] - mu) + ev * (v_ref[begin + m] - mv)
+        if not sums:
+            slope = (h_ref[begin + m] - mh) * scale + slope
+        out_ref[m] = slope
         return 0
 
-    lax.fori_loop(0, contrib_ref.shape[0], member, 0, unroll=4)
-
-
-def contributions(part, cells, fields, means, obs, *more):
+    lax.fori_loop(0, count, member, 0, unroll=4)
+
+
+def slopes(part, fields, means, obs, *sums):
     begin, count = part
+    extra = 0 if begin else 1 + len(sums)
     return pl.pallas_call(
-        functools.partial(contrib_kernel, begin, cells),
-        name="contributions",
+        functools.partial(slope_kernel, begin),
+        name="slopes",
         compiler_params=GRANT,
-        in_specs=[VMEM] * 5 + ([VMEM, VMEM, SMEM] if more else []),
+        in_specs=[VMEM] * (7 + len(sums)),
         out_specs=VMEM,
-        out_shape=f32(count, *fields[0].shape[1:]),
-    )(*fields, means, obs, *more)
-
-
-def rows_kernel(x_ref, above_ref, below_ref, table_ref, out_ref, left_ref, right_ref):
-    members, rows, cols = x_ref.shape
+        out_shape=f32(count + extra, *fields[0].shape[1:]),
+    )(*fields, means, *obs, *sums)
+
+
+def rows_kernel(cells, orders, shared, *refs):
+    blocks = [refs[3 * i : 3 * i + 3] for i in range(orders)]
+    refs = refs[3 * orders :]
+    heads = [refs[3 * i : 3 * i + 3] for i in range(orders)] if shared else blocks
+    refs = refs[3 * orders * shared :]
+    *scales, table_ref, out_ref, left_ref, right_ref = refs
+    members, rows, cols = out_ref.shape
+    first = heads[0][0].shape[0] - 1
     lane = iota((rows, LANES), 1)
     table = table_ref[...]
+
+    def tall(trio, m):
+        own, above, below = trio
+        return jnp.concatenate([above[m], own[m], below[m]], axis=0)
+
+    rest = tall(heads[0], first)
+    if orders > 1:
+        f = factor(0, *scales, cells)
+        rest = rest + f * (tall(heads[1], first) + f * tall(heads[1], first + 1))
 
     def fold(g, _):
         left = right = None
@@ -368,7 +405,10 @@
             halves = []
             for k in (2 * pair, 2 * pair + 1):
                 m = g * FOLD + k
-                high, low = split(jnp.concatenate([above_ref[m], x_ref[m], below_ref[m]], axis=0))
+                slope = tall(blocks[0], m)
+                if orders > 1:
+                    slope = slope + f * tall(blocks[1], m)
+                high, low = split(slope * rest)
                 halves.append(jnp.concatenate([high, low], axis=0))
             both = mm(table, jnp.concatenate(halves, axis=1))
             both = both[:rows] + both[rows:]
@@ -386,17 +426,20 @@
     lax.fori_loop(0, members // FOLD, fold, 0, unroll=2)
 
 
-def taper_rows(x, above, below):
-    members, rows, cols = x.shape
+def taper_rows(part, cells, blocks, heads, scales):
+    begin, members = part
+    _, rows, cols = blocks[0][0].shape
     folds = members // FOLD
+    shared = bool(begin)
+    arrays = [x for trio in blocks + (heads if shared else []) for x in trio]
     return pl.pallas_call(
-        rows_kernel,
+        functools.partial(rows_kernel, cells, len(blocks), shared),
         name="taper_rows",
         compiler_params=GRANT,
-        in_specs=[VMEM] * 4,
+        in_specs=[VMEM] * len(arrays) + ([VMEM, VMEM, SMEM] if scales else []) + [VMEM],
         out_specs=[VMEM] * 3,
         out_shape=[f32(members, rows, cols)] + [f32(folds, rows, LANES)] * 2,
-    )(x, above, below, row_table(rows))
+    )(*arrays, *scales, row_table(rows))
 
 
 def columns_kernel(begin, cells, kinds, *refs):
@@ -430,7 +473,7 @@
     zero = jnp.zeros((SUB, cols), jnp.float32)
     square = names["square0"][...] if "square0" in names else zero
     if "prev" in names:
-        f = factor(names["squares"], names["step"], cells)
+        f = factor(0, names["total"], names["half"], names["step"], cells)
     for start in range(0, rows, SUB):
         part = slice(start, start + SUB)
         means = [mean_ref[i, part] for i in range(3)]
@@ -461,7 +504,7 @@
     if carried:
         ins.update(sums0=carried[0], square0=carried[1])
     if before:
-        ins.update(prev=before[0], squares=before[1], step=before[2])
+        ins.update(zip(("prev", "total", "half", "step"), before))
     grad = f32(count, rows, cols)
     outs = dict(sums=f32(3, rows, cols), square=f32(SUB, LANES))
     if not before:
@@ -480,11 +523,13 @@
 
 
 def analysis_kernel(cells, h_ref, u_ref, v_ref, *refs):
-    s0_ref, s1_ref, q0_ref, q1_ref, step0_ref, step1_ref, *outs, increment_ref = refs
+    s0_ref, s1_ref, *squares, step_ref = refs[:7]
+    *outs, increment_ref = refs[7:]
 
     @pl.when(pl.program_id(0) == 0)
     def _():
-        f0, f1 = factor(q0_ref, step0_ref, cells), factor(q1_ref, step1_ref, cells)
+        f0 = factor(0, *squares[:2], step_ref, cells)
+        f1 = factor(1, *squares[2:], step_ref, cells)
         increment_ref[...] = f0 * s0_ref[...] - f1 * s1_ref[...]
 
     begin = pl.program_id(0) * outs[0].shape[0]
@@ -501,7 +546,7 @@
         name="analysis",
         compiler_params=GRANT,
         grid=(members // (2 * PACK),),
-        in_specs=[VMEM] * 7 + [SMEM] * 2,
+        in_specs=[VMEM] * 9 + [SMEM],
         out_specs=[block] * 3,
         out_shape=[f32(members, rows, cols)] * 3,
         scratch_shapes=[pltpu.VMEM((3, rows, cols), jnp.float32)],
@@ -527,43 +572,44 @@
     above = shifted(bottom, "member", 1, False)
     below = shifted(top, "member", -1, False)
     starts, bottom = lax.optimization_barrier((starts, bottom))
-    first, last, *own = pack_columns(*starts)
+    first, last, *own, east, north, height = pack_columns(*starts)
     hall = shifted(last, "band", 1, True)
     halr = shifted(first, "band", -1, True)
     ends = jnp.concatenate([hall, halr], axis=0)
     cornu = shifted(ends[:, rows - SUB :], "member", 1, False)
     cornd = shifted(ends[:, :SUB], "member", -1, False)
 
-    obs = jnp.stack([obs_value, obs_mask.astype(jnp.float32) * obs_precision])
-    here = lax.axis_index("member")
-    edge = jnp.stack([here == 0, here == lax.axis_size("member") - 1]).astype(jnp.int32)
-    *fields, means = forecast(*starts, above, below, *own, hall, halr, cornu, cornd, edge)
+    obs = (obs_value, obs_mask, obs_precision)
+    *fields, means = forecast(height, east, north, above, below, *own, hall, halr, cornu, cornd)
     cells = float(members * rows * cols * lax.axis_size("member") * lax.axis_size("band"))
     parts = parts_of(members)
-    steps = [(step_sizes[k : k + 1].astype(jnp.float32) / 64.0) for k in range(ITERS)]
-
-    def localized(contribs, before):
-        sent = [
-            (shifted(c, "member", 1, False), shifted(c, "member", -1, False)) for c in contribs
+
+    def sent(slopes):
+        return [
+            (x, shifted(x, "member", 1, False), shifted(x, "member", -1, False)) for x in slopes
         ]
+
+    def localized(orders, scales, grads):
+        heads = [blocks[0] for blocks in orders]
         tapered = []
-        for c, (above, below) in zip(contribs, sent):
-            x, first, last = taper_rows(c, above, below)
+        for i, part in enumerate(parts):
+            blocks = [blocks[i] for blocks in orders]
+            x, first, last = taper_rows(part, cells, blocks, heads, scales)
             tapered.append((x, shifted(last, "band", 1, True), shifted(first, "band", -1, True)))
-        carried, grads = (), []
+        carried, found = (), []
         for i, (part, arrays) in enumerate(zip(parts, tapered)):
-            more = (before[0][i], *before[1:]) if before else ()
+            more = (grads[i], *scales) if grads else ()
             carried, grad = taper_columns(part, cells, *arrays, fields, means, carried, more)
-            grads += grad
-        return carried[0], everywhere_sum(carried[1]), grads
-
-    first = [contributions(part, cells, fields, means, obs) for part in parts]
-    sums0, squares0, grads = localized(first, ())
-    second = [
-        contributions(part, cells, fields, means, obs, sums0, squares0, steps[0]) for part in parts
-    ]
-    sums1, squares1, _ = localized(second, (grads, squares0, steps[0]))
-    return tuple(analysis(cells, fields, sums0, sums1, squares0, squares1, *steps))
+            found += grad
+        return *carried, found
+
+    order0 = sent([slopes(part, fields, means, obs) for part in parts])
+    sums0, squares0, grads = localized([order0], (), ())
+    order1 = sent([slopes(part, fields, means, obs, sums0) for part in parts])
+    squares0 = everywhere_sum(squares0)
+    sums1, squares1, _ = localized([order0, order1], (*squares0, step_sizes), grads)
+    squares1 = everywhere_sum(squares1)
+    return tuple(analysis(cells, fields, sums0, sums1, *squares0, *squares1, step_sizes))
 
 
 def solution(mesh):

time: 184 us -> 167 us (0.908)
  starting transfers between devices: 95.6 us -> 79.3 us
  waiting for transfers between devices: 32.6 us -> 43.6 us
  local copies, waits for them, and re-layouts: 7.72 us -> 1.41 us
  Pallas kernels: 44.6 us -> 40.8 us
    ppermute x10, starting transfers between devices: 48.2 us -> 9.44 us  [everywhere_sum(): half = lax.ppermute(block, axis, [(i, i ^ reach) for i in range(count)])]
    ppermute x22, starting transfers between devices: 47.5 us -> 69.9 us  [shifted(): return lax.ppermute(block, axis, pairs)]
    ppermute x10, waiting for transfers between devices: 23 us -> 35.2 us  [everywhere_sum(): half = lax.ppermute(block, axis, [(i, i ^ reach) for i in range(count)])]
    unnamed x33 -> x29, local copies, waits for them, and re-layouts: 7.11 us -> 1.39 us
    pallas_call x10, Pallas kernels: 28.5 us -> 23.7 us  [the longest x1 12.7 us: forecast(): pl.pallas_call(forecast_kernel, name='forecast', compiler_params=GRANT, g...]
  transfers between devices with their start and end apart: 32 -> 32, of which waited for: 13 -> 15; matrix products, arithmetic and copies ran while one was open for 0% -> 0% of each run, Pallas kernels for 8% -> 9%
where the time goes in v3:
time: 167 us; the launch traced here: 166 us
  starting transfers between devices  79.3 us (47%)
  waiting for transfers between devices  43.6 us (26%)
  Pallas kernels  40.8 us (24%)
    ppermute x22, starting transfers between devices, shifted(): return lax.ppermute(block, axis, pairs)  69.9 us
    ppermute x10, waiting for transfers between devices, everywhere_sum(): half = lax.ppermute(block, axis, [(i, i ^ reach) for i in range(count)])  35.2 us
    pallas_call x1, Pallas kernels, forecast(): pl.pallas_call(forecast_kernel, name='forecast', compiler_params=GRANT, g...  12.7 us
    pallas_call x4, Pallas kernels, taper_columns(): pl.pallas_call(functools.partial(columns_kernel, part[0], cells, kinds),...  11 us
    ppermute x10, starting transfers between devices, everywhere_sum(): half = lax.ppermute(block, axis, [(i, i ^ reach) for i in range(count)])  9.44 us
    ppermute x22, waiting for transfers between devices, shifted(): return lax.ppermute(block, axis, pairs)  8.4 us
    pallas_call x4, Pallas kernels, taper_rows(): pl.pallas_call(functools.partial(rows_kernel, cells, len(blocks), shared)...  7.48 us
    pallas_call x1, Pallas kernels, analysis(): pl.pallas_call(functools.partial(analysis_kernel, cells), name='analysis'...  3.5 us
  transfers between devices with their start and end apart: 32, of which 15 were waited for; matrix products, arithmetic and copies ran while one was open for 0% of the time, Pallas kernels for 9%

profile of v3, /device:TPU:0, one launch (start us, length us, event | category | flops | bytes accessed | tf_op | source)
XLA Modules:
  0.0 166.3 jit_solution(14587068430981273188)
XLA Ops:
  0.7 2.7 %pack_rows.1 = (f32[80,16,128]{2,1,0:T(8,128)}, f32[80,16,128]{2,1,0:T(8,128)}) custom-call(f32[80,32,128]{2,1,0:T(8,128)} %u_ref, f32[80,32,128]{2,1,0:T(8,128)} %v_ref, f32[80,32,128]{2,1,0:T(8,128)} %h_ref, f32[80,32,128]{2,1,0:T(8,128)} %u_ref, f32[80,32,128]{2,1,0:T(8,128)} %v_ref, f32[80,32,128]{2,1,0:T(8,128)} %h_ref), custom_call_target="tpu_custom_call" | custom-call | tf_op jit(solution)/shard_map/pack_rows/pallas_call | solution.py:143
  3.4 1.3 copy-done.2
  4.7 2.6 %pack_columns.1 = (f32[10,32,128]{2,1,0:T(8,128)S(1)}, f32[10,32,128]{2,1,0:T(8,128)S(1)}, f32[10,32,128]{2,1,0:T(8,128)S(1)}, f32[10,32,128]{2,1,0:T(8,128)S(1)...) custom-call(f32[80,32,128]{2,1,0:T(8,128)S(1)} %copy-done, ...), custom_call_target="tpu_custom_call" | custom-call | tf_op jit(solution)/shard_map/pack_columns/pallas_call | solution.py:187
  7.3 3.1 %collective-permute-start.2 = (f32[10,32,128]{2,1,0:T(8,128)S(1)}, f32[10,32,128]{2,1,0:T(8,128)S(1)}, u32[]{:S(2)}, u32[]{:S(2)}) collective-permute-start(f32[10,32,128]{2,1,0:T(8,128)S(1)} %get-tuple-element.53), channel_id=1, source_target_pairs={{0,1},{1,2},{2,3},{3,0},{4,5},{5,6},{6,7},{7,4},{8,9},{9,10},{10,1... | collective-permute-start | bytes 491528 | tf_op jit(solution)/shard_map/ppermute | solution.py:48
  10.4 1.5 collective-permute-start
  11.9 1.3 collective-permute-start.1
  13.2 2.4 %collective-permute-start.3 = (f32[10,32,128]{2,1,0:T(8,128)S(1)}, f32[10,32,128]{2,1,0:T(8,128)S(1)}, u32[]{:S(2)}, u32[]{:S(2)}) collective-permute-start(f32[10,32,128]{2,1,0:T(8,128)S(1)} %get-tuple-element.54), channel_id=1, source_target_pairs={{0,3},{1,0},{2,1},{3,2},{4,7},{5,4},{6,5},{7,6},{8,11},{9,8},{10,9... | collective-permute-start | bytes 491528 | tf_op jit(solution)/shard_map/ppermute | solution.py:48
  16.7 2.0 %collective-permute-done.3.halr_ref = f32[10,32,128]{2,1,0:T(8,128)S(1)} collective-permute-done((f32[10,32,128]{2,1,0:T(8,128)S(1)}, f32[10,32,128]{2,1,0:T(8,128)S(1)}, u32[]{:S(2)}, u32[]{:S(2)}) %collective-permute-start.3) | collective-permute-done | bytes 163872 | tf_op jit(solution)/shard_map/ppermute | solution.py:48
  18.7 3.6 %collective-permute-start.4 = (f32[20,8,128]{2,1,0:T(8,128)S(1)}, f32[20,8,128]{2,1,0:T(8,128)S(1)}, u32[]{:S(2)}, u32[]{:S(2)}) collective-permute-start(f32[20,8,128]{2,1,0:T(8,128)S(1)} %get-tuple-element.82), channel_id=1, source_target_pairs={{0,4},{4,8},{8,12},{12,16},{16,20},{20,24},{24,28},{1,5},{5,9},{9,... | collective-permute-start | bytes 245768 | tf_op jit(solution)/shard_map/ppermute | solution.py:48
  22.3 1.3 collective-permute-start.5
  23.6 4.7 %collective-permute-done.5 = f32[20,8,128]{2,1,0:T(8,128)S(1)} collective-permute-done((f32[20,8,128]{2,1,0:T(8,128)S(1)}, f32[20,8,128]{2,1,0:T(8,128)S(1)}, u32[]{:S(2)}, u32[]{:S(2)}) %collective-permute-start.5) | collective-permute-done | bytes 81952 | tf_op jit(solution)/shard_map/ppermute | solution.py:48
  28.3 12.7 %forecast.1 = (f32[80,32,128]{2,1,0:T(8,128)S(1)}, f32[80,32,128]{2,1,0:T(8,128)S(1)}, f32[80,32,128]{2,1,0:T(8,128)S(1)}, f32[3,32,128]{2,1,0:T(8,128)S(1)}) custom-call(f32[80,32,128]{2,1,0:T(8,128)S(1)} %get-tuple-element.46.h_ref, f32[80,32,128]{2,1,0:T(8,128)S(1)} %get-tuple-element.47.u_ref, f32[80,32,128]{2,1,0:T(8,128)S(1)} %get-tuple-element.48.v_ref, ...), custom_call_target="tpu_custom_call" | custom-call | tf_op jit(solution)/shard_map/forecast/pallas_call | solution.py:314
  41.3 5.6 %collective-permute-start.8 = (f32[49,32,128]{2,1,0:T(8,128)S(1)}, f32[49,32,128]{2,1,0:T(8,128)S(1)}, u32[]{:S(2)}, u32[]{:S(2)}) collective-permute-start(f32[49,32,128]{2,1,0:T(8,128)S(1)} %slopes.5.refs_3_.refs_0_.refs_6_), channel_id=1, source_target_pairs={{0,4},{4,8},{8,12},{12,16},{16,20},{20,24},{24,28},{1,5},{5,9},{9,... | collective-permute-start | bytes 2408456 | tf_op jit(solution)/shard_map/ppermute | solution.py:48
  46.9 1.3 collective-permute-start.9
  48.4 3.1 %collective-permute-start.6 = (f32[32,32,128]{2,1,0:T(8,128)S(1)}, f32[32,32,128]{2,1,0:T(8,128)S(1)}, u32[]{:S(2)}, u32[]{:S(2)}) collective-permute-start(f32[32,32,128]{2,1,0:T(8,128)S(1)} %slopes.4.refs_0_), channel_id=1, source_target_pairs={{0,4},{4,8},{8,12},{12,16},{16,20},{20,24},{24,28},{1,5},{5,9},{9,... | collective-permute-start | bytes 1572872 | tf_op jit(solution)/shard_map/ppermute | solution.py:48
  51.5 1.3 collective-permute-start.7
  52.8 1.7 %taper_rows.5 = (f32[48,32,128]{2,1,0:T(8,128)S(1)}, f32[12,32,128]{2,1,0:T(8,128)S(1)}, f32[12,32,128]{2,1,0:T(8,128)S(1)}) custom-call(f32[49,32,128]{2,1,0:T(8,128)S(1)} %slopes.5.refs_3_.refs_0_.refs_6_, f32[49,32,128]{2,1,0:T(8,128)S(1)} %collective-permute-done.8.refs_4_.refs_1_.refs_7_, ...), custom_call_target="tpu_custom_call" | custom-call | tf_op jit(solution)/shard_map/taper_rows/pallas_call | solution.py:435
  54.6 1.6 collective-permute-start.12
  56.2 2.2 %collective-permute-start.13 = (f32[12,32,128]{2,1,0:T(8,128)S(1)}, f32[12,32,128]{2,1,0:T(8,128)S(1)}, u32[]{:S(2)}, u32[]{:S(2)}) collective-permute-start(f32[12,32,128]{2,1,0:T(8,128)S(1)} %get-tuple-element.64), channel_id=1, source_target_pairs={{0,3},{1,0},{2,1},{3,2},{4,7},{5,4},{6,5},{7,6},{8,11},{9,8},{10,9... | collective-permute-start | bytes 589832 | tf_op jit(solution)/shard_map/ppermute | solution.py:48
  58.4 1.2 taper_rows.4
  59.7 3.8 %collective-permute-start.11 = (f32[8,32,128]{2,1,0:T(8,128)S(1)}, f32[8,32,128]{2,1,0:T(8,128)S(1)}, u32[]{:S(2)}, u32[]{:S(2)}) collective-permute-start(f32[8,32,128]{2,1,0:T(8,128)S(1)} %get-tuple-element.61), channel_id=1, source_target_pairs={{0,3},{1,0},{2,1},{3,2},{4,7},{5,4},{6,5},{7,6},{8,11},{9,8},{10,9... | collective-permute-start | bytes 393224 | tf_op jit(solution)/shard_map/ppermute | solution.py:48
  64.0 2.9 %taper_columns.4 = (f32[3,32,128]{2,1,0:T(8,128)S(1)}, f32[8,128]{1,0:T(8,128)S(1)}, f32[48,32,128]{2,1,0:T(8,128)S(1)}) custom-call(f32[48,32,128]{2,1,0:T(8,128)S(1)} %get-tuple-element.62.refs_0_, f32[12,32,128]{2,1,0:T(8,128)S(1)} %collective-permute-done.12.refs_1_, f32[12,32,128]{2,1,0:T(8,128)S(1)} %collective-permute-done.13.refs_2_, ...), custom_call_target="tpu_custom_call" | custom-call | tf_op jit(solution)/shard_map/taper_columns/pallas_call | solution.py:513
  66.9 1.9 %taper_columns.5 = (f32[3,32,128]{2,1,0:T(8,128)S(1)}, f32[8,128]{1,0:T(8,128)S(1)}, f32[32,32,128]{2,1,0:T(8,128)S(1)}) custom-call(f32[32,32,128]{2,1,0:T(8,128)S(1)} %get-tuple-element.59.refs_0_, f32[8,32,128]{2,1,0:T(8,128)S(1)} %collective-permute-done.10.refs_1_, f32[8,32,128]{2,1,0:T(8,128)S(1)} %collective-permute-done.11.refs_2_, ...), custom_call_target="tpu_custom_call" | custom-call | tf_op jit(solution)/shard_map/taper_columns/pallas_call | solution.py:513
  69.0 21.1 %collective-permute-start.16 = (f32[50,32,128]{2,1,0:T(8,128)S(1)}, f32[50,32,128]{2,1,0:T(8,128)S(1)}, u32[]{:S(2)}, u32[]{:S(2)}) collective-permute-start(f32[50,32,128]{2,1,0:T(8,128)S(1)} %slopes.7.refs_9_.refs_3_), channel_id=1, source_target_pairs={{0,4},{4,8},{8,12},{12,16},{16,20},{20,24},{24,28},{1,5},{5,9},{9,... | collective-permute-start | bytes 2457608 | tf_op jit(solution)/shard_map/ppermute | solution.py:48
  90.1 1.3 collective-permute-start.17
  91.6 6.4 %collective-permute-start.14 = (f32[32,32,128]{2,1,0:T(8,128)S(1)}, f32[32,32,128]{2,1,0:T(8,128)S(1)}, u32[]{:S(2)}, u32[]{:S(2)}) collective-permute-start(f32[32,32,128]{2,1,0:T(8,128)S(1)} %slopes.6.refs_3_), channel_id=1, source_target_pairs={{0,4},{4,8},{8,12},{12,16},{16,20},{20,24},{24,28},{1,5},{5,9},{9,... | collective-permute-start | bytes 1572872 | tf_op jit(solution)/shard_map/ppermute | solution.py:48
  97.9 1.3 collective-permute-start.15
  99.2 1.4 collective-permute-start.18
  100.6 2.3 %collective-permute-done.18 = f32[8,128]{1,0:T(8,128)S(1)} collective-permute-done((f32[8,128]{1,0:T(8,128)S(1)}, f32[8,128]{1,0:T(8,128)S(1)}, u32[]{:S(2)}, u32[]{:S(2)}) %collective-permute-start.18) | collective-permute-done | bytes 4128 | tf_op jit(solution)/shard_map/ppermute | solution.py:61
  102.9 1.1 collective-permute-start.19
  104.0 3.4 %collective-permute-done.19 = f32[8,128]{1,0:T(8,128)S(1)} collective-permute-done((f32[8,128]{1,0:T(8,128)S(1)}, f32[8,128]{1,0:T(8,128)S(1)}, u32[]{:S(2)}, u32[]{:S(2)}) %collective-permute-start.19) | collective-permute-done | bytes 4128 | tf_op jit(solution)/shard_map/ppermute | solution.py:61
  108.6 4.0 %collective-permute-start.21 = (f32[8,128]{1,0:T(8,128)S(1)}, f32[8,128]{1,0:T(8,128)S(1)}, u32[]{:S(2)}, u32[]{:S(2)}) collective-permute-start(f32[8,128]{1,0:T(8,128)S(1)} %add.26), channel_id=1, source_target_pairs={{0,8},{4,12},{8,0},{12,4},{16,24},{20,28},{24,16},{28,20},{1,9},{5... | collective-permute-start | bytes 12296 | tf_op jit(solution)/shard_map/ppermute | solution.py:61
  112.6 11.2 %collective-permute-done.21 = f32[8,128]{1,0:T(8,128)S(1)} collective-permute-done((f32[8,128]{1,0:T(8,128)S(1)}, f32[8,128]{1,0:T(8,128)S(1)}, u32[]{:S(2)}, u32[]{:S(2)}) %collective-permute-start.21) | collective-permute-done | bytes 4128 | tf_op jit(solution)/shard_map/ppermute | solution.py:61
  123.8 3.6 %collective-permute-done.22.refs_13_.refs_7_.refs_12_.refs_14_.refs_3_ = f32[8,128]{1,0:T(8,128)S(1)} collective-permute-done((f32[8,128]{1,0:T(8,128)S(1)}, f32[8,128]{1,0:T(8,128)S(1)}, u32[]{:S(2)}, u32[]{:S(2)}) %collective-permute-start.22) | collective-permute-done | bytes 4128 | tf_op jit(solution)/shard_map/ppermute | solution.py:61
  127.4 2.6 %taper_rows.7 = (f32[48,32,128]{2,1,0:T(8,128)S(1)}, f32[12,32,128]{2,1,0:T(8,128)S(1)}, f32[12,32,128]{2,1,0:T(8,128)S(1)}) custom-call(f32[49,32,128]{2,1,0:T(8,128)S(1)} %slopes.5.refs_3_.refs_0_.refs_6_, f32[49,32,128]{2,1,0:T(8,128)S(1)} %collective-permute-done.8.refs_4_.refs_1_.refs_7_, ...), custom_call_target="tpu_custom_call" | custom-call | tf_op jit(solution)/shard_map/taper_rows/pallas_call | solution.py:435
  130.0 1.3 collective-permute-start.25
  131.2 2.6 %collective-permute-start.26 = (f32[12,32,128]{2,1,0:T(8,128)S(1)}, f32[12,32,128]{2,1,0:T(8,128)S(1)}, u32[]{:S(2)}, u32[]{:S(2)}) collective-permute-start(f32[12,32,128]{2,1,0:T(8,128)S(1)} %get-tuple-element.74), channel_id=1, source_target_pairs={{0,3},{1,0},{2,1},{3,2},{4,7},{5,4},{6,5},{7,6},{8,11},{9,8},{10,9... | collective-permute-start | bytes 589832 | tf_op jit(solution)/shard_map/ppermute | solution.py:48
  133.8 2.0 %taper_rows.6 = (f32[32,32,128]{2,1,0:T(8,128)S(1)}, f32[8,32,128]{2,1,0:T(8,128)S(1)}, f32[8,32,128]{2,1,0:T(8,128)S(1)}) custom-call(f32[32,32,128]{2,1,0:T(8,128)S(1)} %slopes.4.refs_0_, f32[32,32,128]{2,1,0:T(8,128)S(1)} %collective-permute-done.6.refs_1_, f32[32,32,128]{2,1,0:T(8,128)S(1)} %collective-permute-done.7.refs_2_, ...), custom_call_target="tpu_custom_call" | custom-call | tf_op jit(solution)/shard_map/taper_rows/pallas_call | solution.py:435
  135.9 3.8 %collective-permute-start.24 = (f32[8,32,128]{2,1,0:T(8,128)S(1)}, f32[8,32,128]{2,1,0:T(8,128)S(1)}, u32[]{:S(2)}, u32[]{:S(2)}) collective-permute-start(f32[8,32,128]{2,1,0:T(8,128)S(1)} %get-tuple-element.71), channel_id=1, source_target_pairs={{0,3},{1,0},{2,1},{3,2},{4,7},{5,4},{6,5},{7,6},{8,11},{9,8},{10,9... | collective-permute-start | bytes 393224 | tf_op jit(solution)/shard_map/ppermute | solution.py:48
  139.9 3.6 %taper_columns.6 = (f32[3,32,128]{2,1,0:T(8,128)S(1)}, f32[8,128]{1,0:T(8,128)S(1)}) custom-call(f32[48,32,128]{2,1,0:T(8,128)S(1)} %get-tuple-element.72.refs_0_, f32[12,32,128]{2,1,0:T(8,128)S(1)} %collective-permute-done.25.refs_1_, f32[12,32,128]{2,1,0:T(8,128)S(1)} %collective-permute-done.26.refs_2_, ...), custom_call_target="tpu_custom_call" | custom-call | tf_op jit(solution)/shard_map/taper_columns/pallas_call | solution.py:513
  143.5 2.7 %taper_columns.7 = (f32[3,32,128]{2,1,0:T(8,128)S(1)}, f32[8,128]{1,0:T(8,128)S(1)}) custom-call(f32[32,32,128]{2,1,0:T(8,128)S(1)} %get-tuple-element.69.refs_0_, f32[8,32,128]{2,1,0:T(8,128)S(1)} %collective-permute-done.23.refs_1_, f32[8,32,128]{2,1,0:T(8,128)S(1)} %collective-permute-done.24.refs_2_, ...), custom_call_target="tpu_custom_call" | custom-call | tf_op jit(solution)/shard_map/taper_columns/pallas_call | solution.py:513
  146.8 3.1 %collective-permute-done.27 = f32[8,128]{1,0:T(8,128)S(1)} collective-permute-done((f32[8,128]{1,0:T(8,128)S(1)}, f32[8,128]{1,0:T(8,128)S(1)}, u32[]{:S(2)}, u32[]{:S(2)}) %collective-permute-start.27) | collective-permute-done | bytes 4128 | tf_op jit(solution)/shard_map/ppermute | solution.py:61
  149.9 2.0 %collective-permute-start.28 = (f32[8,128]{1,0:T(8,128)S(1)}, f32[8,128]{1,0:T(8,128)S(1)}, u32[]{:S(2)}, u32[]{:S(2)}) collective-permute-start(f32[8,128]{1,0:T(8,128)S(1)} %add.28), channel_id=1, source_target_pairs={{0,2},{1,3},{2,0},{3,1},{4,6},{5,7},{6,4},{7,5},{8,10},{9,11},{10,... | collective-permute-start | bytes 12296 | tf_op jit(solution)/shard_map/ppermute | solution.py:61
  151.8 2.5 %collective-permute-done.28 = f32[8,128]{1,0:T(8,128)S(1)} collective-permute-done((f32[8,128]{1,0:T(8,128)S(1)}, f32[8,128]{1,0:T(8,128)S(1)}, u32[]{:S(2)}, u32[]{:S(2)}) %collective-permute-start.28) | collective-permute-done | bytes 4128 | tf_op jit(solution)/shard_map/ppermute | solution.py:61
  154.4 1.2 collective-permute-done.29
  155.6 3.6 %collective-permute-done.30 = f32[8,128]{1,0:T(8,128)S(1)} collective-permute-done((f32[8,128]{1,0:T(8,128)S(1)}, f32[8,128]{1,0:T(8,128)S(1)}, u32[]{:S(2)}, u32[]{:S(2)}) %collective-permute-start.30) | collective-permute-done | bytes 4128 | tf_op jit(solution)/shard_map/ppermute | solution.py:61
  159.5 3.3 %collective-permute-done.31.refs_5_ = f32[8,128]{1,0:T(8,128)S(1)} collective-permute-done((f32[8,128]{1,0:T(8,128)S(1)}, f32[8,128]{1,0:T(8,128)S(1)}, u32[]{:S(2)}, u32[]{:S(2)}) %collective-permute-start.31) | collective-permute-done | bytes 4128 | tf_op jit(solution)/shard_map/ppermute | solution.py:61
  162.8 3.5 %analysis.1 = (f32[80,32,128]{2,1,0:T(8,128)}, f32[80,32,128]{2,1,0:T(8,128)}, f32[80,32,128]{2,1,0:T(8,128)}) custom-call(f32[80,32,128]{2,1,0:T(8,128)S(1)} %get-tuple-element.55.h_ref.refs_7_, f32[80,32,128]{2,1,0:T(8,128)S(1)} %get-tuple-element.56.u_ref.refs_8_, f32[80,32,128]{2,1,0:T(8,128)S(1)} %get-tuple-element.57.v_ref.refs_9_, ...), custom_call_target="tpu_custom_call" | custom-call | tf_op jit(solution)/shard_map/analysis/pallas_call | solution.py:544
  (71 shorter events, 4.9 us)
Async XLA Ops:
  0.6 2.7 %copy-start = (f32[80,32,128]{2,1,0:T(8,128)S(1)}, f32[80,32,128]{2,1,0:T(8,128)}, u32[]{:S(2)}) copy-start(f32[80,32,128]{2,1,0:T(8,128)} %u_ref) | copy-start | bytes 3932164
  0.6 2.7 %copy-start.1 = (f32[80,32,128]{2,1,0:T(8,128)S(1)}, f32[80,32,128]{2,1,0:T(8,128)}, u32[]{:S(2)}) copy-start(f32[80,32,128]{2,1,0:T(8,128)} %v_ref) | copy-start | bytes 3932164
  3.4 1.3 copy-start.2
  4.7 5.7 %copy-start.13 = (f32[80,16,128]{2,1,0:T(8,128)S(1)}, f32[80,16,128]{2,1,0:T(8,128)}, u32[]{:S(2)}) copy-start(f32[80,16,128]{2,1,0:T(8,128)} %get-tuple-element.42) | copy-start | bytes 1966084
  4.7 7.2 %copy-start.12 = (f32[80,16,128]{2,1,0:T(8,128)S(1)}, f32[80,16,128]{2,1,0:T(8,128)}, u32[]{:S(2)}) copy-start(f32[80,16,128]{2,1,0:T(8,128)} %get-tuple-element.49) | copy-start | bytes 1966084
  4.7 23.6 %copy-start.10 = (bf16[256,128]{1,0:T(8,128)(2,1)S(1)}, bf16[256,128]{1,0:T(8,128)(2,1)}, u32[]{:S(2)}) copy-start(bf16[256,128]{1,0:T(8,128)(2,1)} %constant.10.clone.table_ref) | copy-start | bytes 196612
  7.3 9.3 %collective-permute-start.2 = (f32[10,32,128]{2,1,0:T(8,128)S(1)}, f32[10,32,128]{2,1,0:T(8,128)S(1)}, u32[]{:S(2)}, u32[]{:S(2)}) collective-permute-start(f32[10,32,128]{2,1,0:T(8,128)S(1)} %get-tuple-element.53), channel_id=1, source_target_pairs={{0,1},{1,2},{2,3},{3,0},{4,5},{5,6},{6,7},{7,4},{8,9},{9,10},{10,1... | collective-permute-start | bytes 491528 | tf_op jit(solution)/shard_map/ppermute | solution.py:48
  10.4 17.8 %collective-permute-start = (f32[80,16,128]{2,1,0:T(8,128)S(1)}, f32[80,16,128]{2,1,0:T(8,128)S(1)}, u32[]{:S(2)}, u32[]{:S(2)}) collective-permute-start(f32[80,16,128]{2,1,0:T(8,128)S(1)} %copy-done.13), channel_id=1, source_target_pairs={{0,4},{4,8},{8,12},{12,16},{16,20},{20,24},{24,28},{1,5},{5,9},{9,... | collective-permute-start | bytes 1966088 | tf_op jit(solution)/shard_map/ppermute | solution.py:48
  11.9 16.3 %collective-permute-start.1 = (f32[80,16,128]{2,1,0:T(8,128)S(1)}, f32[80,16,128]{2,1,0:T(8,128)S(1)}, u32[]{:S(2)}, u32[]{:S(2)}) collective-permute-start(f32[80,16,128]{2,1,0:T(8,128)S(1)} %copy-done.12), channel_id=1, source_target_pairs={{4,0},{8,4},{12,8},{16,12},{20,16},{24,20},{28,24},{5,1},{9,5},{13... | collective-permute-start | bytes 1966088 | tf_op jit(solution)/shard_map/ppermute | solution.py:48
  13.2 5.5 %collective-permute-start.3 = (f32[10,32,128]{2,1,0:T(8,128)S(1)}, f32[10,32,128]{2,1,0:T(8,128)S(1)}, u32[]{:S(2)}, u32[]{:S(2)}) collective-permute-start(f32[10,32,128]{2,1,0:T(8,128)S(1)} %get-tuple-element.54), channel_id=1, source_target_pairs={{0,3},{1,0},{2,1},{3,2},{4,7},{5,4},{6,5},{7,6},{8,11},{9,8},{10,9... | collective-permute-start | bytes 491528 | tf_op jit(solution)/shard_map/ppermute | solution.py:48
  18.7 4.9 %collective-permute-start.4 = (f32[20,8,128]{2,1,0:T(8,128)S(1)}, f32[20,8,128]{2,1,0:T(8,128)S(1)}, u32[]{:S(2)}, u32[]{:S(2)}) collective-permute-start(f32[20,8,128]{2,1,0:T(8,128)S(1)} %get-tuple-element.82), channel_id=1, source_target_pairs={{0,4},{4,8},{8,12},{12,16},{16,20},{20,24},{24,28},{1,5},{5,9},{9,... | collective-permute-start | bytes 245768 | tf_op jit(solution)/shard_map/ppermute | solution.py:48
  22.3 6.0 %collective-permute-start.5 = (f32[20,8,128]{2,1,0:T(8,128)S(1)}, f32[20,8,128]{2,1,0:T(8,128)S(1)}, u32[]{:S(2)}, u32[]{:S(2)}) collective-permute-start(f32[20,8,128]{2,1,0:T(8,128)S(1)} %get-tuple-element.81), channel_id=1, source_target_pairs={{4,0},{8,4},{12,8},{16,12},{20,16},{24,20},{28,24},{5,1},{9,5},{13... | collective-permute-start | bytes 245768 | tf_op jit(solution)/shard_map/ppermute | solution.py:48
  28.3 12.7 %copy-start.7 = (f32[32,128]{1,0:T(8,128)S(1)}, f32[32,128]{1,0:T(8,128)}, u32[]{:S(2)}) copy-start(f32[32,128]{1,0:T(8,128)} %value_ref.7) | copy-start | bytes 49156
  28.3 12.7 %copy-start.8 = (s32[32,128]{1,0:T(8,128)S(1)}, s32[32,128]{1,0:T(8,128)}, u32[]{:S(2)}) copy-start(s32[32,128]{1,0:T(8,128)} %seen_ref.7) | copy-start | bytes 49156
  28.3 12.7 %copy-start.9 = (f32[32,128]{1,0:T(8,128)S(1)}, f32[32,128]{1,0:T(8,128)}, u32[]{:S(2)}) copy-start(f32[32,128]{1,0:T(8,128)} %precise_ref.7) | copy-start | bytes 49156
  41.3 11.5 %copy-start.6 = (bf16[64,192]{1,0:T(8,128)(2,1)S(1)}, bf16[64,192]{1,0:T(8,128)(2,1)}, u32[]{:S(2)}) copy-start(bf16[64,192]{1,0:T(8,128)(2,1)} %constant.11.clone.refs_6_.refs_3_.refs_15_.refs_9_) | copy-start | bytes 73732
  41.3 11.4 %collective-permute-start.8 = (f32[49,32,128]{2,1,0:T(8,128)S(1)}, f32[49,32,128]{2,1,0:T(8,128)S(1)}, u32[]{:S(2)}, u32[]{:S(2)}) collective-permute-start(f32[49,32,128]{2,1,0:T(8,128)S(1)} %slopes.5.refs_3_.refs_0_.refs_6_), channel_id=1, source_target_pairs={{0,4},{4,8},{8,12},{12,16},{16,20},{20,24},{24,28},{1,5},{5,9},{9,... | collective-permute-start | bytes 2408456 | tf_op jit(solution)/shard_map/ppermute | solution.py:48
  46.9 5.9 %collective-permute-start.9 = (f32[49,32,128]{2,1,0:T(8,128)S(1)}, f32[49,32,128]{2,1,0:T(8,128)S(1)}, u32[]{:S(2)}, u32[]{:S(2)}) collective-permute-start(f32[49,32,128]{2,1,0:T(8,128)S(1)} %slopes.5.refs_3_.refs_0_.refs_6_), channel_id=1, source_target_pairs={{4,0},{8,4},{12,8},{16,12},{20,16},{24,20},{28,24},{5,1},{9,5},{13... | collective-permute-start | bytes 2408456 | tf_op jit(solution)/shard_map/ppermute | solution.py:48
  48.4 10.0 %collective-permute-start.6 = (f32[32,32,128]{2,1,0:T(8,128)S(1)}, f32[32,32,128]{2,1,0:T(8,128)S(1)}, u32[]{:S(2)}, u32[]{:S(2)}) collective-permute-start(f32[32,32,128]{2,1,0:T(8,128)S(1)} %slopes.4.refs_0_), channel_id=1, source_target_pairs={{0,4},{4,8},{8,12},{12,16},{16,20},{20,24},{24,28},{1,5},{5,9},{9,... | collective-permute-start | bytes 1572872 | tf_op jit(solution)/shard_map/ppermute | solution.py:48
  51.5 7.0 %collective-permute-start.7 = (f32[32,32,128]{2,1,0:T(8,128)S(1)}, f32[32,32,128]{2,1,0:T(8,128)S(1)}, u32[]{:S(2)}, u32[]{:S(2)}) collective-permute-start(f32[32,32,128]{2,1,0:T(8,128)S(1)} %slopes.4.refs_0_), channel_id=1, source_target_pairs={{4,0},{8,4},{12,8},{16,12},{20,16},{24,20},{28,24},{5,1},{9,5},{13... | collective-permute-start | bytes 1572872 | tf_op jit(solution)/shard_map/ppermute | solution.py:48
  54.6 8.9 %collective-permute-start.12 = (f32[12,32,128]{2,1,0:T(8,128)S(1)}, f32[12,32,128]{2,1,0:T(8,128)S(1)}, u32[]{:S(2)}, u32[]{:S(2)}) collective-permute-start(f32[12,32,128]{2,1,0:T(8,128)S(1)} %get-tuple-element.63), channel_id=1, source_target_pairs={{0,1},{1,2},{2,3},{3,0},{4,5},{5,6},{6,7},{7,4},{8,9},{9,10},{10,1... | collective-permute-start | bytes 589832 | tf_op jit(solution)/shard_map/ppermute | solution.py:48
  56.2 7.8 %copy-start.3 = (bf16[256,256]{1,0:T(8,128)(2,1)S(1)}, bf16[256,256]{1,0:T(8,128)(2,1)}, u32[]{:S(2)}) copy-start(bf16[256,256]{1,0:T(8,128)(2,1)} %constant.12.clone.refs_4_) | copy-start | bytes 393220
  56.2 7.8 %copy-start.4 = (bf16[256,256]{1,0:T(8,128)(2,1)S(1)}, bf16[256,256]{1,0:T(8,128)(2,1)}, u32[]{:S(2)}) copy-start(bf16[256,256]{1,0:T(8,128)(2,1)} %constant.13.clone.refs_5_) | copy-start | bytes 393220
  56.2 7.8 %copy-start.5 = (bf16[256,256]{1,0:T(8,128)(2,1)S(1)}, bf16[256,256]{1,0:T(8,128)(2,1)}, u32[]{:S(2)}) copy-start(bf16[256,256]{1,0:T(8,128)(2,1)} %constant.14.clone.refs_6_) | copy-start | bytes 393220
  56.2 7.8 %collective-permute-start.13 = (f32[12,32,128]{2,1,0:T(8,128)S(1)}, f32[12,32,128]{2,1,0:T(8,128)S(1)}, u32[]{:S(2)}, u32[]{:S(2)}) collective-permute-start(f32[12,32,128]{2,1,0:T(8,128)S(1)} %get-tuple-element.64), channel_id=1, source_target_pairs={{0,3},{1,0},{2,1},{3,2},{4,7},{5,4},{6,5},{7,6},{8,11},{9,8},{10,9... | collective-permute-start | bytes 589832 | tf_op jit(solution)/shard_map/ppermute | solution.py:48
  59.6 7.2 %collective-permute-start.10 = (f32[8,32,128]{2,1,0:T(8,128)S(1)}, f32[8,32,128]{2,1,0:T(8,128)S(1)}, u32[]{:S(2)}, u32[]{:S(2)}) collective-permute-start(f32[8,32,128]{2,1,0:T(8,128)S(1)} %get-tuple-element.60), channel_id=1, source_target_pairs={{0,1},{1,2},{2,3},{3,0},{4,5},{5,6},{6,7},{7,4},{8,9},{9,10},{10,1... | collective-permute-start | bytes 393224 | tf_op jit(solution)/shard_map/ppermute | solution.py:48
  59.7 7.2 %collective-permute-start.11 = (f32[8,32,128]{2,1,0:T(8,128)S(1)}, f32[8,32,128]{2,1,0:T(8,128)S(1)}, u32[]{:S(2)}, u32[]{:S(2)}) collective-permute-start(f32[8,32,128]{2,1,0:T(8,128)S(1)} %get-tuple-element.61), channel_id=1, source_target_pairs={{0,3},{1,0},{2,1},{3,2},{4,7},{5,4},{6,5},{7,6},{8,11},{9,8},{10,9... | collective-permute-start | bytes 393224 | tf_op jit(solution)/shard_map/ppermute | solution.py:48
  69.0 58.4 %copy-start.11 = (s32[2]{0:T(128)S(1)}, s32[2]{0:T(128)}, u32[]{:S(2)}) copy-start(s32[2]{0:T(128)} %refs_6_.6) | copy-start | bytes 28
  69.0 58.4 %collective-permute-start.16 = (f32[50,32,128]{2,1,0:T(8,128)S(1)}, f32[50,32,128]{2,1,0:T(8,128)S(1)}, u32[]{:S(2)}, u32[]{:S(2)}) collective-permute-start(f32[50,32,128]{2,1,0:T(8,128)S(1)} %slopes.7.refs_9_.refs_3_), channel_id=1, source_target_pairs={{0,4},{4,8},{8,12},{12,16},{16,20},{20,24},{24,28},{1,5},{5,9},{9,... | collective-permute-start | bytes 2457608 | tf_op jit(solution)/shard_map/ppermute | solution.py:48
  90.1 37.2 %collective-permute-start.17 = (f32[50,32,128]{2,1,0:T(8,128)S(1)}, f32[50,32,128]{2,1,0:T(8,128)S(1)}, u32[]{:S(2)}, u32[]{:S(2)}) collective-permute-start(f32[50,32,128]{2,1,0:T(8,128)S(1)} %slopes.7.refs_9_.refs_3_), channel_id=1, source_target_pairs={{4,0},{8,4},{12,8},{16,12},{20,16},{24,20},{28,24},{5,1},{9,5},{13... | collective-permute-start | bytes 2457608 | tf_op jit(solution)/shard_map/ppermute | solution.py:48
  91.6 42.3 %collective-permute-start.14 = (f32[32,32,128]{2,1,0:T(8,128)S(1)}, f32[32,32,128]{2,1,0:T(8,128)S(1)}, u32[]{:S(2)}, u32[]{:S(2)}) collective-permute-start(f32[32,32,128]{2,1,0:T(8,128)S(1)} %slopes.6.refs_3_), channel_id=1, source_target_pairs={{0,4},{4,8},{8,12},{12,16},{16,20},{20,24},{24,28},{1,5},{5,9},{9,... | collective-permute-start | bytes 1572872 | tf_op jit(solution)/shard_map/ppermute | solution.py:48
  97.9 35.9 %collective-permute-start.15 = (f32[32,32,128]{2,1,0:T(8,128)S(1)}, f32[32,32,128]{2,1,0:T(8,128)S(1)}, u32[]{:S(2)}, u32[]{:S(2)}) collective-permute-start(f32[32,32,128]{2,1,0:T(8,128)S(1)} %slopes.6.refs_3_), channel_id=1, source_target_pairs={{4,0},{8,4},{12,8},{16,12},{20,16},{24,20},{28,24},{5,1},{9,5},{13... | collective-permute-start | bytes 1572872 | tf_op jit(solution)/shard_map/ppermute | solution.py:48
  99.2 3.7 %collective-permute-start.18 = (f32[8,128]{1,0:T(8,128)S(1)}, f32[8,128]{1,0:T(8,128)S(1)}, u32[]{:S(2)}, u32[]{:S(2)}) collective-permute-start(f32[8,128]{1,0:T(8,128)S(1)} %get-tuple-element.68), channel_id=1, source_target_pairs={{0,1},{1,0},{2,3},{3,2},{4,5},{5,4},{6,7},{7,6},{8,9},{9,8},{10,11... | collective-permute-start | bytes 12296 | tf_op jit(solution)/shard_map/ppermute | solution.py:61
  102.9 4.5 %collective-permute-start.19 = (f32[8,128]{1,0:T(8,128)S(1)}, f32[8,128]{1,0:T(8,128)S(1)}, u32[]{:S(2)}, u32[]{:S(2)}) collective-permute-start(f32[8,128]{1,0:T(8,128)S(1)} %add.24), channel_id=1, source_target_pairs={{0,2},{1,3},{2,0},{3,1},{4,6},{5,7},{6,4},{7,5},{8,10},{9,11},{10,... | collective-permute-start | bytes 12296 | tf_op jit(solution)/shard_map/ppermute | solution.py:61
  107.4 1.2 collective-permute-start.20
  108.6 15.1 %collective-permute-start.21 = (f32[8,128]{1,0:T(8,128)S(1)}, f32[8,128]{1,0:T(8,128)S(1)}, u32[]{:S(2)}, u32[]{:S(2)}) collective-permute-start(f32[8,128]{1,0:T(8,128)S(1)} %add.26), channel_id=1, source_target_pairs={{0,8},{4,12},{8,0},{12,4},{16,24},{20,28},{24,16},{28,20},{1,9},{5... | collective-permute-start | bytes 12296 | tf_op jit(solution)/shard_map/ppermute | solution.py:61
  123.8 3.6 %collective-permute-start.22 = (f32[8,128]{1,0:T(8,128)S(1)}, f32[8,128]{1,0:T(8,128)S(1)}, u32[]{:S(2)}, u32[]{:S(2)}) collective-permute-start(f32[8,128]{1,0:T(8,128)S(1)} %add.27.refs_12_.refs_6_.refs_11_.refs_13_.refs_2_), channel_id=1, source_target_pairs={{0,16},{4,20},{8,24},{12,28},{16,0},{20,4},{24,8},{28,12},{1,17},{... | collective-permute-start | bytes 12296 | tf_op jit(solution)/shard_map/ppermute | solution.py:61
  130.0 9.7 %collective-permute-start.25 = (f32[12,32,128]{2,1,0:T(8,128)S(1)}, f32[12,32,128]{2,1,0:T(8,128)S(1)}, u32[]{:S(2)}, u32[]{:S(2)}) collective-permute-start(f32[12,32,128]{2,1,0:T(8,128)S(1)} %get-tuple-element.73), channel_id=1, source_target_pairs={{0,1},{1,2},{2,3},{3,0},{4,5},{5,6},{6,7},{7,4},{8,9},{9,10},{10,1... | collective-permute-start | bytes 589832 | tf_op jit(solution)/shard_map/ppermute | solution.py:48
  131.2 8.7 %collective-permute-start.26 = (f32[12,32,128]{2,1,0:T(8,128)S(1)}, f32[12,32,128]{2,1,0:T(8,128)S(1)}, u32[]{:S(2)}, u32[]{:S(2)}) collective-permute-start(f32[12,32,128]{2,1,0:T(8,128)S(1)} %get-tuple-element.74), channel_id=1, source_target_pairs={{0,3},{1,0},{2,1},{3,2},{4,7},{5,4},{6,5},{7,6},{8,11},{9,8},{10,9... | collective-permute-start | bytes 589832 | tf_op jit(solution)/shard_map/ppermute | solution.py:48
  135.8 7.7 %collective-permute-start.23 = (f32[8,32,128]{2,1,0:T(8,128)S(1)}, f32[8,32,128]{2,1,0:T(8,128)S(1)}, u32[]{:S(2)}, u32[]{:S(2)}) collective-permute-start(f32[8,32,128]{2,1,0:T(8,128)S(1)} %get-tuple-element.70), channel_id=1, source_target_pairs={{0,1},{1,2},{2,3},{3,0},{4,5},{5,6},{6,7},{7,4},{8,9},{9,10},{10,1... | collective-permute-start | bytes 393224 | tf_op jit(solution)/shard_map/ppermute | solution.py:48
  135.9 7.6 %collective-permute-start.24 = (f32[8,32,128]{2,1,0:T(8,128)S(1)}, f32[8,32,128]{2,1,0:T(8,128)S(1)}, u32[]{:S(2)}, u32[]{:S(2)}) collective-permute-start(f32[8,32,128]{2,1,0:T(8,128)S(1)} %get-tuple-element.71), channel_id=1, source_target_pairs={{0,3},{1,0},{2,1},{3,2},{4,7},{5,4},{6,5},{7,6},{8,11},{9,8},{10,9... | collective-permute-start | bytes 393224 | tf_op jit(solution)/shard_map/ppermute | solution.py:48
  146.2 3.7 %collective-permute-start.27 = (f32[8,128]{1,0:T(8,128)S(1)}, f32[8,128]{1,0:T(8,128)S(1)}, u32[]{:S(2)}, u32[]{:S(2)}) collective-permute-start(f32[8,128]{1,0:T(8,128)S(1)} %get-tuple-element.80), channel_id=1, source_target_pairs={{0,1},{1,0},{2,3},{3,2},{4,5},{5,4},{6,7},{7,6},{8,9},{9,8},{10,11... | collective-permute-start | bytes 12296 | tf_op jit(solution)/shard_map/ppermute | solution.py:61
  149.9 4.5 %collective-permute-start.28 = (f32[8,128]{1,0:T(8,128)S(1)}, f32[8,128]{1,0:T(8,128)S(1)}, u32[]{:S(2)}, u32[]{:S(2)}) collective-permute-start(f32[8,128]{1,0:T(8,128)S(1)} %add.28), channel_id=1, source_target_pairs={{0,2},{1,3},{2,0},{3,1},{4,6},{5,7},{6,4},{7,5},{8,10},{9,11},{10,... | collective-permute-start | bytes 12296 | tf_op jit(solution)/shard_map/ppermute | solution.py:61
  154.4 1.2 collective-permute-start.29
  155.6 3.6 %collective-permute-start.30 = (f32[8,128]{1,0:T(8,128)S(1)}, f32[8,128]{1,0:T(8,128)S(1)}, u32[]{:S(2)}, u32[]{:S(2)}) collective-permute-start(f32[8,128]{1,0:T(8,128)S(1)} %add.30), channel_id=1, source_target_pairs={{0,8},{4,12},{8,0},{12,4},{16,24},{20,28},{24,16},{28,20},{1,9},{5... | collective-permute-start | bytes 12296 | tf_op jit(solution)/shard_map/ppermute | solution.py:61
  159.2 3.6 %collective-permute-start.31 = (f32[8,128]{1,0:T(8,128)S(1)}, f32[8,128]{1,0:T(8,128)S(1)}, u32[]{:S(2)}, u32[]{:S(2)}) collective-permute-start(f32[8,128]{1,0:T(8,128)S(1)} %add.31.refs_4_), channel_id=1, source_target_pairs={{0,16},{4,20},{8,24},{12,28},{16,0},{20,4},{24,8},{28,12},{1,17},{... | collective-permute-start | bytes 12296 | tf_op jit(solution)/shard_map/ppermute | solution.py:61
